TPU v7x, 256 devices: a whole 4x4x8 slice. The times are simulated.
256 devices in a mesh: lat: 32 (over y, z), rad: 8 (over x, core).
Axes of the slice: x: 4, y: 4, z: 8, core: 2. Of those that a mesh axis runs over, the one named last changes fastest.
Arguments:
- source: float32 [128, 131072], P('rad', 'lat'), may hold values from -6 to 6
- to_modes: float32 [128, 128], replicated, may hold values from -0.5 to 0.5
- from_modes: float32 [128, 128], replicated, may hold values from -0.5 to 0.5
- eigenvalue: float32 [128], replicated, may hold values from 0.1 to 20
- shifts: float32 [131072], P('lat'), may hold values from 0.5 to 2
- weights: float32 [31, 131072], P(None, 'lat'), may hold values from 0.02 to 0.12
- neighbors: int32 [31, 1024], P(None, 'lat'), may hold values from -8 to 8, as said below
Outputs:
- smoothed: float32 [128, 131072], P('rad', 'lat')
- residual_norm: float32 [128], P('rad')
Inputs may be any that keep to these rules, and one draw needn't show every extreme that they name: `neighbors`: every entry is nonzero; some entry equals -8.
All inputs are finite; a program needn't handle non-finite values.
Results may differ from a plain program's by a relative error of at most 0.000073.
Values sent between devices are 32-bit elements; how exact they have to be, the bound alone decides.
No kernel may reach another device: no remote copies, remote signals or barrier semaphores. Data moves between devices by JAX's collectives and lax.ppermute only.
A program may use at most 64 MiB of HBM per device.

v0:
```python
import functools

import jax
import jax.numpy as jnp
import numpy as np
from jax import lax
from jax.experimental import pallas as pl
from jax.experimental.pallas import tpu as pltpu
from jax.sharding import Mesh, PartitionSpec as P

LANES = 128
HALO = 8
STENCIL = 31
ROWS = STENCIL + 1
BLOCKS = 32
EXT1 = BLOCKS + 2 * HALO
EXT2 = BLOCKS + 4 * HALO
SLAB = 16
PARTS = 8
PART = BLOCKS * LANES // PARTS
MODES = 128
WIDE = 2 * HALO * LANES
NEAR = HALO * LANES
LAT = ("y", "z")
RAD = ("x", "core")
STAGE_1 = ("y", "x", "core")
STAGE_2 = "z"
VMEM = pl.BlockSpec(memory_space=pltpu.VMEM)
SMEM = pl.BlockSpec(memory_space=pltpu.SMEM)
HIGHEST = lax.Precision.HIGHEST


def f32(*shape):
    return jax.ShapeDtypeStruct(shape, jnp.float32)


def mm(a, b):
    return jnp.dot(a, b, precision=HIGHEST, preferred_element_type=jnp.float32)


def pack_kernel(src, weights, shifts, neighbors, up, down, own):
    nb = neighbors[...].astype(jnp.float32)
    last = BLOCKS * LANES
    for out, start, near, blocks, place in (
        (up, last - WIDE, last - NEAR, BLOCKS - HALO, 0),
        (down, 0, 0, 0, HALO + BLOCKS),
    ):
        out[0:SLAB, 0:NEAR] = src[:, start : start + NEAR]
        out[SLAB : 2 * SLAB, 0:NEAR] = src[:, start + NEAR : start + WIDE]
        out[0:STENCIL, NEAR:WIDE] = weights[:, near : near + NEAR]
        out[STENCIL:ROWS, NEAR:WIDE] = shifts[:, near : near + NEAR]
        out[:, WIDE:] = jnp.zeros((ROWS, LANES), jnp.float32)
        out[0:STENCIL, WIDE + place : WIDE + place + HALO] = nb[:, blocks : blocks + HALO]
    own[...] = jnp.zeros((ROWS, LANES), jnp.float32)
    own[0:STENCIL, HALO : HALO + BLOCKS] = nb


def stencil_kernel(src, left, right, weights, shifts, own, out, x0, x1, w, diag, nbv, nbs, sem):
    lane = lax.broadcasted_iota(jnp.int32, (ROWS, LANES), 1)
    nb = jnp.where(
        lane < HALO, left[:, WIDE:], jnp.where(lane < HALO + BLOCKS, own[...], right[:, WIDE:])
    )
    nbv[...] = nb.astype(jnp.int32)
    copy = pltpu.make_async_copy(nbv, nbs, sem)
    copy.start()
    for half in range(2):
        rows = slice(half * SLAB, half * SLAB + SLAB)
        for j in range(HALO):
            cols = slice(j * LANES, (j + 1) * LANES)
            x0[half * HALO + j] = left[rows, cols]
            x0[2 * HALO + BLOCKS + half * HALO + j] = right[rows, cols]
    for j in range(BLOCKS):
        x0[2 * HALO + j] = src[:, j * LANES : (j + 1) * LANES]
    for r in range(PARTS):
        out[r, 0:SLAB, :] = src[:, r * PART : (r + 1) * PART]
    for j in range(HALO):
        cols = slice(NEAR + j * LANES, NEAR + (j + 1) * LANES)
        w[j] = left[:, cols]
        w[HALO + BLOCKS + j] = right[:, cols]
    for j in range(BLOCKS):
        cols = slice(j * LANES, (j + 1) * LANES)
        w[HALO + j, 0:STENCIL, :] = weights[:, cols]
        w[HALO + j, STENCIL:ROWS, :] = shifts[:, cols]
    copy.wait()

    def apply(field, block, centre, d):
        acc = d * field[block + centre]
        for s in range(STENCIL):
            moved = field[nbs[s, block] + (block + centre)]
            if s:
                moved = pltpu.roll(moved, LANES - s, 1)
            acc = acc - w[block, s : s + 1, :] * moved
        return acc

    def first(e, _):
        d = jnp.sum(w[e], axis=0, keepdims=True)
        diag[e] = d
        x1[e] = apply(x0, e, HALO, d)
        return 0

    lax.fori_loop(0, EXT1, first, 0)

    def second(b, _):
        part = lax.div(b, PART // LANES)
        cols = pl.ds(pl.multiple_of(lax.rem(b, PART // LANES) * LANES, LANES), LANES)
        e = b + HALO
        out[part, SLAB : 2 * SLAB, cols] = x1[e]
        out[part, 2 * SLAB : 3 * SLAB, cols] = apply(x1, e, 0, diag[e])
        return 0

    lax.fori_loop(0, BLOCKS, second, 0)


def gram_kernel(z, to_modes, eig, out, s):
    for r in range(PARTS):
        rows = slice(r * SLAB, (r + 1) * SLAB)
        for q in range(3):
            s[rows, q * PART : (q + 1) * PART] = z[r, q * SLAB : (q + 1) * SLAB, :]
    m = mm(to_modes[...], s[...])
    row = lax.broadcasted_iota(jnp.int32, (MODES, MODES), 0)
    col = lax.broadcasted_iota(jnp.int32, (MODES, MODES), 1)
    e = jnp.sum(jnp.where(row == col, eig[...], 0.0), axis=1, keepdims=True)
    m0, m1, m2 = (m[:, q * PART : (q + 1) * PART] for q in range(3))
    image = m1 + e * m0
    again = (m2 + e * m1) + e * image
    folded = []
    for a, b in ((m0, m0), (m0, image), (image, image), (m0, again), (image, again), (again, again)):
        p = a * b
        folded.append(sum(p[:, k * LANES : (k + 1) * LANES] for k in range(PART // LANES)))
    stack = jnp.concatenate(folded, axis=1)
    which = lax.broadcasted_iota(jnp.int32, (8, 6 * LANES), 1) // LANES
    pick = (which == lax.broadcasted_iota(jnp.int32, (8, 6 * LANES), 0)).astype(jnp.float32)
    g = lax.dot_general(
        pick, stack, (((1,), (1,)), ((), ())), precision=HIGHEST, preferred_element_type=jnp.float32
    )
    out[...] = jnp.broadcast_to(g[None], out.shape)


def relay_kernel(got, out):
    out[...] = jnp.broadcast_to(jnp.sum(got[...], axis=0)[None], out.shape)


def finish_kernel(got, z, to_modes, from_modes, eig, out, norm, s):
    g = jnp.sum(got[...], axis=0)
    mm_, mi, ii, mj, ij, jj = (g[k : k + 1, :] for k in range(6))
    e = eig[...]
    scale = mm_ + 1e-06
    upper = 1.5 * jnp.sqrt(ii / scale)
    lower = upper * 0.125
    center = (upper + lower) * 0.5
    half_width = (upper - lower) * 0.5
    sigma = center / half_width
    rho_zero = 1.0 / sigma
    rho_one = 1.0 / (2.0 * sigma - rho_zero)
    over = 1.0 / center
    c2 = 2.0 * rho_one / half_width
    u0 = rho_one * rho_zero * over + c2
    u1 = -c2 * over
    a = -over - u0
    b = -u1
    squares = mm_ + a * (2.0 * mi + a * ii) + b * (2.0 * (mj + a * ij) + b * jj)
    norm[...] = jnp.sqrt(jnp.maximum(squares, 0.0) / scale)
    for r in range(PARTS):
        for q in range(2):
            s[q * MODES + r * SLAB : q * MODES + (r + 1) * SLAB, :] = z[r, q * SLAB : (q + 1) * SLAB, :]
    from_m = from_modes[...]
    to_m = to_modes[...]
    mix = jnp.concatenate([mm(from_m * (over + u0 + u1 * e), to_m), mm(from_m * u1, to_m)], axis=1)
    out[...] = mm(mix, s[...]).reshape(out.shape)


def unpack_kernel(got, out):
    for r in range(PARTS):
        out[:, r * PART : (r + 1) * PART] = got[r]


def call(kernel, out_shape, in_specs, scratch=()):
    multiple = isinstance(out_shape, tuple)
    return pl.pallas_call(
        kernel,
        out_shape=out_shape,
        in_specs=in_specs,
        out_specs=(VMEM,) * len(out_shape) if multiple else VMEM,
        scratch_shapes=scratch,
        compiler_params=pltpu.CompilerParams(vmem_limit_bytes=32 * 1024 * 1024),
    )


def on_device(sizes, source, to_modes, from_modes, eigenvalue, shifts, weights, neighbors):
    lat = sizes["y"] * sizes["z"]
    shift_row = shifts.reshape(1, -1)
    eig = eigenvalue.reshape(1, -1)
    up, down, own = call(
        pack_kernel, (f32(ROWS, WIDE + LANES), f32(ROWS, WIDE + LANES), f32(ROWS, LANES)), [VMEM] * 4
    )(source, weights, shift_row, neighbors)
    left = lax.ppermute(up, LAT, [(i, (i + 1) % lat) for i in range(lat)])
    right = lax.ppermute(down, LAT, [((i + 1) % lat, i) for i in range(lat)])
    sent = call(
        stencil_kernel,
        f32(PARTS, 3 * SLAB, PART),
        [VMEM] * 6,
        [
            pltpu.VMEM((EXT2, SLAB, LANES), jnp.float32),
            pltpu.VMEM((EXT1, SLAB, LANES), jnp.float32),
            pltpu.VMEM((EXT1, ROWS, LANES), jnp.float32),
            pltpu.VMEM((EXT1, 1, LANES), jnp.float32),
            pltpu.VMEM((ROWS, LANES), jnp.int32),
            pltpu.SMEM((ROWS, LANES), jnp.int32),
            pltpu.SemaphoreType.DMA,
        ],
    )(source, left, right, weights, shift_row, own)
    z = lax.all_to_all(sent, RAD, 0, 0, tiled=True)
    peers_1 = sizes["y"] * sizes["x"] * sizes["core"]
    peers_2 = sizes["z"]
    g = call(
        gram_kernel,
        f32(peers_1, 8, LANES),
        [VMEM] * 3,
        [pltpu.VMEM((MODES, 3 * PART), jnp.float32)],
    )(z, to_modes, eig)
    g = lax.all_to_all(g, STAGE_1, 0, 0, tiled=True)
    g = call(relay_kernel, f32(peers_2, 8, LANES), [VMEM])(g)
    g = lax.all_to_all(g, STAGE_2, 0, 0, tiled=True)
    mixed, norm = call(
        finish_kernel,
        (f32(PARTS, SLAB, PART), f32(1, LANES)),
        [VMEM] * 5,
        [pltpu.VMEM((2 * MODES, PART), jnp.float32)],
    )(g, z, to_modes, from_modes, eig)
    got = lax.all_to_all(mixed, RAD, 0, 0, tiled=True)
    smoothed = call(unpack_kernel, f32(SLAB, BLOCKS * LANES), [VMEM])(got)
    residual_norm = lax.dynamic_slice_in_dim(norm[0], lax.axis_index(RAD) * SLAB, SLAB)
    return smoothed, residual_norm


def solution(mesh):
    names = ("y", "z", "x", "core")
    fine = Mesh(np.asarray(mesh.devices).reshape(4, 8, 4, 2), names)
    return jax.shard_map(
        functools.partial(on_device, dict(fine.shape)),
        mesh=fine,
        in_specs=(P(RAD, LAT), P(), P(), P(), P(LAT), P(None, LAT), P(None, LAT)),
        out_specs=(P(RAD, LAT), P(RAD)),
        check_vma=False,
    )
```

profile of v0, /device:TPU:1, one launch (start us, length us, event | category | flops | bytes accessed | tf_op | source)
XLA Modules:
  0.0 88.8 jit_solution(4959489017750954285)
XLA Ops:
  0.6 0.0 copy-start
  0.6 1.0 %copy-done = f32[31,4096]{1,0:T(8,128)S(1)} copy-done((f32[31,4096]{1,0:T(8,128)S(1)}, f32[31,4096]{1,0:T(8,128)}, u32[]{:S(2)}) %copy-start) | copy-done | bytes 507928
  1.7 0.0 copy-start.1
  1.7 0.9 %copy-done.1 = f32[16,4096]{1,0:T(8,128)S(1)} copy-done((f32[16,4096]{1,0:T(8,128)S(1)}, f32[16,4096]{1,0:T(8,128)}, u32[]{:S(2)}) %copy-start.1) | copy-done | bytes 262168
  2.6 0.0 copy-start.3
  2.6 0.7 copy-done.3
  3.3 0.0 copy-start.5
  3.3 0.7 copy-done.5
  4.1 0.1 shard_map.86
  4.1 2.5 %collective-permute-start = (f32[32,2176]{1,0:T(8,128)S(1)}, f32[32,2176]{1,0:T(8,128)S(1)}, u32[]{:S(2)}, u32[]{:S(2)}) collective-permute-start(f32[32,2176]{1,0:T(8,128)S(1)} %get-tuple-element.7), channel_id=1, source_target_pairs={{0,8},{8,16},{16,24},{24,32},{32,40},{40,48},{48,56},{56,64},{64,7... | collective-permute-start | bytes 835592 | tf_op jit(solution)/shard_map/ppermute | solution.py:196
  6.7 6.5 %collective-permute-start.1 = (f32[32,2176]{1,0:T(8,128)S(1)}, f32[32,2176]{1,0:T(8,128)S(1)}, u32[]{:S(2)}, u32[]{:S(2)}) collective-permute-start(f32[32,2176]{1,0:T(8,128)S(1)} %get-tuple-element.8), channel_id=1, source_target_pairs={{8,0},{16,8},{24,16},{32,24},{40,32},{48,40},{56,48},{64,56},{72,6... | collective-permute-start | bytes 835592 | tf_op jit(solution)/shard_map/ppermute | solution.py:197
  13.1 6.3 %collective-permute-done.left = f32[32,2176]{1,0:T(8,128)S(1)} collective-permute-done((f32[32,2176]{1,0:T(8,128)S(1)}, f32[32,2176]{1,0:T(8,128)S(1)}, u32[]{:S(2)}, u32[]{:S(2)}) %collective-permute-start) | collective-permute-done | bytes 278560 | tf_op jit(solution)/shard_map/ppermute | solution.py:196
  19.4 0.0 collective-permute-done.1.right
  19.4 11.6 %shard_map.87 = f32[8,48,512]{2,1,0:T(8,128)S(1)} custom-call(f32[16,4096]{1,0:T(8,128)S(1)} %copy-done.1, f32[32,2176]{1,0:T(8,128)S(1)} %collective-permute-done.left, f32[32,2176]{1,0:T(8,128)S(1)} %collective-permute-done.1.right, f32[31,4096]{1,0:T(8,128)S(1)} %copy-done, f32[1,4096]{1,0:T(1,128)S(1)} %bitcast.5, f32[32,128]{1,0:T(8,128)S(1)} %get-tuple-element.9.own), custom_call_target="tpu_custom_call" | custom-call | tf_op jit(solution)/shard_map/pallas_call | solution.py:198
  31.1 0.0 copy-start.2
  31.1 17.7 %all_to_all.20.z = f32[8,48,512]{2,1,0:T(8,128)S(1)} all-to-all(f32[8,48,512]{2,1,0:T(8,128)S(1)} %shard_map.87), channel_id=1, replica_groups=mesh['y'=4,'z'=8,'x'=4,'core'=2] {'x','core'}, dimensions={0} | all-to-all | bytes 1572864 | tf_op jit(solution)/shard_map/all_to_all | solution.py:212
  48.8 0.0 copy-start.6
  48.8 0.0 copy-done.2
  48.8 0.7 copy-done.6
  49.4 1.5 %shard_map.88 = f32[32,8,128]{2,1,0:T(8,128)S(1)} custom-call(f32[8,48,512]{2,1,0:T(8,128)S(1)} %all_to_all.20.z, f32[128,128]{1,0:T(8,128)S(1)} %copy-done.2, f32[1,128]{1,0:T(1,128)S(1)} %bitcast.6), custom_call_target="tpu_custom_call" | custom-call | tf_op jit(solution)/shard_map/pallas_call | solution.py:215
  51.0 11.4 %all_to_all.21.got = f32[32,8,128]{2,1,0:T(8,128)S(1)} all-to-all(f32[32,8,128]{2,1,0:T(8,128)S(1)} %shard_map.88), channel_id=1, replica_groups=mesh['y'=4,'z'=8,'x'=4,'core'=2] {'y','x','core'}, dimensions={0} | all-to-all | bytes 262144 | tf_op jit(solution)/shard_map/all_to_all | solution.py:221
  62.4 0.0 copy-start.4
  62.4 12.7 %all_to_all.22.got = f32[8,8,128]{2,1,0:T(8,128)S(1)} all-to-all(f32[8,8,128]{2,1,0:T(8,128)S(1)} %shard_map.89), channel_id=1, replica_groups=mesh['y'=4,'z'=8,'x'=4,'core'=2] {'z'}, dimensions={0} | all-to-all | bytes 65536 | tf_op jit(solution)/shard_map/all_to_all | solution.py:223
  75.1 0.0 copy-done.4
  75.1 1.4 %shard_map.90 = (f32[8,16,512]{2,1,0:T(8,128)}, f32[1,128]{1,0:T(1,128)S(1)}) custom-call(f32[8,8,128]{2,1,0:T(8,128)S(1)} %all_to_all.22.got, f32[8,48,512]{2,1,0:T(8,128)S(1)} %all_to_all.20.z, f32[128,128]{1,0:T(8,128)S(1)} %copy-done.2, f32[128,128]{1,0:T(8,128)S(1)} %copy-done.4, f32[1,128]{1,0:T(1,128)S(1)} %bitcast.7), custom_call_target="tpu_custom_call" | custom-call | tf_op jit(solution)/shard_map/pallas_call | solution.py:224
  76.5 5.0 %all-to-all-start.3 = ((f32[8,16,512]{2,1,0:T(8,128)}), f32[8,16,512]{2,1,0:T(8,128)S(1)}, u32[]{:S(2)}, u32[]{:S(2)}) async-start(f32[8,16,512]{2,1,0:T(8,128)} %get-tuple-element.10), calls=%async_computation.3 | async-start | bytes 524288 | tf_op jit(solution)/shard_map/all_to_all | solution.py:230
  81.5 0.6 dynamic-slice_bitcast_fusion
  82.1 5.9 %all-to-all-done.3.got = f32[8,16,512]{2,1,0:T(8,128)S(1)} async-done(((f32[8,16,512]{2,1,0:T(8,128)}), f32[8,16,512]{2,1,0:T(8,128)S(1)}, u32[]{:S(2)}, u32[]{:S(2)}) %all-to-all-start.3) | async-done | bytes 262176 | tf_op jit(solution)/shard_map/all_to_all | solution.py:230
  88.1 0.7 shard_map.91
  (1 shorter events, 0.0 us)
Async XLA Ops:
  0.6 1.0 %copy-start = (f32[31,4096]{1,0:T(8,128)S(1)}, f32[31,4096]{1,0:T(8,128)}, u32[]{:S(2)}) copy-start(f32[31,4096]{1,0:T(8,128)} %weights.3) | copy-start | bytes 1523716
  1.7 0.9 %copy-start.1 = (f32[16,4096]{1,0:T(8,128)S(1)}, f32[16,4096]{1,0:T(8,128)}, u32[]{:S(2)}) copy-start(f32[16,4096]{1,0:T(8,128)} %src.3) | copy-start | bytes 786436
  2.6 0.7 copy-start.3
  3.3 0.7 copy-start.5
  4.1 15.3 %collective-permute-start = (f32[32,2176]{1,0:T(8,128)S(1)}, f32[32,2176]{1,0:T(8,128)S(1)}, u32[]{:S(2)}, u32[]{:S(2)}) collective-permute-start(f32[32,2176]{1,0:T(8,128)S(1)} %get-tuple-element.7), channel_id=1, source_target_pairs={{0,8},{8,16},{16,24},{24,32},{32,40},{40,48},{48,56},{56,64},{64,7... | collective-permute-start | bytes 835592 | tf_op jit(solution)/shard_map/ppermute | solution.py:196
  6.7 12.8 %collective-permute-start.1 = (f32[32,2176]{1,0:T(8,128)S(1)}, f32[32,2176]{1,0:T(8,128)S(1)}, u32[]{:S(2)}, u32[]{:S(2)}) collective-permute-start(f32[32,2176]{1,0:T(8,128)S(1)} %get-tuple-element.8), channel_id=1, source_target_pairs={{8,0},{16,8},{24,16},{32,24},{40,32},{48,40},{56,48},{64,56},{72,6... | collective-permute-start | bytes 835592 | tf_op jit(solution)/shard_map/ppermute | solution.py:197
  31.1 17.7 %copy-start.2 = (f32[128,128]{1,0:T(8,128)S(1)}, f32[128,128]{1,0:T(8,128)}, u32[]{:S(2)}) copy-start(f32[128,128]{1,0:T(8,128)} %to_modes.3) | copy-start | bytes 196612
  48.8 0.7 copy-start.6
  62.4 12.7 %copy-start.4 = (f32[128,128]{1,0:T(8,128)S(1)}, f32[128,128]{1,0:T(8,128)}, u32[]{:S(2)}) copy-start(f32[128,128]{1,0:T(8,128)} %from_modes.1) | copy-start | bytes 196612
  76.5 11.6 %all-to-all-start.3 = ((f32[8,16,512]{2,1,0:T(8,128)}), f32[8,16,512]{2,1,0:T(8,128)S(1)}, u32[]{:S(2)}, u32[]{:S(2)}) async-start(f32[8,16,512]{2,1,0:T(8,128)} %get-tuple-element.10), calls=%async_computation.3 | async-start | bytes 524288 | tf_op jit(solution)/shard_map/all_to_all | solution.py:230
where the time goes:
time: 89.3 us; the launch traced here: 88.8 us
  blocking collectives  41.8 us (47%)
  Pallas kernels  15.4 us (17%)
  starting transfers between devices  14 us (16%)
  waiting for transfers between devices  12.2 us (14%)
  local copies, waits for them, and re-layouts  4.66 us (5%)
    all_to_all x1, blocking collectives, on_device(): z = lax.all_to_all(sent, RAD, 0, 0, tiled=True)  17.7 us
    all_to_all x1, blocking collectives, on_device(): g = lax.all_to_all(g, STAGE_2, 0, 0, tiled=True)  12.7 us
    pallas_call x1, Pallas kernels, on_device(): call(stencil_kernel, f32(PARTS, 3 * SLAB, PART), [VMEM] * 6, [pltpu.VMEM(...  11.6 us
    all_to_all x1, blocking collectives, on_device(): g = lax.all_to_all(g, STAGE_1, 0, 0, tiled=True)  11.4 us
    ppermute x1, starting transfers between devices, on_device(): right = lax.ppermute(down, LAT, [((i + 1) % lat, i) for i in range(lat)])  6.48 us
    ppermute x1, waiting for transfers between devices, on_device(): left = lax.ppermute(up, LAT, [(i, (i + 1) % lat) for i in range(lat)])  6.29 us
    all_to_all x1, waiting for transfers between devices, on_device(): got = lax.all_to_all(mixed, RAD, 0, 0, tiled=True)  5.94 us
    all_to_all x1, starting transfers between devices, on_device(): got = lax.all_to_all(mixed, RAD, 0, 0, tiled=True)  5.04 us
  transfers between devices with their start and end apart: 3, of which 2 were waited for; matrix products, arithmetic and copies ran while one was open for 1% of the time, Pallas kernels for 0%

commit v1 on v0

v1 whole, which is shorter than its diff:
```python
import functools

import jax
import jax.numpy as jnp
import numpy as np
from jax import lax
from jax.experimental import pallas as pl
from jax.experimental.pallas import tpu as pltpu
from jax.sharding import Mesh, PartitionSpec as P

LANES = 128
HALO = 8
UNROLL = 8
STENCIL = 31
ROWS = STENCIL + 1
BLOCKS = 32
EXT1 = BLOCKS + 2 * HALO
EXT2 = BLOCKS + 4 * HALO
SLAB = 16
PARTS = 8
PART = BLOCKS * LANES // PARTS
MODES = 128
WIDE = 2 * HALO * LANES
NEAR = HALO * LANES
LAT = ("y", "z")
RAD = ("x", "core")
STAGE_1 = ("y", "x", "core")
STAGE_2 = "z"
VMEM = pl.BlockSpec(memory_space=pltpu.VMEM)
SMEM = pl.BlockSpec(memory_space=pltpu.SMEM)
HBM = pl.BlockSpec(memory_space=pltpu.HBM)
HIGHEST = lax.Precision.HIGHEST


def f32(*shape):
    return jax.ShapeDtypeStruct(shape, jnp.float32)


def mm(a, b):
    return jnp.dot(a, b, precision=HIGHEST, preferred_element_type=jnp.float32)


def start_all(sems, pairs):
    copies = [pltpu.make_async_copy(src, dst, sems.at[k]) for k, (src, dst) in enumerate(pairs)]
    for copy in copies:
        copy.start()
    return copies


def wait_all(copies):
    for copy in copies:
        copy.wait()


def pack_kernel(src, weights, shifts, neighbors, eig, up, down, own, nb_in, w_in, sh_in, eig_in, sems):
    last = BLOCKS * LANES
    ends = ((up, last - WIDE, last - NEAR), (down, 0, 0))
    pairs = [(neighbors, nb_in), (eig, eig_in)]
    for k, (out, start, near) in enumerate(ends):
        pairs += [
            (weights.at[:, pl.ds(near, NEAR)], w_in.at[k]),
            (shifts.at[:, pl.ds(near, NEAR)], sh_in.at[k]),
            (src.at[:, pl.ds(start, NEAR)], out.at[0:SLAB, 0:NEAR]),
            (src.at[:, pl.ds(start + NEAR, NEAR)], out.at[SLAB : 2 * SLAB, 0:NEAR]),
        ]
    wait_all(start_all(sems, pairs))
    nb = nb_in[...].astype(jnp.float32)
    for k, (out, first) in enumerate(((up, BLOCKS - HALO), (down, 0))):
        out[0:STENCIL, NEAR:WIDE] = w_in[k]
        out[STENCIL:ROWS, NEAR:WIDE] = sh_in[k]
        out[:, WIDE:] = jnp.zeros((ROWS, LANES), jnp.float32)
        out[0:STENCIL, WIDE : WIDE + HALO] = nb[:, first : first + HALO]
    own[...] = jnp.broadcast_to(eig_in[...], own.shape)


def deal_kernel(src, out, sems):
    wait_all(
        start_all(sems, [(src.at[:, pl.ds(r * PART, PART)], out.at[r]) for r in range(PARTS)])
    )


def column(start, block):
    return pl.ds(pl.multiple_of(start + block * LANES, LANES), LANES)


def apply(read, centre, d, weight, offset):
    acc = d * read(centre)
    for s in range(STENCIL):
        moved = read(offset(s) + centre)
        if s:
            moved = pltpu.roll(moved, LANES - s, 1)
        acc = acc - weight(s) * moved
    return acc


def inner_kernel(src, weights, shifts, nb, x1, diag):
    for j in range(BLOCKS):
        cols = slice(j * LANES, (j + 1) * LANES)
        diag[j] = jnp.sum(weights[:, cols], axis=0, keepdims=True) + shifts[:, cols]

    def step(i, _):
        for u in range(UNROLL):
            b = HALO + i * UNROLL + u
            x1[b - HALO] = apply(
                lambda c: src[:, column(0, c)],
                b,
                diag[b],
                lambda s: weights[s : s + 1, column(0, b)],
                lambda s: nb[s, b],
            )
        return 0

    lax.fori_loop(0, (BLOCKS - 2 * HALO) // UNROLL, step, 0)


def stencil_kernel(src, left, right, weights, diag, inner, nb, out, x0, x1, nbv, nbs, sems):
    nbv[0] = left[:, WIDE:].astype(jnp.int32)
    nbv[1] = right[:, WIDE:].astype(jnp.int32)
    copies = start_all(sems, [(nbv.at[k], nbs.at[k]) for k in range(2)])
    for half in range(2):
        rows = slice(half * SLAB, half * SLAB + SLAB)
        for j in range(HALO):
            cols = slice(j * LANES, (j + 1) * LANES)
            x0[half * HALO + j] = left[rows, cols]
            x0[2 * HALO + BLOCKS + half * HALO + j] = right[rows, cols]
    for j in range(BLOCKS):
        x0[2 * HALO + j] = src[:, j * LANES : (j + 1) * LANES]
    for j in range(BLOCKS - 2 * HALO):
        x1[2 * HALO + j] = inner[j]

    def own(b):
        x1[b + HALO] = apply(
            lambda c: x0[c],
            b + 2 * HALO,
            diag[b],
            lambda s: weights[s : s + 1, column(0, b)],
            lambda s: nb[s, b],
        )

    def far(side, ref, j):
        e = j + side * (HALO + BLOCKS)
        x1[e] = apply(
            lambda c: x0[c],
            e + HALO,
            jnp.sum(ref[:, column(NEAR, j)], axis=0, keepdims=True),
            lambda s: ref[s : s + 1, column(NEAR, j)],
            lambda s: nbs[side, s, j],
        )

    def first(i, _):
        for u in range(UNROLL):
            b = i * UNROLL + u
            own(b + jnp.where(b < HALO, 0, BLOCKS - 2 * HALO))
        return 0

    lax.fori_loop(0, 2 * HALO // UNROLL, first, 0)
    wait_all(copies)
    for side, ref in ((0, left), (1, right)):

        def outer(i, _, side=side, ref=ref):
            for u in range(UNROLL):
                far(side, ref, i * UNROLL + u)
            return 0

        lax.fori_loop(0, HALO // UNROLL, outer, 0)

    def second(i, _):
        for u in range(UNROLL):
            b = i * UNROLL + u
            part = lax.div(b, PART // LANES)
            cols = column(0, lax.rem(b, PART // LANES))
            e = b + HALO
            out[part, 0:SLAB, cols] = x1[e]
            out[part, SLAB : 2 * SLAB, cols] = apply(
                lambda c: x1[c],
                e,
                diag[b],
                lambda s: weights[s : s + 1, column(0, b)],
                lambda s: nb[s, b],
            )
        return 0

    lax.fori_loop(0, BLOCKS // UNROLL, second, 0)


def gram_kernel(z0, z12, to_modes, own, out, s):
    eig = own[0:1, :]
    for r in range(PARTS):
        rows = slice(r * SLAB, (r + 1) * SLAB)
        s[rows, 0:PART] = z0[r]
        for q in range(2):
            s[rows, (q + 1) * PART : (q + 2) * PART] = z12[r, q * SLAB : (q + 1) * SLAB, :]
    m = mm(to_modes[...], s[...])
    row = lax.broadcasted_iota(jnp.int32, (MODES, MODES), 0)
    col = lax.broadcasted_iota(jnp.int32, (MODES, MODES), 1)
    e = jnp.sum(jnp.where(row == col, eig, 0.0), axis=1, keepdims=True)
    m0, m1, m2 = (m[:, q * PART : (q + 1) * PART] for q in range(3))
    image = m1 + e * m0
    again = (m2 + e * m1) + e * image
    folded = []
    for a, b in ((m0, m0), (m0, image), (image, image), (m0, again), (image, again), (again, again)):
        p = a * b
        folded.append(sum(p[:, k * LANES : (k + 1) * LANES] for k in range(PART // LANES)))
    stack = jnp.concatenate(folded, axis=1)
    which = lax.broadcasted_iota(jnp.int32, (8, 6 * LANES), 1) // LANES
    pick = (which == lax.broadcasted_iota(jnp.int32, (8, 6 * LANES), 0)).astype(jnp.float32)
    g = lax.dot_general(
        pick, stack, (((1,), (1,)), ((), ())), precision=HIGHEST, preferred_element_type=jnp.float32
    )
    out[...] = jnp.broadcast_to(g[None], out.shape)


def relay_kernel(got, out):
    out[...] = jnp.broadcast_to(jnp.sum(got[...], axis=0)[None], out.shape)


def finish_kernel(got, z0, z12, to_modes, from_modes, own, out, norm, s):
    g = jnp.sum(got[...], axis=0)
    mm_, mi, ii, mj, ij, jj = (g[k : k + 1, :] for k in range(6))
    e = own[0:1, :]
    scale = mm_ + 1e-06
    upper = 1.5 * jnp.sqrt(ii / scale)
    lower = upper * 0.125
    center = (upper + lower) * 0.5
    half_width = (upper - lower) * 0.5
    sigma = center / half_width
    rho_zero = 1.0 / sigma
    rho_one = 1.0 / (2.0 * sigma - rho_zero)
    over = 1.0 / center
    c2 = 2.0 * rho_one / half_width
    u0 = rho_one * rho_zero * over + c2
    u1 = -c2 * over
    a = -over - u0
    b = -u1
    squares = mm_ + a * (2.0 * mi + a * ii) + b * (2.0 * (mj + a * ij) + b * jj)
    norm[...] = jnp.sqrt(jnp.maximum(squares, 0.0) / scale)
    for r in range(PARTS):
        s[r * SLAB : (r + 1) * SLAB, :] = z0[r]
        s[MODES + r * SLAB : MODES + (r + 1) * SLAB, :] = z12[r, 0:SLAB, :]
    from_m = from_modes[...]
    to_m = to_modes[...]
    mix = jnp.concatenate([mm(from_m * (over + u0 + u1 * e), to_m), mm(from_m * u1, to_m)], axis=1)
    out[...] = mm(mix, s[...]).reshape(out.shape)


def unpack_kernel(got, out):
    for r in range(PARTS):
        out[:, r * PART : (r + 1) * PART] = got[r]


def call(kernel, out_shape, in_specs, scratch=()):
    multiple = isinstance(out_shape, tuple)
    return pl.pallas_call(
        kernel,
        out_shape=out_shape,
        in_specs=in_specs,
        out_specs=(VMEM,) * len(out_shape) if multiple else VMEM,
        scratch_shapes=scratch,
        compiler_params=pltpu.CompilerParams(vmem_limit_bytes=32 * 1024 * 1024),
    )


def on_device(sizes, source, to_modes, from_modes, eigenvalue, shifts, weights, neighbors):
    lat = sizes["y"] * sizes["z"]
    shift_row = shifts.reshape(1, -1)
    eig = eigenvalue.reshape(1, -1)
    up, down, own = call(
        pack_kernel,
        (f32(ROWS, WIDE + LANES), f32(ROWS, WIDE + LANES), f32(8, LANES)),
        [HBM] * 5,
        [
            pltpu.VMEM((STENCIL, BLOCKS), jnp.int32),
            pltpu.VMEM((2, STENCIL, NEAR), jnp.float32),
            pltpu.VMEM((2, 1, NEAR), jnp.float32),
            pltpu.VMEM((1, LANES), jnp.float32),
            pltpu.SemaphoreType.DMA((10,)),
        ],
    )(*(pltpu.with_memory_space_constraint(v, pltpu.HBM) for v in (source, weights, shift_row, neighbors, eig)))
    left = lax.ppermute(up, LAT, [(i, (i + 1) % lat) for i in range(lat)])
    right = lax.ppermute(down, LAT, [((i + 1) % lat, i) for i in range(lat)])
    dealt = call(
        deal_kernel, f32(PARTS, SLAB, PART), [HBM], [pltpu.SemaphoreType.DMA((PARTS,))]
    )(pltpu.with_memory_space_constraint(source, pltpu.HBM))
    z0 = lax.all_to_all(dealt, RAD, 0, 0, tiled=True)
    inner, diag = call(
        inner_kernel,
        (f32(BLOCKS - 2 * HALO, SLAB, LANES), f32(BLOCKS, 1, LANES)),
        [VMEM] * 3 + [SMEM],
    )(source, weights, shift_row, neighbors)
    sent = call(
        stencil_kernel,
        f32(PARTS, 2 * SLAB, PART),
        [VMEM] * 6 + [SMEM],
        [
            pltpu.VMEM((EXT2, SLAB, LANES), jnp.float32),
            pltpu.VMEM((EXT1, SLAB, LANES), jnp.float32),
            pltpu.VMEM((2, ROWS, LANES), jnp.int32),
            pltpu.SMEM((2, ROWS, LANES), jnp.int32),
            pltpu.SemaphoreType.DMA((2,)),
        ],
    )(source, left, right, weights, diag, inner, neighbors)
    z12 = lax.all_to_all(sent, RAD, 0, 0, tiled=True)
    peers_1 = sizes["y"] * sizes["x"] * sizes["core"]
    peers_2 = sizes["z"]
    g = call(
        gram_kernel,
        f32(peers_1, 8, LANES),
        [VMEM] * 4,
        [pltpu.VMEM((MODES, 3 * PART), jnp.float32)],
    )(z0, z12, to_modes, own)
    g = lax.all_to_all(g, STAGE_1, 0, 0, tiled=True)
    g = call(relay_kernel, f32(peers_2, 8, LANES), [VMEM])(g)
    g = lax.all_to_all(g, STAGE_2, 0, 0, tiled=True)
    mixed, norm = call(
        finish_kernel,
        (f32(PARTS, SLAB, PART), f32(1, LANES)),
        [VMEM] * 6,
        [pltpu.VMEM((2 * MODES, PART), jnp.float32)],
    )(g, z0, z12, to_modes, from_modes, own)
    got = lax.all_to_all(mixed, RAD, 0, 0, tiled=True)
    smoothed = call(unpack_kernel, f32(SLAB, BLOCKS * LANES), [VMEM])(got)
    residual_norm = lax.dynamic_slice_in_dim(norm[0], lax.axis_index(RAD) * SLAB, SLAB)
    return smoothed, residual_norm


def solution(mesh):
    names = ("y", "z", "x", "core")
    fine = Mesh(np.asarray(mesh.devices).reshape(4, 8, 4, 2), names)
    return jax.shard_map(
        functools.partial(on_device, dict(fine.shape)),
        mesh=fine,
        in_specs=(P(RAD, LAT), P(), P(), P(), P(LAT), P(None, LAT), P(None, LAT)),
        out_specs=(P(RAD, LAT), P(RAD)),
        check_vma=False,
    )
```

time: 89.3 us -> 79.3 us (0.89)
  waiting for transfers between devices: 12.2 us -> 5.95 us
  starting transfers between devices: 14 us -> 19.5 us
  blocking collectives: 41.8 us -> 37.6 us
  local copies, waits for them, and re-layouts: 4.66 us -> 0.61 us
  Pallas kernels: 15.4 us -> 14.3 us
    ppermute x1, waiting for transfers between devices: 6.29 us -> 0.01 us  [on_device(): left = lax.ppermute(up, LAT, [(i, (i + 1) % lat) for i in range(lat)])]
    all_to_all x0 -> x1, starting transfers between devices: none -> 5.39 us  [on_device(): z0 = lax.all_to_all(dealt, RAD, 0, 0, tiled=True)]
    unnamed x14 -> x12, local copies, waits for them, and re-layouts: 4.08 us -> 0.03 us
    all_to_all x1, blocking collectives: 17.7 us -> 14 us  [on_device(): z12 = lax.all_to_all(sent, RAD, 0, 0, tiled=True)]
    pallas_call x3 -> x5, Pallas kernels: 14.5 us -> 12.2 us  [the longest x1 5.52 us: on_device(): call(stencil_kernel, f32(PARTS, 2 * SLAB, PART), [VMEM] * 6 + [SMEM], [pl...]
    pallas_call x1, Pallas kernels: 0.09 us -> 1.31 us  [on_device(): call(pack_kernel, (f32(ROWS, WIDE + LANES), f32(ROWS, WIDE + LANES), f32(...]
  transfers between devices with their start and end apart: 3 -> 4, of which waited for: 2 -> 1; matrix products, arithmetic and copies ran while one was open for 1% -> 1% of each run, Pallas kernels for 0% -> 12%
where the time goes in v1:
time: 79.3 us; the launch traced here: 78.7 us
  blocking collectives  37.6 us (47%)
  starting transfers between devices  19.5 us (25%)
  Pallas kernels  14.3 us (18%)
  waiting for transfers between devices  5.95 us (8%)
    all_to_all x1, blocking collectives, on_device(): z12 = lax.all_to_all(sent, RAD, 0, 0, tiled=True)  14 us
    all_to_all x1, blocking collectives, on_device(): g = lax.all_to_all(g, STAGE_2, 0, 0, tiled=True)  12.2 us
    all_to_all x1, blocking collectives, on_device(): g = lax.all_to_all(g, STAGE_1, 0, 0, tiled=True)  11.4 us
    ppermute x1, starting transfers between devices, on_device(): right = lax.ppermute(down, LAT, [((i + 1) % lat, i) for i in range(lat)])  6.49 us
    all_to_all x1, waiting for transfers between devices, on_device(): got = lax.all_to_all(mixed, RAD, 0, 0, tiled=True)  5.94 us
    pallas_call x1, Pallas kernels, on_device(): call(stencil_kernel, f32(PARTS, 2 * SLAB, PART), [VMEM] * 6 + [SMEM], [pl...  5.52 us
    all_to_all x1, starting transfers between devices, on_device(): z0 = lax.all_to_all(dealt, RAD, 0, 0, tiled=True)  5.39 us
    all_to_all x1, starting transfers between devices, on_device(): got = lax.all_to_all(mixed, RAD, 0, 0, tiled=True)  5.05 us
  transfers between devices with their start and end apart: 4, of which 1 were waited for; matrix products, arithmetic and copies ran while one was open for 1% of the time, Pallas kernels for 12%

profile of v1, /device:TPU:1, one launch (start us, length us, event | category | flops | bytes accessed | tf_op | source)
XLA Modules:
  0.0 78.7 jit_solution(2227371870635178810)
XLA Ops:
  0.6 1.3 %shard_map.87 = (f32[32,2176]{1,0:T(8,128)S(1)}, f32[32,2176]{1,0:T(8,128)S(1)}, f32[8,128]{1,0:T(8,128)S(1)}) custom-call(f32[16,4096]{1,0:T(8,128)} %src.7, f32[31,4096]{1,0:T(8,128)} %weights.5, f32[1,4096]{1,0:T(1,128)} %bitcast.4, s32[31,32]{1,0:T(8,128)} %nb.3, f32[1,128]{1,0:T(1,128)} %bitcast.6), custom_call_target="tpu_custom_call" | custom-call | tf_op jit(solution)/shard_map/pallas_call | solution.py:267
  1.9 2.5 %collective-permute-start = (f32[32,2176]{1,0:T(8,128)S(1)}, f32[32,2176]{1,0:T(8,128)S(1)}, u32[]{:S(2)}, u32[]{:S(2)}) collective-permute-start(f32[32,2176]{1,0:T(8,128)S(1)} %get-tuple-element.9), channel_id=1, source_target_pairs={{0,8},{8,16},{16,24},{24,32},{32,40},{40,48},{48,56},{56,64},{64,7... | collective-permute-start | bytes 835592 | tf_op jit(solution)/shard_map/ppermute | solution.py:279
  4.5 0.0 copy-start
  4.5 6.5 %collective-permute-start.1 = (f32[32,2176]{1,0:T(8,128)S(1)}, f32[32,2176]{1,0:T(8,128)S(1)}, u32[]{:S(2)}, u32[]{:S(2)}) collective-permute-start(f32[32,2176]{1,0:T(8,128)S(1)} %get-tuple-element.10), channel_id=1, source_target_pairs={{8,0},{16,8},{24,16},{32,24},{40,32},{48,40},{56,48},{64,56},{72,6... | collective-permute-start | bytes 835592 | tf_op jit(solution)/shard_map/ppermute | solution.py:280
  11.0 1.6 %shard_map.86 = f32[8,16,512]{2,1,0:T(8,128)} custom-call(f32[16,4096]{1,0:T(8,128)} %src.7), custom_call_target="tpu_custom_call" | custom-call | tf_op jit(solution)/shard_map/pallas_call | solution.py:281
  12.6 0.0 copy-start.1
  12.6 0.0 copy-start.3
  12.7 0.0 copy-start.4
  12.7 5.4 %all-to-all-start = ((f32[8,16,512]{2,1,0:T(8,128)}), f32[8,16,512]{2,1,0:T(8,128)S(1)}, u32[]{:S(2)}, u32[]{:S(2)}) async-start(f32[8,16,512]{2,1,0:T(8,128)} %shard_map.86), calls=%async_computation | async-start | bytes 524288 | tf_op jit(solution)/shard_map/all_to_all | solution.py:284
  18.1 0.0 copy-done
  18.1 0.0 copy-done.1
  18.1 0.0 copy-done.3
  18.1 0.0 copy-done.4
  18.1 2.2 %shard_map.88 = (f32[16,16,128]{2,1,0:T(8,128)S(1)}, f32[32,1,128]{2,1,0:T(1,128)S(1)}) custom-call(f32[16,4096]{1,0:T(8,128)S(1)} %copy-done.1, f32[31,4096]{1,0:T(8,128)S(1)} %copy-done, f32[1,4096]{1,0:T(1,128)S(1)} %bitcast.5, s32[31,32]{1,0:T(8,128)S(1)} %copy-done.3), custom_call_target="tpu_custom_call" | custom-call | tf_op jit(solution)/shard_map/pallas_call | solution.py:285
  20.3 0.0 collective-permute-done.left
  20.3 0.0 collective-permute-done.1.right
  20.3 5.5 %shard_map.89 = f32[8,32,512]{2,1,0:T(8,128)S(1)} custom-call(f32[16,4096]{1,0:T(8,128)S(1)} %copy-done.1, f32[32,2176]{1,0:T(8,128)S(1)} %collective-permute-done.left, f32[32,2176]{1,0:T(8,128)S(1)} %collective-permute-done.1.right, f32[31,4096]{1,0:T(8,128)S(1)} %copy-done, f32[32,1,128]{2,1,0:T(1,128)S(1)} %get-tuple-element.11.diag, ...), custom_call_target="tpu_custom_call" | custom-call | tf_op jit(solution)/shard_map/pallas_call | solution.py:290
  25.8 0.0 copy-start.2
  25.9 0.0 all-to-all-done.z0
  25.9 14.0 %all_to_all.25.z12 = f32[8,32,512]{2,1,0:T(8,128)S(1)} all-to-all(f32[8,32,512]{2,1,0:T(8,128)S(1)} %shard_map.89), channel_id=1, replica_groups=mesh['y'=4,'z'=8,'x'=4,'core'=2] {'x','core'}, dimensions={0} | all-to-all | bytes 1048576 | tf_op jit(solution)/shard_map/all_to_all | solution.py:302
  39.8 0.0 copy-done.2
  39.8 1.5 %shard_map.90 = f32[32,8,128]{2,1,0:T(8,128)S(1)} custom-call(f32[8,16,512]{2,1,0:T(8,128)S(1)} %all-to-all-done.z0, f32[8,32,512]{2,1,0:T(8,128)S(1)} %all_to_all.25.z12, f32[128,128]{1,0:T(8,128)S(1)} %copy-done.2, f32[8,128]{1,0:T(8,128)S(1)} %get-tuple-element.13.own), custom_call_target="tpu_custom_call" | custom-call | tf_op jit(solution)/shard_map/pallas_call | solution.py:305
  41.4 11.4 %all_to_all.26.got = f32[32,8,128]{2,1,0:T(8,128)S(1)} all-to-all(f32[32,8,128]{2,1,0:T(8,128)S(1)} %shard_map.90), channel_id=1, replica_groups=mesh['y'=4,'z'=8,'x'=4,'core'=2] {'y','x','core'}, dimensions={0} | all-to-all | bytes 262144 | tf_op jit(solution)/shard_map/all_to_all | solution.py:311
  52.8 0.0 copy-start.5
  52.8 12.2 %all_to_all.27.got = f32[8,8,128]{2,1,0:T(8,128)S(1)} all-to-all(f32[8,8,128]{2,1,0:T(8,128)S(1)} %shard_map.91), channel_id=1, replica_groups=mesh['y'=4,'z'=8,'x'=4,'core'=2] {'z'}, dimensions={0} | all-to-all | bytes 65536 | tf_op jit(solution)/shard_map/all_to_all | solution.py:313
  65.1 0.0 copy-done.5
  65.1 1.4 %shard_map.92 = (f32[8,16,512]{2,1,0:T(8,128)}, f32[1,128]{1,0:T(1,128)S(1)}) custom-call(f32[8,8,128]{2,1,0:T(8,128)S(1)} %all_to_all.27.got, f32[8,16,512]{2,1,0:T(8,128)S(1)} %all-to-all-done.z0, f32[8,32,512]{2,1,0:T(8,128)S(1)} %all_to_all.25.z12, f32[128,128]{1,0:T(8,128)S(1)} %copy-done.2, f32[128,128]{1,0:T(8,128)S(1)} %copy-done.5, ...), custom_call_target="tpu_custom_call" | custom-call | tf_op jit(solution)/shard_map/pallas_call | solution.py:314
  66.4 5.1 %all-to-all-start.4 = ((f32[8,16,512]{2,1,0:T(8,128)}), f32[8,16,512]{2,1,0:T(8,128)S(1)}, u32[]{:S(2)}, u32[]{:S(2)}) async-start(f32[8,16,512]{2,1,0:T(8,128)} %get-tuple-element.14), calls=%async_computation.4 | async-start | bytes 524288 | tf_op jit(solution)/shard_map/all_to_all | solution.py:320
  71.5 0.6 dynamic-slice_bitcast_fusion
  72.0 5.9 %all-to-all-done.4.got = f32[8,16,512]{2,1,0:T(8,128)S(1)} async-done(((f32[8,16,512]{2,1,0:T(8,128)}), f32[8,16,512]{2,1,0:T(8,128)S(1)}, u32[]{:S(2)}, u32[]{:S(2)}) %all-to-all-start.4) | async-done | bytes 262176 | tf_op jit(solution)/shard_map/all_to_all | solution.py:320
  78.0 0.7 shard_map.93
  (1 shorter events, 0.0 us)
Async XLA Ops:
  1.9 18.4 %collective-permute-start = (f32[32,2176]{1,0:T(8,128)S(1)}, f32[32,2176]{1,0:T(8,128)S(1)}, u32[]{:S(2)}, u32[]{:S(2)}) collective-permute-start(f32[32,2176]{1,0:T(8,128)S(1)} %get-tuple-element.9), channel_id=1, source_target_pairs={{0,8},{8,16},{16,24},{24,32},{32,40},{40,48},{48,56},{56,64},{64,7... | collective-permute-start | bytes 835592 | tf_op jit(solution)/shard_map/ppermute | solution.py:279
  4.5 13.6 %copy-start = (f32[31,4096]{1,0:T(8,128)S(1)}, f32[31,4096]{1,0:T(8,128)}, u32[]{:S(2)}) copy-start(f32[31,4096]{1,0:T(8,128)} %weights.5) | copy-start | bytes 1523716
  4.5 15.8 %collective-permute-start.1 = (f32[32,2176]{1,0:T(8,128)S(1)}, f32[32,2176]{1,0:T(8,128)S(1)}, u32[]{:S(2)}, u32[]{:S(2)}) collective-permute-start(f32[32,2176]{1,0:T(8,128)S(1)} %get-tuple-element.10), channel_id=1, source_target_pairs={{8,0},{16,8},{24,16},{32,24},{40,32},{48,40},{56,48},{64,56},{72,6... | collective-permute-start | bytes 835592 | tf_op jit(solution)/shard_map/ppermute | solution.py:280
  12.6 5.4 %copy-start.1 = (f32[16,4096]{1,0:T(8,128)S(1)}, f32[16,4096]{1,0:T(8,128)}, u32[]{:S(2)}) copy-start(f32[16,4096]{1,0:T(8,128)} %src.7) | copy-start | bytes 786436
  12.6 5.4 %copy-start.3 = (s32[31,32]{1,0:T(8,128)S(1)}, s32[31,32]{1,0:T(8,128)}, u32[]{:S(2)}) copy-start(s32[31,32]{1,0:T(8,128)} %nb.3) | copy-start | bytes 11908
  12.7 5.4 %copy-start.4 = (f32[4096]{0:T(1024)S(1)}, f32[4096]{0:T(1024)}, u32[]{:S(2)}) copy-start(f32[4096]{0:T(1024)} %param.11) | copy-start | bytes 49156
  12.7 13.2 %all-to-all-start = ((f32[8,16,512]{2,1,0:T(8,128)}), f32[8,16,512]{2,1,0:T(8,128)S(1)}, u32[]{:S(2)}, u32[]{:S(2)}) async-start(f32[8,16,512]{2,1,0:T(8,128)} %shard_map.86), calls=%async_computation | async-start | bytes 524288 | tf_op jit(solution)/shard_map/all_to_all | solution.py:284
  25.8 14.0 %copy-start.2 = (f32[128,128]{1,0:T(8,128)S(1)}, f32[128,128]{1,0:T(8,128)}, u32[]{:S(2)}) copy-start(f32[128,128]{1,0:T(8,128)} %to_modes.3) | copy-start | bytes 196612
  52.8 12.2 %copy-start.5 = (f32[128,128]{1,0:T(8,128)S(1)}, f32[128,128]{1,0:T(8,128)}, u32[]{:S(2)}) copy-start(f32[128,128]{1,0:T(8,128)} %from_modes.1) | copy-start | bytes 196612
  66.4 11.6 %all-to-all-start.4 = ((f32[8,16,512]{2,1,0:T(8,128)}), f32[8,16,512]{2,1,0:T(8,128)S(1)}, u32[]{:S(2)}, u32[]{:S(2)}) async-start(f32[8,16,512]{2,1,0:T(8,128)} %get-tuple-element.14), calls=%async_computation.4 | async-start | bytes 524288 | tf_op jit(solution)/shard_map/all_to_all | solution.py:320

commit v2 on v1

--- a/solution.py
+++ b/solution.py
@@ -52,7 +52,7 @@
         copy.wait()
 
 
-def pack_kernel(src, weights, shifts, neighbors, eig, up, down, own, nb_in, w_in, sh_in, eig_in, sems):
+def pack_kernel(src, weights, shifts, neighbors, eig, up, down, own, dealt, nb_in, w_in, sh_in, eig_in, sems):
     last = BLOCKS * LANES
     ends = ((up, last - WIDE, last - NEAR), (down, 0, 0))
     pairs = [(neighbors, nb_in), (eig, eig_in)]
@@ -63,6 +63,7 @@
             (src.at[:, pl.ds(start, NEAR)], out.at[0:SLAB, 0:NEAR]),
             (src.at[:, pl.ds(start + NEAR, NEAR)], out.at[SLAB : 2 * SLAB, 0:NEAR]),
         ]
+    pairs += [(src.at[:, pl.ds(r * PART, PART)], dealt.at[r]) for r in range(PARTS)]
     wait_all(start_all(sems, pairs))
     nb = nb_in[...].astype(jnp.float32)
     for k, (out, first) in enumerate(((up, BLOCKS - HALO), (down, 0))):
@@ -73,12 +74,6 @@
     own[...] = jnp.broadcast_to(eig_in[...], own.shape)
 
 
-def deal_kernel(src, out, sems):
-    wait_all(
-        start_all(sems, [(src.at[:, pl.ds(r * PART, PART)], out.at[r]) for r in range(PARTS)])
-    )
-
-
 def column(start, block):
     return pl.ds(pl.multiple_of(start + block * LANES, LANES), LANES)
 
@@ -93,7 +88,8 @@
     return acc
 
 
-def inner_kernel(src, weights, shifts, nb, x1, diag):
+def inner_kernel(src, weights, shifts, nb, place_in, x1, diag, place):
+    place[0] = place_in[0]
     for j in range(BLOCKS):
         cols = slice(j * LANES, (j + 1) * LANES)
         diag[j] = jnp.sum(weights[:, cols], axis=0, keepdims=True) + shifts[:, cols]
@@ -214,7 +210,7 @@
     out[...] = jnp.broadcast_to(jnp.sum(got[...], axis=0)[None], out.shape)
 
 
-def finish_kernel(got, z0, z12, to_modes, from_modes, own, out, norm, s):
+def finish_kernel(place, got, z0, z12, to_modes, from_modes, own, out, mine, s):
     g = jnp.sum(got[...], axis=0)
     mm_, mi, ii, mj, ij, jj = (g[k : k + 1, :] for k in range(6))
     e = own[0:1, :]
@@ -233,7 +229,8 @@
     a = -over - u0
     b = -u1
     squares = mm_ + a * (2.0 * mi + a * ii) + b * (2.0 * (mj + a * ij) + b * jj)
-    norm[...] = jnp.sqrt(jnp.maximum(squares, 0.0) / scale)
+    norm = jnp.broadcast_to(jnp.sqrt(jnp.maximum(squares, 0.0) / scale), (8, LANES))
+    mine[...] = pltpu.roll(norm, LANES - place[0] * SLAB, 1)[0:1, 0:SLAB]
     for r in range(PARTS):
         s[r * SLAB : (r + 1) * SLAB, :] = z0[r]
         s[MODES + r * SLAB : MODES + (r + 1) * SLAB, :] = z12[r, 0:SLAB, :]
@@ -248,13 +245,14 @@
         out[:, r * PART : (r + 1) * PART] = got[r]
 
 
-def call(kernel, out_shape, in_specs, scratch=()):
-    multiple = isinstance(out_shape, tuple)
+def call(kernel, out_shape, in_specs, scratch=(), out_specs=None):
+    if out_specs is None:
+        out_specs = (VMEM,) * len(out_shape) if isinstance(out_shape, tuple) else VMEM
     return pl.pallas_call(
         kernel,
         out_shape=out_shape,
         in_specs=in_specs,
-        out_specs=(VMEM,) * len(out_shape) if multiple else VMEM,
+        out_specs=out_specs,
         scratch_shapes=scratch,
         compiler_params=pltpu.CompilerParams(vmem_limit_bytes=32 * 1024 * 1024),
     )
@@ -262,31 +260,34 @@
 
 def on_device(sizes, source, to_modes, from_modes, eigenvalue, shifts, weights, neighbors):
     lat = sizes["y"] * sizes["z"]
+    place = lax.axis_index(RAD).astype(jnp.int32).reshape(1)
     shift_row = shifts.reshape(1, -1)
     eig = eigenvalue.reshape(1, -1)
-    up, down, own = call(
+    up, down, own, dealt = call(
         pack_kernel,
-        (f32(ROWS, WIDE + LANES), f32(ROWS, WIDE + LANES), f32(8, LANES)),
+        (f32(ROWS, WIDE + LANES), f32(ROWS, WIDE + LANES), f32(8, LANES), f32(PARTS, SLAB, PART)),
         [HBM] * 5,
         [
             pltpu.VMEM((STENCIL, BLOCKS), jnp.int32),
             pltpu.VMEM((2, STENCIL, NEAR), jnp.float32),
             pltpu.VMEM((2, 1, NEAR), jnp.float32),
             pltpu.VMEM((1, LANES), jnp.float32),
-            pltpu.SemaphoreType.DMA((10,)),
+            pltpu.SemaphoreType.DMA((10 + PARTS,)),
         ],
     )(*(pltpu.with_memory_space_constraint(v, pltpu.HBM) for v in (source, weights, shift_row, neighbors, eig)))
     left = lax.ppermute(up, LAT, [(i, (i + 1) % lat) for i in range(lat)])
     right = lax.ppermute(down, LAT, [((i + 1) % lat, i) for i in range(lat)])
-    dealt = call(
-        deal_kernel, f32(PARTS, SLAB, PART), [HBM], [pltpu.SemaphoreType.DMA((PARTS,))]
-    )(pltpu.with_memory_space_constraint(source, pltpu.HBM))
     z0 = lax.all_to_all(dealt, RAD, 0, 0, tiled=True)
-    inner, diag = call(
+    inner, diag, place = call(
         inner_kernel,
-        (f32(BLOCKS - 2 * HALO, SLAB, LANES), f32(BLOCKS, 1, LANES)),
-        [VMEM] * 3 + [SMEM],
-    )(source, weights, shift_row, neighbors)
+        (
+            f32(BLOCKS - 2 * HALO, SLAB, LANES),
+            f32(BLOCKS, 1, LANES),
+            jax.ShapeDtypeStruct((1,), jnp.int32),
+        ),
+        [VMEM] * 3 + [SMEM] * 2,
+        out_specs=(VMEM, VMEM, SMEM),
+    )(source, weights, shift_row, neighbors, place)
     sent = call(
         stencil_kernel,
         f32(PARTS, 2 * SLAB, PART),
@@ -311,16 +312,15 @@
     g = lax.all_to_all(g, STAGE_1, 0, 0, tiled=True)
     g = call(relay_kernel, f32(peers_2, 8, LANES), [VMEM])(g)
     g = lax.all_to_all(g, STAGE_2, 0, 0, tiled=True)
-    mixed, norm = call(
+    mixed, residual_norm = call(
         finish_kernel,
-        (f32(PARTS, SLAB, PART), f32(1, LANES)),
-        [VMEM] * 6,
+        (f32(PARTS, SLAB, PART), f32(1, SLAB)),
+        [SMEM] + [VMEM] * 6,
         [pltpu.VMEM((2 * MODES, PART), jnp.float32)],
-    )(g, z0, z12, to_modes, from_modes, own)
+    )(place, g, z0, z12, to_modes, from_modes, own)
     got = lax.all_to_all(mixed, RAD, 0, 0, tiled=True)
     smoothed = call(unpack_kernel, f32(SLAB, BLOCKS * LANES), [VMEM])(got)
-    residual_norm = lax.dynamic_slice_in_dim(norm[0], lax.axis_index(RAD) * SLAB, SLAB)
-    return smoothed, residual_norm
+    return smoothed, residual_norm.reshape(SLAB)
 
 
 def solution(mesh):

time: 79.3 us -> 78.8 us (level)
  blocking collectives: 37.6 us -> 48.2 us
  waiting for transfers between devices: 5.95 us -> 0.01 us
  starting transfers between devices: 19.5 us -> 14.4 us
    all_to_all x0 -> x1, blocking collectives: none -> 10.6 us  [on_device(): got = lax.all_to_all(mixed, RAD, 0, 0, tiled=True)]
    all_to_all x1 -> x0, waiting for transfers between devices: 5.94 us -> none  [on_device(): got = lax.all_to_all(mixed, RAD, 0, 0, tiled=True)]
    all_to_all x1 -> x0, starting transfers between devices: 5.05 us -> none  [on_device(): got = lax.all_to_all(mixed, RAD, 0, 0, tiled=True)]
    pallas_call x2 -> x1, Pallas kernels: 3 us -> 1.72 us  [on_device(): call(finish_kernel, (f32(PARTS, SLAB, PART), f32(1, SLAB)), [SMEM] + [VME...]
  transfers between devices with their start and end apart: 4 -> 3, of which waited for: 1 -> 0; matrix products, arithmetic and copies ran while one was open for 1% -> 0% of each run, Pallas kernels for 12% -> 10%
where the time goes in v2:
time: 78.8 us; the launch traced here: 78.4 us
  blocking collectives  48.2 us (61%)
  starting transfers between devices  14.4 us (18%)
  Pallas kernels  14.3 us (18%)
    all_to_all x1, blocking collectives, on_device(): z12 = lax.all_to_all(sent, RAD, 0, 0, tiled=True)  14 us
    all_to_all x1, blocking collectives, on_device(): g = lax.all_to_all(g, STAGE_2, 0, 0, tiled=True)  12.2 us
    all_to_all x1, blocking collectives, on_device(): g = lax.all_to_all(g, STAGE_1, 0, 0, tiled=True)  11.4 us
    all_to_all x1, blocking collectives, on_device(): got = lax.all_to_all(mixed, RAD, 0, 0, tiled=True)  10.6 us
    ppermute x1, starting transfers between devices, on_device(): right = lax.ppermute(down, LAT, [((i + 1) % lat, i) for i in range(lat)])  6.48 us
    pallas_call x1, Pallas kernels, on_device(): call(stencil_kernel, f32(PARTS, 2 * SLAB, PART), [VMEM] * 6 + [SMEM], [pl...  5.52 us
    all_to_all x1, starting transfers between devices, on_device(): z0 = lax.all_to_all(dealt, RAD, 0, 0, tiled=True)  5.38 us
    pallas_call x1, Pallas kernels, on_device(): call(inner_kernel, (f32(BLOCKS - 2 * HALO, SLAB, LANES), f32(BLOCKS, 1, L...  2.69 us
  transfers between devices with their start and end apart: 3, of which 0 were waited for; matrix products, arithmetic and copies ran while one was open for 0% of the time, Pallas kernels for 10%

profile of v2, /device:TPU:1, one launch (start us, length us, event | category | flops | bytes accessed | tf_op | source)
XLA Modules:
  0.0 78.4 jit_solution(4015514332696765634)
XLA Ops:
  0.6 0.0 copy-start
  0.6 2.1 %shard_map.87 = (f32[32,2176]{1,0:T(8,128)S(1)}, f32[32,2176]{1,0:T(8,128)S(1)}, f32[8,128]{1,0:T(8,128)S(1)}, f32[8,16,512]{2,1,0:T(8,128)}) custom-call(f32[16,4096]{1,0:T(8,128)} %src.5, f32[31,4096]{1,0:T(8,128)} %weights.5, f32[1,4096]{1,0:T(1,128)} %bitcast.4, s32[31,32]{1,0:T(8,128)} %nb.3, f32[1,128]{1,0:T(1,128)} %bitcast.6), custom_call_target="tpu_custom_call" | custom-call | tf_op jit(solution)/shard_map/pallas_call | solution.py:266
  2.7 2.5 %collective-permute-start = (f32[32,2176]{1,0:T(8,128)S(1)}, f32[32,2176]{1,0:T(8,128)S(1)}, u32[]{:S(2)}, u32[]{:S(2)}) collective-permute-start(f32[32,2176]{1,0:T(8,128)S(1)} %get-tuple-element.13), channel_id=1, source_target_pairs={{0,8},{8,16},{16,24},{24,32},{32,40},{40,48},{48,56},{56,64},{64,7... | collective-permute-start | bytes 835592 | tf_op jit(solution)/shard_map/ppermute | solution.py:278
  5.2 6.5 %collective-permute-start.1 = (f32[32,2176]{1,0:T(8,128)S(1)}, f32[32,2176]{1,0:T(8,128)S(1)}, u32[]{:S(2)}, u32[]{:S(2)}) collective-permute-start(f32[32,2176]{1,0:T(8,128)S(1)} %get-tuple-element.14), channel_id=1, source_target_pairs={{8,0},{16,8},{24,16},{32,24},{40,32},{48,40},{56,48},{64,56},{72,6... | collective-permute-start | bytes 835592 | tf_op jit(solution)/shard_map/ppermute | solution.py:279
  11.7 0.0 copy-start.1
  11.7 0.0 copy-start.5
  11.7 5.4 %all-to-all-start = ((f32[8,16,512]{2,1,0:T(8,128)}), f32[8,16,512]{2,1,0:T(8,128)S(1)}, u32[]{:S(2)}, u32[]{:S(2)}) async-start(f32[8,16,512]{2,1,0:T(8,128)} %get-tuple-element.12), calls=%async_computation | async-start | bytes 524288 | tf_op jit(solution)/shard_map/all_to_all | solution.py:280
  17.1 0.0 copy-start.3
  17.1 0.0 copy-done
  17.1 0.0 copy-done.1
  17.1 0.0 copy-done.5
  17.1 0.7 copy-done.3
  17.8 2.7 %shard_map.86 = (f32[16,16,128]{2,1,0:T(8,128)S(1)}, f32[32,1,128]{2,1,0:T(1,128)S(1)}, s32[1]{0:T(128)}) custom-call(f32[16,4096]{1,0:T(8,128)S(1)} %copy-done.1, f32[31,4096]{1,0:T(8,128)S(1)} %copy-done, f32[1,4096]{1,0:T(1,128)S(1)} %bitcast.5, s32[31,32]{1,0:T(8,128)S(1)} %copy-done.3, s32[1]{0:T(128)} %bitcast.1.place_in), custom_call_target="tpu_custom_call" | custom-call | tf_op jit(solution)/shard_map/pallas_call | solution.py:281
  20.5 0.0 collective-permute-done.left
  20.5 0.0 collective-permute-done.1.right
  20.5 5.5 %shard_map.88 = f32[8,32,512]{2,1,0:T(8,128)S(1)} custom-call(f32[16,4096]{1,0:T(8,128)S(1)} %copy-done.1, f32[32,2176]{1,0:T(8,128)S(1)} %collective-permute-done.left, f32[32,2176]{1,0:T(8,128)S(1)} %collective-permute-done.1.right, f32[31,4096]{1,0:T(8,128)S(1)} %copy-done, f32[32,1,128]{2,1,0:T(1,128)S(1)} %get-tuple-element.15.diag, ...), custom_call_target="tpu_custom_call" | custom-call | tf_op jit(solution)/shard_map/pallas_call | solution.py:291
  26.1 0.0 copy-start.2
  26.1 0.0 all-to-all-done.z0
  26.1 14.0 %all_to_all.25.z12 = f32[8,32,512]{2,1,0:T(8,128)S(1)} all-to-all(f32[8,32,512]{2,1,0:T(8,128)S(1)} %shard_map.88), channel_id=1, replica_groups=mesh['y'=4,'z'=8,'x'=4,'core'=2] {'x','core'}, dimensions={0} | all-to-all | bytes 1048576 | tf_op jit(solution)/shard_map/all_to_all | solution.py:303
  40.1 0.0 copy-done.2
  40.1 1.5 %shard_map.89 = f32[32,8,128]{2,1,0:T(8,128)S(1)} custom-call(f32[8,16,512]{2,1,0:T(8,128)S(1)} %all-to-all-done.z0, f32[8,32,512]{2,1,0:T(8,128)S(1)} %all_to_all.25.z12, f32[128,128]{1,0:T(8,128)S(1)} %copy-done.2, f32[8,128]{1,0:T(8,128)S(1)} %get-tuple-element.17.own), custom_call_target="tpu_custom_call" | custom-call | tf_op jit(solution)/shard_map/pallas_call | solution.py:306
  41.6 11.4 %all_to_all.26.got = f32[32,8,128]{2,1,0:T(8,128)S(1)} all-to-all(f32[32,8,128]{2,1,0:T(8,128)S(1)} %shard_map.89), channel_id=1, replica_groups=mesh['y'=4,'z'=8,'x'=4,'core'=2] {'y','x','core'}, dimensions={0} | all-to-all | bytes 262144 | tf_op jit(solution)/shard_map/all_to_all | solution.py:312
  53.1 0.0 copy-start.4
  53.1 12.2 %all_to_all.27.got = f32[8,8,128]{2,1,0:T(8,128)S(1)} all-to-all(f32[8,8,128]{2,1,0:T(8,128)S(1)} %shard_map.90), channel_id=1, replica_groups=mesh['y'=4,'z'=8,'x'=4,'core'=2] {'z'}, dimensions={0} | all-to-all | bytes 65536 | tf_op jit(solution)/shard_map/all_to_all | solution.py:314
  65.3 0.0 copy-done.4
  65.3 1.7 %shard_map.91 = (f32[8,16,512]{2,1,0:T(8,128)S(1)}, f32[1,16]{1,0:T(1,128)}) custom-call(s32[1]{0:T(128)} %get-tuple-element.11.place, f32[8,8,128]{2,1,0:T(8,128)S(1)} %all_to_all.27.got, f32[8,16,512]{2,1,0:T(8,128)S(1)} %all-to-all-done.z0, f32[8,32,512]{2,1,0:T(8,128)S(1)} %all_to_all.25.z12, f32[128,128]{1,0:T(8,128)S(1)} %copy-done.2, ...), custom_call_target="tpu_custom_call" | custom-call | tf_op jit(solution)/shard_map/pallas_call | solution.py:315
  67.0 10.6 %all_to_all.28.got = f32[8,16,512]{2,1,0:T(8,128)S(1)} all-to-all(f32[8,16,512]{2,1,0:T(8,128)S(1)} %get-tuple-element.18), channel_id=1, replica_groups=mesh['y'=4,'z'=8,'x'=4,'core'=2] {'x','core'}, dimensions={0} | all-to-all | bytes 524288 | tf_op jit(solution)/shard_map/all_to_all | solution.py:321
  77.6 0.7 shard_map.92
  (1 shorter events, 0.0 us)
Async XLA Ops:
  0.6 16.5 %copy-start = (f32[31,4096]{1,0:T(8,128)S(1)}, f32[31,4096]{1,0:T(8,128)}, u32[]{:S(2)}) copy-start(f32[31,4096]{1,0:T(8,128)} %weights.5) | copy-start | bytes 1523716
  2.7 17.8 %collective-permute-start = (f32[32,2176]{1,0:T(8,128)S(1)}, f32[32,2176]{1,0:T(8,128)S(1)}, u32[]{:S(2)}, u32[]{:S(2)}) collective-permute-start(f32[32,2176]{1,0:T(8,128)S(1)} %get-tuple-element.13), channel_id=1, source_target_pairs={{0,8},{8,16},{16,24},{24,32},{32,40},{40,48},{48,56},{56,64},{64,7... | collective-permute-start | bytes 835592 | tf_op jit(solution)/shard_map/ppermute | solution.py:278
  5.2 15.3 %collective-permute-start.1 = (f32[32,2176]{1,0:T(8,128)S(1)}, f32[32,2176]{1,0:T(8,128)S(1)}, u32[]{:S(2)}, u32[]{:S(2)}) collective-permute-start(f32[32,2176]{1,0:T(8,128)S(1)} %get-tuple-element.14), channel_id=1, source_target_pairs={{8,0},{16,8},{24,16},{32,24},{40,32},{48,40},{56,48},{64,56},{72,6... | collective-permute-start | bytes 835592 | tf_op jit(solution)/shard_map/ppermute | solution.py:279
  11.7 5.4 %copy-start.1 = (f32[16,4096]{1,0:T(8,128)S(1)}, f32[16,4096]{1,0:T(8,128)}, u32[]{:S(2)}) copy-start(f32[16,4096]{1,0:T(8,128)} %src.5) | copy-start | bytes 786436
  11.7 5.4 %copy-start.5 = (f32[4096]{0:T(1024)S(1)}, f32[4096]{0:T(1024)}, u32[]{:S(2)}) copy-start(f32[4096]{0:T(1024)} %param.11) | copy-start | bytes 49156
  11.7 14.4 %all-to-all-start = ((f32[8,16,512]{2,1,0:T(8,128)}), f32[8,16,512]{2,1,0:T(8,128)S(1)}, u32[]{:S(2)}, u32[]{:S(2)}) async-start(f32[8,16,512]{2,1,0:T(8,128)} %get-tuple-element.12), calls=%async_computation | async-start | bytes 524288 | tf_op jit(solution)/shard_map/all_to_all | solution.py:280
  17.1 0.7 copy-start.3
  26.1 14.0 %copy-start.2 = (f32[128,128]{1,0:T(8,128)S(1)}, f32[128,128]{1,0:T(8,128)}, u32[]{:S(2)}) copy-start(f32[128,128]{1,0:T(8,128)} %to_modes.3) | copy-start | bytes 196612
  53.1 12.2 %copy-start.4 = (f32[128,128]{1,0:T(8,128)S(1)}, f32[128,128]{1,0:T(8,128)}, u32[]{:S(2)}) copy-start(f32[128,128]{1,0:T(8,128)} %from_modes.1) | copy-start | bytes 196612

commit v3 on v2

--- a/solution.py
+++ b/solution.py
@@ -36,8 +36,15 @@
     return jax.ShapeDtypeStruct(shape, jnp.float32)
 
 
+def split(a):
+    high = a.astype(jnp.bfloat16)
+    return high, (a - high.astype(jnp.float32)).astype(jnp.bfloat16)
+
+
 def mm(a, b):
-    return jnp.dot(a, b, precision=HIGHEST, preferred_element_type=jnp.float32)
+    (ah, al), (bh, bl) = split(a), split(b)
+    dot = functools.partial(jnp.dot, preferred_element_type=jnp.float32)
+    return dot(ah, bh) + (dot(ah, bl) + dot(al, bh))
 
 
 def start_all(sems, pairs):
@@ -64,7 +71,8 @@
             (src.at[:, pl.ds(start + NEAR, NEAR)], out.at[SLAB : 2 * SLAB, 0:NEAR]),
         ]
     pairs += [(src.at[:, pl.ds(r * PART, PART)], dealt.at[r]) for r in range(PARTS)]
-    wait_all(start_all(sems, pairs))
+    copies = start_all(sems, pairs)
+    wait_all(copies[: -PARTS])
     nb = nb_in[...].astype(jnp.float32)
     for k, (out, first) in enumerate(((up, BLOCKS - HALO), (down, 0))):
         out[0:STENCIL, NEAR:WIDE] = w_in[k]
@@ -72,6 +80,7 @@
         out[:, WIDE:] = jnp.zeros((ROWS, LANES), jnp.float32)
         out[0:STENCIL, WIDE : WIDE + HALO] = nb[:, first : first + HALO]
     own[...] = jnp.broadcast_to(eig_in[...], own.shape)
+    wait_all(copies[-PARTS:])
 
 
 def column(start, block):
@@ -88,11 +97,13 @@
     return acc
 
 
-def inner_kernel(src, weights, shifts, nb, place_in, x1, diag, place):
-    place[0] = place_in[0]
+def inner_kernel(src, weights, shifts, nb_in, place_in, x1, diag, place, nb, sems):
+    copies = start_all(sems, [(nb_in, nb)])
+    place[...] = place_in[...]
     for j in range(BLOCKS):
         cols = slice(j * LANES, (j + 1) * LANES)
         diag[j] = jnp.sum(weights[:, cols], axis=0, keepdims=True) + shifts[:, cols]
+    wait_all(copies)
 
     def step(i, _):
         for u in range(UNROLL):
@@ -109,10 +120,10 @@
     lax.fori_loop(0, (BLOCKS - 2 * HALO) // UNROLL, step, 0)
 
 
-def stencil_kernel(src, left, right, weights, diag, inner, nb, out, x0, x1, nbv, nbs, sems):
+def stencil_kernel(src, left, right, weights, diag, inner, nb_in, out, x0, x1, nbv, nbs, nb, sems):
     nbv[0] = left[:, WIDE:].astype(jnp.int32)
     nbv[1] = right[:, WIDE:].astype(jnp.int32)
-    copies = start_all(sems, [(nbv.at[k], nbs.at[k]) for k in range(2)])
+    copies = start_all(sems, [(nb_in, nb)] + [(nbv.at[k], nbs.at[k]) for k in range(2)])
     for half in range(2):
         rows = slice(half * SLAB, half * SLAB + SLAB)
         for j in range(HALO):
@@ -149,8 +160,9 @@
             own(b + jnp.where(b < HALO, 0, BLOCKS - 2 * HALO))
         return 0
 
+    copies[0].wait()
     lax.fori_loop(0, 2 * HALO // UNROLL, first, 0)
-    wait_all(copies)
+    wait_all(copies[1:])
     for side, ref in ((0, left), (1, right)):
 
         def outer(i, _, side=side, ref=ref):
@@ -229,8 +241,12 @@
     a = -over - u0
     b = -u1
     squares = mm_ + a * (2.0 * mi + a * ii) + b * (2.0 * (mj + a * ij) + b * jj)
-    norm = jnp.broadcast_to(jnp.sqrt(jnp.maximum(squares, 0.0) / scale), (8, LANES))
-    mine[...] = pltpu.roll(norm, LANES - place[0] * SLAB, 1)[0:1, 0:SLAB]
+    norm = jnp.sqrt(jnp.maximum(squares, 0.0) / scale)
+    here = place[0:1, 0:SLAB]
+    picked = norm[:, 0:SLAB]
+    for r in range(1, PARTS):
+        picked = jnp.where(here == r, norm[:, r * SLAB : (r + 1) * SLAB], picked)
+    mine[...] = picked
     for r in range(PARTS):
         s[r * SLAB : (r + 1) * SLAB, :] = z0[r]
         s[MODES + r * SLAB : MODES + (r + 1) * SLAB, :] = z12[r, 0:SLAB, :]
@@ -240,9 +256,10 @@
     out[...] = mm(mix, s[...]).reshape(out.shape)
 
 
-def unpack_kernel(got, out):
-    for r in range(PARTS):
-        out[:, r * PART : (r + 1) * PART] = got[r]
+def unpack_kernel(got, out, sems):
+    wait_all(
+        start_all(sems, [(got.at[r], out.at[:, pl.ds(r * PART, PART)]) for r in range(PARTS)])
+    )
 
 
 def call(kernel, out_shape, in_specs, scratch=(), out_specs=None):
@@ -258,9 +275,13 @@
     )
 
 
+def pinned(value):
+    return pltpu.with_memory_space_constraint(value, pltpu.HBM)
+
+
 def on_device(sizes, source, to_modes, from_modes, eigenvalue, shifts, weights, neighbors):
     lat = sizes["y"] * sizes["z"]
-    place = lax.axis_index(RAD).astype(jnp.int32).reshape(1)
+    place = jnp.full((8, LANES), lax.axis_index(RAD).astype(jnp.float32))
     shift_row = shifts.reshape(1, -1)
     eig = eigenvalue.reshape(1, -1)
     up, down, own, dealt = call(
@@ -274,7 +295,8 @@
             pltpu.VMEM((1, LANES), jnp.float32),
             pltpu.SemaphoreType.DMA((10 + PARTS,)),
         ],
-    )(*(pltpu.with_memory_space_constraint(v, pltpu.HBM) for v in (source, weights, shift_row, neighbors, eig)))
+        out_specs=(VMEM, VMEM, VMEM, HBM),
+    )(*(pinned(v) for v in (source, weights, shift_row, neighbors, eig)))
     left = lax.ppermute(up, LAT, [(i, (i + 1) % lat) for i in range(lat)])
     right = lax.ppermute(down, LAT, [((i + 1) % lat, i) for i in range(lat)])
     z0 = lax.all_to_all(dealt, RAD, 0, 0, tiled=True)
@@ -283,23 +305,24 @@
         (
             f32(BLOCKS - 2 * HALO, SLAB, LANES),
             f32(BLOCKS, 1, LANES),
-            jax.ShapeDtypeStruct((1,), jnp.int32),
+            f32(8, LANES),
         ),
-        [VMEM] * 3 + [SMEM] * 2,
-        out_specs=(VMEM, VMEM, SMEM),
-    )(source, weights, shift_row, neighbors, place)
+        [VMEM] * 3 + [HBM, VMEM],
+        [pltpu.SMEM((STENCIL, BLOCKS), jnp.int32), pltpu.SemaphoreType.DMA((1,))],
+    )(source, weights, shift_row, pinned(neighbors), place)
     sent = call(
         stencil_kernel,
         f32(PARTS, 2 * SLAB, PART),
-        [VMEM] * 6 + [SMEM],
+        [VMEM] * 6 + [HBM],
         [
             pltpu.VMEM((EXT2, SLAB, LANES), jnp.float32),
             pltpu.VMEM((EXT1, SLAB, LANES), jnp.float32),
             pltpu.VMEM((2, ROWS, LANES), jnp.int32),
             pltpu.SMEM((2, ROWS, LANES), jnp.int32),
-            pltpu.SemaphoreType.DMA((2,)),
+            pltpu.SMEM((STENCIL, BLOCKS), jnp.int32),
+            pltpu.SemaphoreType.DMA((3,)),
         ],
-    )(source, left, right, weights, diag, inner, neighbors)
+    )(source, left, right, weights, diag, inner, pinned(neighbors))
     z12 = lax.all_to_all(sent, RAD, 0, 0, tiled=True)
     peers_1 = sizes["y"] * sizes["x"] * sizes["core"]
     peers_2 = sizes["z"]
@@ -315,11 +338,17 @@
     mixed, residual_norm = call(
         finish_kernel,
         (f32(PARTS, SLAB, PART), f32(1, SLAB)),
-        [SMEM] + [VMEM] * 6,
+        [VMEM] * 7,
         [pltpu.VMEM((2 * MODES, PART), jnp.float32)],
     )(place, g, z0, z12, to_modes, from_modes, own)
     got = lax.all_to_all(mixed, RAD, 0, 0, tiled=True)
-    smoothed = call(unpack_kernel, f32(SLAB, BLOCKS * LANES), [VMEM])(got)
+    smoothed = call(
+        unpack_kernel,
+        f32(SLAB, BLOCKS * LANES),
+        [VMEM],
+        [pltpu.SemaphoreType.DMA((PARTS,))],
+        out_specs=HBM,
+    )(got)
     return smoothed, residual_norm.reshape(SLAB)
 
 

time: 78.8 us -> 85 us (1.079)
  Pallas kernels: 14.3 us -> 20.2 us
    pallas_call x1, Pallas kernels: 2.05 us -> 9.22 us  [on_device(): call(pack_kernel, (f32(ROWS, WIDE + LANES), f32(ROWS, WIDE + LANES), f32(...]
  transfers between devices with their start and end apart: 3 -> 3, of which waited for: 0 -> 0; matrix products, arithmetic and copies ran while one was open for 0% -> 0% of each run, Pallas kernels for 10% -> 9%
where the time goes in v3:
time: 85 us; the launch traced here: 84.3 us
  blocking collectives  48.2 us (57%)
  Pallas kernels  20.2 us (24%)
  starting transfers between devices  14.4 us (17%)
    all_to_all x1, blocking collectives, on_device(): z12 = lax.all_to_all(sent, RAD, 0, 0, tiled=True)  14 us
    all_to_all x1, blocking collectives, on_device(): g = lax.all_to_all(g, STAGE_2, 0, 0, tiled=True)  12.2 us
    all_to_all x1, blocking collectives, on_device(): g = lax.all_to_all(g, STAGE_1, 0, 0, tiled=True)  11.4 us
    all_to_all x1, blocking collectives, on_device(): got = lax.all_to_all(mixed, RAD, 0, 0, tiled=True)  10.6 us
    pallas_call x1, Pallas kernels, on_device(): call(pack_kernel, (f32(ROWS, WIDE + LANES), f32(ROWS, WIDE + LANES), f32(...  9.22 us
    ppermute x1, starting transfers between devices, on_device(): right = lax.ppermute(down, LAT, [((i + 1) % lat, i) for i in range(lat)])  6.48 us
    pallas_call x1, Pallas kernels, on_device(): call(stencil_kernel, f32(PARTS, 2 * SLAB, PART), [VMEM] * 6 + [HBM], [plt...  5.59 us
    all_to_all x1, starting transfers between devices, on_device(): z0 = lax.all_to_all(dealt, RAD, 0, 0, tiled=True)  5.38 us
  transfers between devices with their start and end apart: 3, of which 0 were waited for; matrix products, arithmetic and copies ran while one was open for 0% of the time, Pallas kernels for 9%

profile of v3, /device:TPU:1, one launch (start us, length us, event | category | flops | bytes accessed | tf_op | source)
XLA Modules:
  0.0 84.3 jit_solution(2126788310896370439)
XLA Ops:
  0.6 0.0 copy-start
  0.6 9.2 %shard_map.87 = (f32[32,2176]{1,0:T(8,128)S(1)}, f32[32,2176]{1,0:T(8,128)S(1)}, f32[8,128]{1,0:T(8,128)S(1)}, f32[8,16,512]{2,1,0:T(8,128)}) custom-call(f32[16,4096]{1,0:T(8,128)} %src.5, f32[31,4096]{1,0:T(8,128)} %weights.5, f32[1,4096]{1,0:T(1,128)} %bitcast.3, s32[31,32]{1,0:T(8,128)} %nb_in.3, f32[1,128]{1,0:T(1,128)} %bitcast.5), custom_call_target="tpu_custom_call" | custom-call | tf_op jit(solution)/shard_map/pallas_call | solution.py:287
  9.9 2.5 %collective-permute-start = (f32[32,2176]{1,0:T(8,128)S(1)}, f32[32,2176]{1,0:T(8,128)S(1)}, u32[]{:S(2)}, u32[]{:S(2)}) collective-permute-start(f32[32,2176]{1,0:T(8,128)S(1)} %get-tuple-element.13), channel_id=1, source_target_pairs={{0,8},{8,16},{16,24},{24,32},{32,40},{40,48},{48,56},{56,64},{64,7... | collective-permute-start | bytes 835592 | tf_op jit(solution)/shard_map/ppermute | solution.py:300
  12.4 6.5 %collective-permute-start.1 = (f32[32,2176]{1,0:T(8,128)S(1)}, f32[32,2176]{1,0:T(8,128)S(1)}, u32[]{:S(2)}, u32[]{:S(2)}) collective-permute-start(f32[32,2176]{1,0:T(8,128)S(1)} %get-tuple-element.14), channel_id=1, source_target_pairs={{8,0},{16,8},{24,16},{32,24},{40,32},{48,40},{56,48},{64,56},{72,6... | collective-permute-start | bytes 835592 | tf_op jit(solution)/shard_map/ppermute | solution.py:301
  18.9 0.0 copy-start.1
  18.9 5.4 %all-to-all-start = ((f32[8,16,512]{2,1,0:T(8,128)}), f32[8,16,512]{2,1,0:T(8,128)S(1)}, u32[]{:S(2)}, u32[]{:S(2)}) async-start(f32[8,16,512]{2,1,0:T(8,128)} %get-tuple-element.12), calls=%async_computation | async-start | bytes 524288 | tf_op jit(solution)/shard_map/all_to_all | solution.py:302
  24.3 0.0 copy-start.3
  24.3 0.0 copy-done
  24.3 0.0 copy-done.1
  24.3 0.7 copy-done.3
  25.0 2.4 %shard_map.86 = (f32[16,16,128]{2,1,0:T(8,128)S(1)}, f32[32,1,128]{2,1,0:T(1,128)S(1)}, f32[8,128]{1,0:T(8,128)S(1)}) custom-call(f32[16,4096]{1,0:T(8,128)S(1)} %copy-done.1, f32[31,4096]{1,0:T(8,128)S(1)} %copy-done, f32[1,4096]{1,0:T(1,128)S(1)} %bitcast.4, s32[31,32]{1,0:T(8,128)} %nb_in.3, f32[8,128]{1,0:T(8,128)S(1)} %broadcast_in_dim.3.place_in), custom_call_target="tpu_custom_call" | custom-call | tf_op jit(solution)/shard_map/pallas_call | solution.py:303
  27.4 0.0 collective-permute-done.left
  27.4 0.0 collective-permute-done.1.right
  27.4 5.6 %shard_map.88 = f32[8,32,512]{2,1,0:T(8,128)S(1)} custom-call(f32[16,4096]{1,0:T(8,128)S(1)} %copy-done.1, f32[32,2176]{1,0:T(8,128)S(1)} %collective-permute-done.left, f32[32,2176]{1,0:T(8,128)S(1)} %collective-permute-done.1.right, f32[31,4096]{1,0:T(8,128)S(1)} %copy-done, f32[32,1,128]{2,1,0:T(1,128)S(1)} %get-tuple-element.15.diag, ...), custom_call_target="tpu_custom_call" | custom-call | tf_op jit(solution)/shard_map/pallas_call | solution.py:313
  33.0 0.0 copy-start.2
  33.0 0.0 all-to-all-done.z0
  33.0 14.0 %all_to_all.25.z12 = f32[8,32,512]{2,1,0:T(8,128)S(1)} all-to-all(f32[8,32,512]{2,1,0:T(8,128)S(1)} %shard_map.88), channel_id=1, replica_groups=mesh['y'=4,'z'=8,'x'=4,'core'=2] {'x','core'}, dimensions={0} | all-to-all | bytes 1048576 | tf_op jit(solution)/shard_map/all_to_all | solution.py:326
  47.0 0.0 copy-done.2
  47.0 1.4 %shard_map.89 = f32[32,8,128]{2,1,0:T(8,128)S(1)} custom-call(f32[8,16,512]{2,1,0:T(8,128)S(1)} %all-to-all-done.z0, f32[8,32,512]{2,1,0:T(8,128)S(1)} %all_to_all.25.z12, f32[128,128]{1,0:T(8,128)S(1)} %copy-done.2, f32[8,128]{1,0:T(8,128)S(1)} %get-tuple-element.17.own), custom_call_target="tpu_custom_call" | custom-call | tf_op jit(solution)/shard_map/pallas_call | solution.py:329
  48.4 11.4 %all_to_all.26.got = f32[32,8,128]{2,1,0:T(8,128)S(1)} all-to-all(f32[32,8,128]{2,1,0:T(8,128)S(1)} %shard_map.89), channel_id=1, replica_groups=mesh['y'=4,'z'=8,'x'=4,'core'=2] {'y','x','core'}, dimensions={0} | all-to-all | bytes 262144 | tf_op jit(solution)/shard_map/all_to_all | solution.py:335
  59.8 0.0 copy-start.4
  59.8 12.2 %all_to_all.27.got = f32[8,8,128]{2,1,0:T(8,128)S(1)} all-to-all(f32[8,8,128]{2,1,0:T(8,128)S(1)} %shard_map.90), channel_id=1, replica_groups=mesh['y'=4,'z'=8,'x'=4,'core'=2] {'z'}, dimensions={0} | all-to-all | bytes 65536 | tf_op jit(solution)/shard_map/all_to_all | solution.py:337
  72.1 0.0 copy-done.4
  72.1 0.9 %shard_map.91 = (f32[8,16,512]{2,1,0:T(8,128)S(1)}, f32[1,16]{1,0:T(1,128)}) custom-call(f32[8,128]{1,0:T(8,128)S(1)} %get-tuple-element.11.place, f32[8,8,128]{2,1,0:T(8,128)S(1)} %all_to_all.27.got, f32[8,16,512]{2,1,0:T(8,128)S(1)} %all-to-all-done.z0, f32[8,32,512]{2,1,0:T(8,128)S(1)} %all_to_all.25.z12, f32[128,128]{1,0:T(8,128)S(1)} %copy-done.2, ...), custom_call_target="tpu_custom_call" | custom-call | tf_op jit(solution)/shard_map/pallas_call | solution.py:338
  73.0 10.6 %all_to_all.28.got = f32[8,16,512]{2,1,0:T(8,128)S(1)} all-to-all(f32[8,16,512]{2,1,0:T(8,128)S(1)} %get-tuple-element.18), channel_id=1, replica_groups=mesh['y'=4,'z'=8,'x'=4,'core'=2] {'x','core'}, dimensions={0} | all-to-all | bytes 524288 | tf_op jit(solution)/shard_map/all_to_all | solution.py:344
  83.6 0.8 shard_map.92
  (2 shorter events, 0.0 us)
Async XLA Ops:
  0.6 23.7 %copy-start = (f32[31,4096]{1,0:T(8,128)S(1)}, f32[31,4096]{1,0:T(8,128)}, u32[]{:S(2)}) copy-start(f32[31,4096]{1,0:T(8,128)} %weights.5) | copy-start | bytes 1523716
  9.9 17.5 %collective-permute-start = (f32[32,2176]{1,0:T(8,128)S(1)}, f32[32,2176]{1,0:T(8,128)S(1)}, u32[]{:S(2)}, u32[]{:S(2)}) collective-permute-start(f32[32,2176]{1,0:T(8,128)S(1)} %get-tuple-element.13), channel_id=1, source_target_pairs={{0,8},{8,16},{16,24},{24,32},{32,40},{40,48},{48,56},{56,64},{64,7... | collective-permute-start | bytes 835592 | tf_op jit(solution)/shard_map/ppermute | solution.py:300
  12.4 15.0 %collective-permute-start.1 = (f32[32,2176]{1,0:T(8,128)S(1)}, f32[32,2176]{1,0:T(8,128)S(1)}, u32[]{:S(2)}, u32[]{:S(2)}) collective-permute-start(f32[32,2176]{1,0:T(8,128)S(1)} %get-tuple-element.14), channel_id=1, source_target_pairs={{8,0},{16,8},{24,16},{32,24},{40,32},{48,40},{56,48},{64,56},{72,6... | collective-permute-start | bytes 835592 | tf_op jit(solution)/shard_map/ppermute | solution.py:301
  18.9 5.4 %copy-start.1 = (f32[16,4096]{1,0:T(8,128)S(1)}, f32[16,4096]{1,0:T(8,128)}, u32[]{:S(2)}) copy-start(f32[16,4096]{1,0:T(8,128)} %src.5) | copy-start | bytes 786436
  18.9 14.1 %all-to-all-start = ((f32[8,16,512]{2,1,0:T(8,128)}), f32[8,16,512]{2,1,0:T(8,128)S(1)}, u32[]{:S(2)}, u32[]{:S(2)}) async-start(f32[8,16,512]{2,1,0:T(8,128)} %get-tuple-element.12), calls=%async_computation | async-start | bytes 524288 | tf_op jit(solution)/shard_map/all_to_all | solution.py:302
  24.3 0.7 copy-start.3
  33.0 14.0 %copy-start.2 = (f32[128,128]{1,0:T(8,128)S(1)}, f32[128,128]{1,0:T(8,128)}, u32[]{:S(2)}) copy-start(f32[128,128]{1,0:T(8,128)} %to_modes.3) | copy-start | bytes 196612
  59.8 12.2 %copy-start.4 = (f32[128,128]{1,0:T(8,128)S(1)}, f32[128,128]{1,0:T(8,128)}, u32[]{:S(2)}) copy-start(f32[128,128]{1,0:T(8,128)} %from_modes.1) | copy-start | bytes 196612

commit v4 on v3

--- a/solution.py
+++ b/solution.py
@@ -59,28 +59,25 @@
         copy.wait()
 
 
-def pack_kernel(src, weights, shifts, neighbors, eig, up, down, own, dealt, nb_in, w_in, sh_in, eig_in, sems):
+def pack_kernel(src, weights, shifts, neighbors, eig, up, down, own, nb_in, sh_in, w_in, eig_in, sems):
     last = BLOCKS * LANES
     ends = ((up, last - WIDE, last - NEAR), (down, 0, 0))
-    pairs = [(neighbors, nb_in), (eig, eig_in)]
+    pairs = [(neighbors, nb_in), (eig, eig_in), (shifts, sh_in)]
     for k, (out, start, near) in enumerate(ends):
         pairs += [
             (weights.at[:, pl.ds(near, NEAR)], w_in.at[k]),
-            (shifts.at[:, pl.ds(near, NEAR)], sh_in.at[k]),
             (src.at[:, pl.ds(start, NEAR)], out.at[0:SLAB, 0:NEAR]),
             (src.at[:, pl.ds(start + NEAR, NEAR)], out.at[SLAB : 2 * SLAB, 0:NEAR]),
         ]
-    pairs += [(src.at[:, pl.ds(r * PART, PART)], dealt.at[r]) for r in range(PARTS)]
-    copies = start_all(sems, pairs)
-    wait_all(copies[: -PARTS])
+    wait_all(start_all(sems, pairs))
     nb = nb_in[...].astype(jnp.float32)
     for k, (out, first) in enumerate(((up, BLOCKS - HALO), (down, 0))):
+        near = first * LANES
         out[0:STENCIL, NEAR:WIDE] = w_in[k]
-        out[STENCIL:ROWS, NEAR:WIDE] = sh_in[k]
+        out[STENCIL:ROWS, NEAR:WIDE] = sh_in[:, near : near + NEAR]
         out[:, WIDE:] = jnp.zeros((ROWS, LANES), jnp.float32)
         out[0:STENCIL, WIDE : WIDE + HALO] = nb[:, first : first + HALO]
     own[...] = jnp.broadcast_to(eig_in[...], own.shape)
-    wait_all(copies[-PARTS:])
 
 
 def column(start, block):
@@ -97,9 +94,11 @@
     return acc
 
 
-def inner_kernel(src, weights, shifts, nb_in, place_in, x1, diag, place, nb, sems):
+def inner_kernel(src, weights, shifts, nb_in, place_in, x1, diag, place, dealt, nb, sems):
     copies = start_all(sems, [(nb_in, nb)])
     place[...] = place_in[...]
+    for r in range(PARTS):
+        dealt[r] = src[:, r * PART : (r + 1) * PART]
     for j in range(BLOCKS):
         cols = slice(j * LANES, (j + 1) * LANES)
         diag[j] = jnp.sum(weights[:, cols], axis=0, keepdims=True) + shifts[:, cols]
@@ -256,10 +255,9 @@
     out[...] = mm(mix, s[...]).reshape(out.shape)
 
 
-def unpack_kernel(got, out, sems):
-    wait_all(
-        start_all(sems, [(got.at[r], out.at[:, pl.ds(r * PART, PART)]) for r in range(PARTS)])
-    )
+def unpack_kernel(got, out):
+    for r in range(PARTS):
+        out[:, r * PART : (r + 1) * PART] = got[r]
 
 
 def call(kernel, out_shape, in_specs, scratch=(), out_specs=None):
@@ -284,36 +282,35 @@
     place = jnp.full((8, LANES), lax.axis_index(RAD).astype(jnp.float32))
     shift_row = shifts.reshape(1, -1)
     eig = eigenvalue.reshape(1, -1)
-    up, down, own, dealt = call(
+    up, down, own, nb, shift_row = call(
         pack_kernel,
-        (f32(ROWS, WIDE + LANES), f32(ROWS, WIDE + LANES), f32(8, LANES), f32(PARTS, SLAB, PART)),
+        (f32(ROWS, WIDE + LANES), f32(ROWS, WIDE + LANES), f32(8, LANES),
+         jax.ShapeDtypeStruct(neighbors.shape, neighbors.dtype), f32(1, BLOCKS * LANES)),
         [HBM] * 5,
         [
-            pltpu.VMEM((STENCIL, BLOCKS), jnp.int32),
             pltpu.VMEM((2, STENCIL, NEAR), jnp.float32),
-            pltpu.VMEM((2, 1, NEAR), jnp.float32),
             pltpu.VMEM((1, LANES), jnp.float32),
-            pltpu.SemaphoreType.DMA((10 + PARTS,)),
+            pltpu.SemaphoreType.DMA((9,)),
         ],
-        out_specs=(VMEM, VMEM, VMEM, HBM),
     )(*(pinned(v) for v in (source, weights, shift_row, neighbors, eig)))
     left = lax.ppermute(up, LAT, [(i, (i + 1) % lat) for i in range(lat)])
     right = lax.ppermute(down, LAT, [((i + 1) % lat, i) for i in range(lat)])
-    z0 = lax.all_to_all(dealt, RAD, 0, 0, tiled=True)
-    inner, diag, place = call(
+    inner, diag, place, dealt = call(
         inner_kernel,
         (
             f32(BLOCKS - 2 * HALO, SLAB, LANES),
             f32(BLOCKS, 1, LANES),
             f32(8, LANES),
+            f32(PARTS, SLAB, PART),
         ),
-        [VMEM] * 3 + [HBM, VMEM],
+        [VMEM] * 5,
         [pltpu.SMEM((STENCIL, BLOCKS), jnp.int32), pltpu.SemaphoreType.DMA((1,))],
-    )(source, weights, shift_row, pinned(neighbors), place)
+    )(source, weights, shift_row, nb, place)
+    z0 = lax.all_to_all(dealt, RAD, 0, 0, tiled=True)
     sent = call(
         stencil_kernel,
         f32(PARTS, 2 * SLAB, PART),
-        [VMEM] * 6 + [HBM],
+        [VMEM] * 7,
         [
             pltpu.VMEM((EXT2, SLAB, LANES), jnp.float32),
             pltpu.VMEM((EXT1, SLAB, LANES), jnp.float32),
@@ -322,7 +319,7 @@
             pltpu.SMEM((STENCIL, BLOCKS), jnp.int32),
             pltpu.SemaphoreType.DMA((3,)),
         ],
-    )(source, left, right, weights, diag, inner, pinned(neighbors))
+    )(source, left, right, weights, diag, inner, nb)
     z12 = lax.all_to_all(sent, RAD, 0, 0, tiled=True)
     peers_1 = sizes["y"] * sizes["x"] * sizes["core"]
     peers_2 = sizes["z"]
@@ -342,13 +339,7 @@
         [pltpu.VMEM((2 * MODES, PART), jnp.float32)],
     )(place, g, z0, z12, to_modes, from_modes, own)
     got = lax.all_to_all(mixed, RAD, 0, 0, tiled=True)
-    smoothed = call(
-        unpack_kernel,
-        f32(SLAB, BLOCKS * LANES),
-        [VMEM],
-        [pltpu.SemaphoreType.DMA((PARTS,))],
-        out_specs=HBM,
-    )(got)
+    smoothed = call(unpack_kernel, f32(SLAB, BLOCKS * LANES), [VMEM])(got)
     return smoothed, residual_norm.reshape(SLAB)
 
 

time: 85 us -> 76.4 us (0.90)
  Pallas kernels: 20.2 us -> 12.8 us
  blocking collectives: 48.2 us -> 47.2 us
  waiting for transfers between devices: 0.01 us -> 1 us
    pallas_call x1, Pallas kernels: 9.22 us -> 1.35 us  [on_device(): call(pack_kernel, (f32(ROWS, WIDE + LANES), f32(ROWS, WIDE + LANES), f32(...]
    all_to_all x1, waiting for transfers between devices: 0.01 us -> 1 us  [on_device(): z0 = lax.all_to_all(dealt, RAD, 0, 0, tiled=True)]
    all_to_all x1, blocking collectives: 14 us -> 13 us  [on_device(): z12 = lax.all_to_all(sent, RAD, 0, 0, tiled=True)]
  transfers between devices with their start and end apart: 3 -> 3, of which waited for: 0 -> 1; matrix products, arithmetic and copies ran while one was open for 0% -> 0% of each run, Pallas kernels for 9% -> 11%
where the time goes in v4:
time: 76.4 us; the launch traced here: 76 us
  blocking collectives  47.2 us (62%)
  starting transfers between devices  14.3 us (19%)
  Pallas kernels  12.8 us (17%)
  waiting for transfers between devices  1 us (1%)
    all_to_all x1, blocking collectives, on_device(): z12 = lax.all_to_all(sent, RAD, 0, 0, tiled=True)  13 us
    all_to_all x1, blocking collectives, on_device(): g = lax.all_to_all(g, STAGE_2, 0, 0, tiled=True)  12.2 us
    all_to_all x1, blocking collectives, on_device(): g = lax.all_to_all(g, STAGE_1, 0, 0, tiled=True)  11.4 us
    all_to_all x1, blocking collectives, on_device(): got = lax.all_to_all(mixed, RAD, 0, 0, tiled=True)  10.6 us
    ppermute x1, starting transfers between devices, on_device(): right = lax.ppermute(down, LAT, [((i + 1) % lat, i) for i in range(lat)])  6.48 us
    pallas_call x1, Pallas kernels, on_device(): call(stencil_kernel, f32(PARTS, 2 * SLAB, PART), [VMEM] * 7, [pltpu.VMEM(...  5.48 us
    all_to_all x1, starting transfers between devices, on_device(): z0 = lax.all_to_all(dealt, RAD, 0, 0, tiled=True)  5.26 us
    pallas_call x1, Pallas kernels, on_device(): call(inner_kernel, (f32(BLOCKS - 2 * HALO, SLAB, LANES), f32(BLOCKS, 1, L...  2.91 us
  transfers between devices with their start and end apart: 3, of which 1 were waited for; matrix products, arithmetic and copies ran while one was open for 0% of the time, Pallas kernels for 11%

profile of v4, /device:TPU:1, one launch (start us, length us, event | category | flops | bytes accessed | tf_op | source)
XLA Modules:
  0.0 76.0 jit_solution(16683098141891223525)
XLA Ops:
  0.6 0.0 copy-start
  0.6 0.0 copy-start.1
  0.7 1.4 %shard_map.86 = (f32[32,2176]{1,0:T(8,128)S(1)}, f32[32,2176]{1,0:T(8,128)S(1)}, f32[8,128]{1,0:T(8,128)S(1)}, s32[31,32]{1,0:T(8,128)S(1)}, f32[1,4096]{1,0:T(1,128)S(1)}) custom-call(f32[16,4096]{1,0:T(8,128)} %src.5, f32[31,4096]{1,0:T(8,128)} %weights.5, f32[1,4096]{1,0:T(1,128)} %bitcast.3, s32[31,32]{1,0:T(8,128)} %neighbors.1, f32[1,128]{1,0:T(1,128)} %bitcast.4), custom_call_target="tpu_custom_call" | custom-call | tf_op jit(solution)/shard_map/pallas_call | solution.py:285
  2.0 2.5 %collective-permute-start = (f32[32,2176]{1,0:T(8,128)S(1)}, f32[32,2176]{1,0:T(8,128)S(1)}, u32[]{:S(2)}, u32[]{:S(2)}) collective-permute-start(f32[32,2176]{1,0:T(8,128)S(1)} %get-tuple-element.17), channel_id=1, source_target_pairs={{0,8},{8,16},{16,24},{24,32},{32,40},{40,48},{48,56},{56,64},{64,7... | collective-permute-start | bytes 835592 | tf_op jit(solution)/shard_map/ppermute | solution.py:296
  4.6 6.5 %collective-permute-start.1 = (f32[32,2176]{1,0:T(8,128)S(1)}, f32[32,2176]{1,0:T(8,128)S(1)}, u32[]{:S(2)}, u32[]{:S(2)}) collective-permute-start(f32[32,2176]{1,0:T(8,128)S(1)} %get-tuple-element.18), channel_id=1, source_target_pairs={{8,0},{16,8},{24,16},{32,24},{40,32},{48,40},{56,48},{64,56},{72,6... | collective-permute-start | bytes 835592 | tf_op jit(solution)/shard_map/ppermute | solution.py:297
  11.0 0.0 copy-done
  11.0 0.0 copy-done.1
  11.0 2.9 %shard_map.87 = (f32[16,16,128]{2,1,0:T(8,128)S(1)}, f32[32,1,128]{2,1,0:T(1,128)S(1)}, f32[8,128]{1,0:T(8,128)S(1)}, f32[8,16,512]{2,1,0:T(8,128)}) custom-call(f32[16,4096]{1,0:T(8,128)S(1)} %copy-done.1, f32[31,4096]{1,0:T(8,128)S(1)} %copy-done, f32[1,4096]{1,0:T(1,128)S(1)} %get-tuple-element.13.shifts, s32[31,32]{1,0:T(8,128)S(1)} %get-tuple-element.14.nb_in, ...), custom_call_target="tpu_custom_call" | custom-call | tf_op jit(solution)/shard_map/pallas_call | solution.py:298
  14.0 5.3 %all-to-all-start = ((f32[8,16,512]{2,1,0:T(8,128)}), f32[8,16,512]{2,1,0:T(8,128)S(1)}, u32[]{:S(2)}, u32[]{:S(2)}) async-start(f32[8,16,512]{2,1,0:T(8,128)} %get-tuple-element.16), calls=%async_computation | async-start | bytes 524288 | tf_op jit(solution)/shard_map/all_to_all | solution.py:309
  19.2 0.0 collective-permute-done.left
  19.2 0.0 collective-permute-done.1.right
  19.2 5.5 %shard_map.88 = f32[8,32,512]{2,1,0:T(8,128)S(1)} custom-call(f32[16,4096]{1,0:T(8,128)S(1)} %copy-done.1, f32[32,2176]{1,0:T(8,128)S(1)} %collective-permute-done.left, f32[32,2176]{1,0:T(8,128)S(1)} %collective-permute-done.1.right, f32[31,4096]{1,0:T(8,128)S(1)} %copy-done, f32[32,1,128]{2,1,0:T(1,128)S(1)} %get-tuple-element.19.diag, ...), custom_call_target="tpu_custom_call" | custom-call | tf_op jit(solution)/shard_map/pallas_call | solution.py:310
  24.7 0.0 copy-start.2
  24.7 1.0 %all-to-all-done.z0 = f32[8,16,512]{2,1,0:T(8,128)S(1)} async-done(((f32[8,16,512]{2,1,0:T(8,128)}), f32[8,16,512]{2,1,0:T(8,128)S(1)}, u32[]{:S(2)}, u32[]{:S(2)}) %all-to-all-start) | async-done | bytes 262176 | tf_op jit(solution)/shard_map/all_to_all | solution.py:309
  25.7 13.0 %all_to_all.25.z12 = f32[8,32,512]{2,1,0:T(8,128)S(1)} all-to-all(f32[8,32,512]{2,1,0:T(8,128)S(1)} %shard_map.88), channel_id=1, replica_groups=mesh['y'=4,'z'=8,'x'=4,'core'=2] {'x','core'}, dimensions={0} | all-to-all | bytes 1048576 | tf_op jit(solution)/shard_map/all_to_all | solution.py:323
  38.7 0.0 copy-done.2
  38.7 1.4 %shard_map.89 = f32[32,8,128]{2,1,0:T(8,128)S(1)} custom-call(f32[8,16,512]{2,1,0:T(8,128)S(1)} %all-to-all-done.z0, f32[8,32,512]{2,1,0:T(8,128)S(1)} %all_to_all.25.z12, f32[128,128]{1,0:T(8,128)S(1)} %copy-done.2, f32[8,128]{1,0:T(8,128)S(1)} %get-tuple-element.21.own), custom_call_target="tpu_custom_call" | custom-call | tf_op jit(solution)/shard_map/pallas_call | solution.py:326
  40.1 11.4 %all_to_all.26.got = f32[32,8,128]{2,1,0:T(8,128)S(1)} all-to-all(f32[32,8,128]{2,1,0:T(8,128)S(1)} %shard_map.89), channel_id=1, replica_groups=mesh['y'=4,'z'=8,'x'=4,'core'=2] {'y','x','core'}, dimensions={0} | all-to-all | bytes 262144 | tf_op jit(solution)/shard_map/all_to_all | solution.py:332
  51.5 0.0 copy-start.3
  51.6 12.2 %all_to_all.27.got = f32[8,8,128]{2,1,0:T(8,128)S(1)} all-to-all(f32[8,8,128]{2,1,0:T(8,128)S(1)} %shard_map.90), channel_id=1, replica_groups=mesh['y'=4,'z'=8,'x'=4,'core'=2] {'z'}, dimensions={0} | all-to-all | bytes 65536 | tf_op jit(solution)/shard_map/all_to_all | solution.py:334
  63.8 0.0 copy-done.3
  63.8 0.9 %shard_map.91 = (f32[8,16,512]{2,1,0:T(8,128)S(1)}, f32[1,16]{1,0:T(1,128)}) custom-call(f32[8,128]{1,0:T(8,128)S(1)} %get-tuple-element.15.place, f32[8,8,128]{2,1,0:T(8,128)S(1)} %all_to_all.27.got, f32[8,16,512]{2,1,0:T(8,128)S(1)} %all-to-all-done.z0, f32[8,32,512]{2,1,0:T(8,128)S(1)} %all_to_all.25.z12, f32[128,128]{1,0:T(8,128)S(1)} %copy-done.2, ...), custom_call_target="tpu_custom_call" | custom-call | tf_op jit(solution)/shard_map/pallas_call | solution.py:335
  64.7 10.6 %all_to_all.28.got = f32[8,16,512]{2,1,0:T(8,128)S(1)} all-to-all(f32[8,16,512]{2,1,0:T(8,128)S(1)} %get-tuple-element.22), channel_id=1, replica_groups=mesh['y'=4,'z'=8,'x'=4,'core'=2] {'x','core'}, dimensions={0} | all-to-all | bytes 524288 | tf_op jit(solution)/shard_map/all_to_all | solution.py:341
  75.3 0.7 shard_map.92
  (2 shorter events, 0.0 us)
Async XLA Ops:
  0.6 10.4 %copy-start = (f32[31,4096]{1,0:T(8,128)S(1)}, f32[31,4096]{1,0:T(8,128)}, u32[]{:S(2)}) copy-start(f32[31,4096]{1,0:T(8,128)} %weights.5) | copy-start | bytes 1523716
  0.6 10.4 %copy-start.1 = (f32[16,4096]{1,0:T(8,128)S(1)}, f32[16,4096]{1,0:T(8,128)}, u32[]{:S(2)}) copy-start(f32[16,4096]{1,0:T(8,128)} %src.5) | copy-start | bytes 786436
  2.0 17.2 %collective-permute-start = (f32[32,2176]{1,0:T(8,128)S(1)}, f32[32,2176]{1,0:T(8,128)S(1)}, u32[]{:S(2)}, u32[]{:S(2)}) collective-permute-start(f32[32,2176]{1,0:T(8,128)S(1)} %get-tuple-element.17), channel_id=1, source_target_pairs={{0,8},{8,16},{16,24},{24,32},{32,40},{40,48},{48,56},{56,64},{64,7... | collective-permute-start | bytes 835592 | tf_op jit(solution)/shard_map/ppermute | solution.py:296
  4.6 14.7 %collective-permute-start.1 = (f32[32,2176]{1,0:T(8,128)S(1)}, f32[32,2176]{1,0:T(8,128)S(1)}, u32[]{:S(2)}, u32[]{:S(2)}) collective-permute-start(f32[32,2176]{1,0:T(8,128)S(1)} %get-tuple-element.18), channel_id=1, source_target_pairs={{8,0},{16,8},{24,16},{32,24},{40,32},{48,40},{56,48},{64,56},{72,6... | collective-permute-start | bytes 835592 | tf_op jit(solution)/shard_map/ppermute | solution.py:297
  14.0 11.8 %all-to-all-start = ((f32[8,16,512]{2,1,0:T(8,128)}), f32[8,16,512]{2,1,0:T(8,128)S(1)}, u32[]{:S(2)}, u32[]{:S(2)}) async-start(f32[8,16,512]{2,1,0:T(8,128)} %get-tuple-element.16), calls=%async_computation | async-start | bytes 524288 | tf_op jit(solution)/shard_map/all_to_all | solution.py:309
  24.7 14.0 %copy-start.2 = (f32[128,128]{1,0:T(8,128)S(1)}, f32[128,128]{1,0:T(8,128)}, u32[]{:S(2)}) copy-start(f32[128,128]{1,0:T(8,128)} %to_modes.3) | copy-start | bytes 196612
  51.5 12.2 %copy-start.3 = (f32[128,128]{1,0:T(8,128)S(1)}, f32[128,128]{1,0:T(8,128)}, u32[]{:S(2)}) copy-start(f32[128,128]{1,0:T(8,128)} %from_modes.1) | copy-start | bytes 196612

commit v5 on v4

--- a/solution.py
+++ b/solution.py
@@ -20,12 +20,11 @@
 PARTS = 8
 PART = BLOCKS * LANES // PARTS
 MODES = 128
+FLAT = SLAB * PART // LANES
 WIDE = 2 * HALO * LANES
 NEAR = HALO * LANES
 LAT = ("y", "z")
 RAD = ("x", "core")
-STAGE_1 = ("y", "x", "core")
-STAGE_2 = "z"
 VMEM = pl.BlockSpec(memory_space=pltpu.VMEM)
 SMEM = pl.BlockSpec(memory_space=pltpu.SMEM)
 HBM = pl.BlockSpec(memory_space=pltpu.HBM)
@@ -119,10 +118,8 @@
     lax.fori_loop(0, (BLOCKS - 2 * HALO) // UNROLL, step, 0)
 
 
-def stencil_kernel(src, left, right, weights, diag, inner, nb_in, out, x0, x1, nbv, nbs, nb, sems):
-    nbv[0] = left[:, WIDE:].astype(jnp.int32)
-    nbv[1] = right[:, WIDE:].astype(jnp.int32)
-    copies = start_all(sems, [(nb_in, nb)] + [(nbv.at[k], nbs.at[k]) for k in range(2)])
+def edge_kernel(src, left, right, weights, diag, inner, nb_in, out, x0, x1, nb, sems):
+    copies = start_all(sems, [(nb_in, nb)])
     for half in range(2):
         rows = slice(half * SLAB, half * SLAB + SLAB)
         for j in range(HALO):
@@ -131,97 +128,110 @@
             x0[2 * HALO + BLOCKS + half * HALO + j] = right[rows, cols]
     for j in range(BLOCKS):
         x0[2 * HALO + j] = src[:, j * LANES : (j + 1) * LANES]
-    for j in range(BLOCKS - 2 * HALO):
-        x1[2 * HALO + j] = inner[j]
-
-    def own(b):
-        x1[b + HALO] = apply(
-            lambda c: x0[c],
-            b + 2 * HALO,
-            diag[b],
-            lambda s: weights[s : s + 1, column(0, b)],
-            lambda s: nb[s, b],
-        )
-
-    def far(side, ref, j):
-        e = j + side * (HALO + BLOCKS)
-        x1[e] = apply(
-            lambda c: x0[c],
-            e + HALO,
-            jnp.sum(ref[:, column(NEAR, j)], axis=0, keepdims=True),
-            lambda s: ref[s : s + 1, column(NEAR, j)],
-            lambda s: nbs[side, s, j],
-        )
-
-    def first(i, _):
+    for j in range(HALO, BLOCKS - HALO):
+        x1[j] = inner[j - HALO]
+        part, place = divmod(j, PART // LANES)
+        out[part, :, place * LANES : (place + 1) * LANES] = inner[j - HALO]
+    wait_all(copies)
+
+    def step(i, _):
+        for u in range(UNROLL):
+            b = i * (BLOCKS - HALO) + u
+            value = apply(
+                lambda c: x0[c],
+                b + 2 * HALO,
+                diag[b],
+                lambda s: weights[s : s + 1, column(0, b)],
+                lambda s: nb[s, b],
+            )
+            x1[b] = value
+            out[lax.div(b, PART // LANES), :, column(0, lax.rem(b, PART // LANES))] = value
+        return 0
+
+    lax.fori_loop(0, 2, step, 0)
+
+
+def outer_kernel(x0, x1_own, left, right, weights, diag, nb_in, out, x1, nbv, nbs, nb, sems):
+    nbv[0] = left[:, WIDE:].astype(jnp.int32)
+    nbv[1] = right[:, WIDE:].astype(jnp.int32)
+    copies = start_all(sems, [(nbv.at[k], nbs.at[k]) for k in range(2)] + [(nb_in, nb)])
+    for j in range(BLOCKS):
+        x1[HALO + j] = x1_own[j]
+    wait_all(copies)
+    for side, ref in ((0, left), (1, right)):
+        for j in range(HALO):
+            e = j + side * (HALO + BLOCKS)
+            cols = slice(NEAR + j * LANES, NEAR + (j + 1) * LANES)
+            x1[e] = apply(
+                lambda c: x0[c],
+                e + HALO,
+                jnp.sum(ref[:, cols], axis=0, keepdims=True),
+                lambda s: ref[s : s + 1, cols],
+                lambda s: nbs[side, s, j],
+            )
+
+    def step(i, _):
         for u in range(UNROLL):
             b = i * UNROLL + u
-            own(b + jnp.where(b < HALO, 0, BLOCKS - 2 * HALO))
-        return 0
-
-    copies[0].wait()
-    lax.fori_loop(0, 2 * HALO // UNROLL, first, 0)
-    wait_all(copies[1:])
-    for side, ref in ((0, left), (1, right)):
-
-        def outer(i, _, side=side, ref=ref):
-            for u in range(UNROLL):
-                far(side, ref, i * UNROLL + u)
-            return 0
-
-        lax.fori_loop(0, HALO // UNROLL, outer, 0)
-
-    def second(i, _):
-        for u in range(UNROLL):
-            b = i * UNROLL + u
-            part = lax.div(b, PART // LANES)
-            cols = column(0, lax.rem(b, PART // LANES))
-            e = b + HALO
-            out[part, 0:SLAB, cols] = x1[e]
-            out[part, SLAB : 2 * SLAB, cols] = apply(
+            rows = pl.ds(pl.multiple_of(lax.rem(b, PART // LANES) * SLAB, SLAB), SLAB)
+            out[lax.div(b, PART // LANES), rows, :] = apply(
                 lambda c: x1[c],
-                e,
+                b + HALO,
                 diag[b],
                 lambda s: weights[s : s + 1, column(0, b)],
                 lambda s: nb[s, b],
             )
         return 0
 
-    lax.fori_loop(0, BLOCKS // UNROLL, second, 0)
-
-
-def gram_kernel(z0, z12, to_modes, own, out, s):
-    eig = own[0:1, :]
+    lax.fori_loop(0, BLOCKS // UNROLL, step, 0)
+
+
+def sums(pairs, first):
+    folded = []
+    for a, b in pairs:
+        p = a * b
+        folded.append(sum(p[:, k * LANES : (k + 1) * LANES] for k in range(PART // LANES)))
+    stack = jnp.concatenate(folded, axis=1)
+    shape = (8, stack.shape[1])
+    which = lax.broadcasted_iota(jnp.int32, shape, 1) // LANES + first
+    pick = (which == lax.broadcasted_iota(jnp.int32, shape, 0)).astype(jnp.float32)
+    return lax.dot_general(
+        pick, stack, (((1,), (1,)), ((), ())), precision=HIGHEST, preferred_element_type=jnp.float32
+    )
+
+
+def gram_kernel(z0, z1, second, to_modes, own, out, modal, image, partial, s):
     for r in range(PARTS):
         rows = slice(r * SLAB, (r + 1) * SLAB)
         s[rows, 0:PART] = z0[r]
-        for q in range(2):
-            s[rows, (q + 1) * PART : (q + 2) * PART] = z12[r, q * SLAB : (q + 1) * SLAB, :]
+        s[rows, PART : 2 * PART] = z1[r]
     m = mm(to_modes[...], s[...])
     row = lax.broadcasted_iota(jnp.int32, (MODES, MODES), 0)
     col = lax.broadcasted_iota(jnp.int32, (MODES, MODES), 1)
-    e = jnp.sum(jnp.where(row == col, eig, 0.0), axis=1, keepdims=True)
-    m0, m1, m2 = (m[:, q * PART : (q + 1) * PART] for q in range(3))
-    image = m1 + e * m0
-    again = (m2 + e * m1) + e * image
-    folded = []
-    for a, b in ((m0, m0), (m0, image), (image, image), (m0, again), (image, again), (again, again)):
-        p = a * b
-        folded.append(sum(p[:, k * LANES : (k + 1) * LANES] for k in range(PART // LANES)))
-    stack = jnp.concatenate(folded, axis=1)
-    which = lax.broadcasted_iota(jnp.int32, (8, 6 * LANES), 1) // LANES
-    pick = (which == lax.broadcasted_iota(jnp.int32, (8, 6 * LANES), 0)).astype(jnp.float32)
-    g = lax.dot_general(
-        pick, stack, (((1,), (1,)), ((), ())), precision=HIGHEST, preferred_element_type=jnp.float32
-    )
+    e = jnp.sum(jnp.where(row == col, own[0:1, :], 0.0), axis=1, keepdims=True)
+    m0, m1 = m[:, 0:PART], m[:, PART : 2 * PART]
+    i0 = m1 + e * m0
+    modal[...] = m0
+    image[...] = i0
+    partial[...] = e * (m1 + i0)
+    g = sums(((m0, m0), (m0, i0), (i0, i0)), 0)
+    for r in range(PARTS):
+        out[r, 0:FLAT, :] = second[r]
+        out[r, FLAT:, :] = g
+
+
+def again_kernel(z2, modal, image, partial, to_modes, out, s):
+    for r in range(PARTS):
+        for j in range(PART // LANES):
+            cols = slice(j * LANES, (j + 1) * LANES)
+            s[r * SLAB : (r + 1) * SLAB, cols] = z2[r, j * SLAB : (j + 1) * SLAB, :]
+    again = mm(to_modes[...], s[...]) + partial[...]
+    m0, i0 = modal[...], image[...]
+    g = jnp.sum(z2[:, FLAT:, :], axis=0) + sums(((m0, again), (i0, again), (again, again)), 3)
     out[...] = jnp.broadcast_to(g[None], out.shape)
 
 
-def relay_kernel(got, out):
-    out[...] = jnp.broadcast_to(jnp.sum(got[...], axis=0)[None], out.shape)
-
-
-def finish_kernel(place, got, z0, z12, to_modes, from_modes, own, out, mine, s):
+def finish_kernel(got, z0, z1, to_modes, from_modes, own, out, side, s):
     g = jnp.sum(got[...], axis=0)
     mm_, mi, ii, mj, ij, jj = (g[k : k + 1, :] for k in range(6))
     e = own[0:1, :]
@@ -239,25 +249,35 @@
     u1 = -c2 * over
     a = -over - u0
     b = -u1
-    squares = mm_ + a * (2.0 * mi + a * ii) + b * (2.0 * (mj + a * ij) + b * jj)
-    norm = jnp.sqrt(jnp.maximum(squares, 0.0) / scale)
+    side[0:1, :] = mm_ + a * (2.0 * mi + a * ii)
+    side[1:2, :] = scale
+    ours = jnp.broadcast_to(b * (2.0 * (mj + a * ij) + b * jj), (8, LANES))
+    for r in range(PARTS):
+        s[r * SLAB : (r + 1) * SLAB, :] = z0[r]
+        s[MODES + r * SLAB : MODES + (r + 1) * SLAB, :] = z1[r]
+    from_m = from_modes[...]
+    to_m = to_modes[...]
+    mix = jnp.concatenate([mm(from_m * (over + u0 + u1 * e), to_m), mm(from_m * u1, to_m)], axis=1)
+    value = mm(mix, s[...])
+    for r in range(PARTS):
+        for j in range(PART // LANES):
+            cols = slice(j * LANES, (j + 1) * LANES)
+            out[r, j * SLAB : (j + 1) * SLAB, :] = value[r * SLAB : (r + 1) * SLAB, cols]
+        out[r, FLAT:, :] = ours
+
+
+def unpack_kernel(got, side, place, out, mine):
+    for r in range(PARTS):
+        for j in range(PART // LANES):
+            start = r * PART + j * LANES
+            out[:, start : start + LANES] = got[r, j * SLAB : (j + 1) * SLAB, :]
+    squares = side[0:1, :] + sum(got[r, FLAT : FLAT + 1, :] for r in range(PARTS))
+    norm = jnp.sqrt(jnp.maximum(squares, 0.0) / side[1:2, :])
     here = place[0:1, 0:SLAB]
     picked = norm[:, 0:SLAB]
     for r in range(1, PARTS):
         picked = jnp.where(here == r, norm[:, r * SLAB : (r + 1) * SLAB], picked)
     mine[...] = picked
-    for r in range(PARTS):
-        s[r * SLAB : (r + 1) * SLAB, :] = z0[r]
-        s[MODES + r * SLAB : MODES + (r + 1) * SLAB, :] = z12[r, 0:SLAB, :]
-    from_m = from_modes[...]
-    to_m = to_modes[...]
-    mix = jnp.concatenate([mm(from_m * (over + u0 + u1 * e), to_m), mm(from_m * u1, to_m)], axis=1)
-    out[...] = mm(mix, s[...]).reshape(out.shape)
-
-
-def unpack_kernel(got, out):
-    for r in range(PARTS):
-        out[:, r * PART : (r + 1) * PART] = got[r]
 
 
 def call(kernel, out_shape, in_specs, scratch=(), out_specs=None):
@@ -307,39 +327,49 @@
         [pltpu.SMEM((STENCIL, BLOCKS), jnp.int32), pltpu.SemaphoreType.DMA((1,))],
     )(source, weights, shift_row, nb, place)
     z0 = lax.all_to_all(dealt, RAD, 0, 0, tiled=True)
-    sent = call(
-        stencil_kernel,
-        f32(PARTS, 2 * SLAB, PART),
+    first, x0, x1 = call(
+        edge_kernel,
+        (f32(PARTS, SLAB, PART), f32(EXT2, SLAB, LANES), f32(BLOCKS, SLAB, LANES)),
+        [VMEM] * 7,
+        [pltpu.SMEM((STENCIL, BLOCKS), jnp.int32), pltpu.SemaphoreType.DMA((1,))],
+    )(source, left, right, weights, diag, inner, nb)
+    z1 = lax.all_to_all(first, RAD, 0, 0, tiled=True)
+    second = call(
+        outer_kernel,
+        f32(PARTS, FLAT, LANES),
         [VMEM] * 7,
         [
-            pltpu.VMEM((EXT2, SLAB, LANES), jnp.float32),
             pltpu.VMEM((EXT1, SLAB, LANES), jnp.float32),
             pltpu.VMEM((2, ROWS, LANES), jnp.int32),
             pltpu.SMEM((2, ROWS, LANES), jnp.int32),
             pltpu.SMEM((STENCIL, BLOCKS), jnp.int32),
             pltpu.SemaphoreType.DMA((3,)),
         ],
-    )(source, left, right, weights, diag, inner, nb)
-    z12 = lax.all_to_all(sent, RAD, 0, 0, tiled=True)
-    peers_1 = sizes["y"] * sizes["x"] * sizes["core"]
-    peers_2 = sizes["z"]
+    )(x0, x1, left, right, weights, diag, nb)
+    sent, modal, image, partial = call(
+        gram_kernel,
+        (f32(PARTS, FLAT + 8, LANES),) + (f32(MODES, PART),) * 3,
+        [VMEM] * 5,
+        [pltpu.VMEM((MODES, 2 * PART), jnp.float32)],
+    )(z0, z1, second, to_modes, own)
+    z2 = lax.all_to_all(sent, RAD, 0, 0, tiled=True)
     g = call(
-        gram_kernel,
-        f32(peers_1, 8, LANES),
-        [VMEM] * 4,
-        [pltpu.VMEM((MODES, 3 * PART), jnp.float32)],
-    )(z0, z12, to_modes, own)
-    g = lax.all_to_all(g, STAGE_1, 0, 0, tiled=True)
-    g = call(relay_kernel, f32(peers_2, 8, LANES), [VMEM])(g)
-    g = lax.all_to_all(g, STAGE_2, 0, 0, tiled=True)
-    mixed, residual_norm = call(
+        again_kernel,
+        f32(lat, 8, LANES),
+        [VMEM] * 5,
+        [pltpu.VMEM((MODES, PART), jnp.float32)],
+    )(z2, modal, image, partial, to_modes)
+    g = lax.all_to_all(g, LAT, 0, 0, tiled=True)
+    mixed, side = call(
         finish_kernel,
-        (f32(PARTS, SLAB, PART), f32(1, SLAB)),
-        [VMEM] * 7,
+        (f32(PARTS, FLAT + 8, LANES), f32(8, LANES)),
+        [VMEM] * 6,
         [pltpu.VMEM((2 * MODES, PART), jnp.float32)],
-    )(place, g, z0, z12, to_modes, from_modes, own)
+    )(g, z0, z1, to_modes, from_modes, own)
     got = lax.all_to_all(mixed, RAD, 0, 0, tiled=True)
-    smoothed = call(unpack_kernel, f32(SLAB, BLOCKS * LANES), [VMEM])(got)
+    smoothed, residual_norm = call(
+        unpack_kernel, (f32(SLAB, BLOCKS * LANES), f32(1, SLAB)), [VMEM] * 3
+    )(got, side, place)
     return smoothed, residual_norm.reshape(SLAB)
 
 

time: 76.4 us -> 77.4 us (1.013)
  blocking collectives: 47.2 us -> 37.5 us
  waiting for transfers between devices: 1 us -> 5.51 us
  starting transfers between devices: 14.3 us -> 18.6 us
  Pallas kernels: 12.8 us -> 14.6 us
    all_to_all x3 -> x2, blocking collectives: 36.6 us -> 26 us  [the longest x1 15.2 us: on_device(): g = lax.all_to_all(g, LAT, 0, 0, tiled=True)]
    all_to_all x0 -> x1, starting transfers between devices: none -> 4.35 us  [on_device(): z1 = lax.all_to_all(first, RAD, 0, 0, tiled=True)]
    all_to_all x1, waiting for transfers between devices: 1 us -> 3.79 us  [on_device(): z0 = lax.all_to_all(dealt, RAD, 0, 0, tiled=True)]
    pallas_call x5 -> x6, Pallas kernels: 8.5 us -> 10.3 us  [the longest x1 4.8 us: on_device(): call(outer_kernel, f32(PARTS, FLAT, LANES), [VMEM] * 7, [pltpu.VMEM((EXT1...]
    all_to_all x0 -> x1, waiting for transfers between devices: none -> 1.71 us  [on_device(): z1 = lax.all_to_all(first, RAD, 0, 0, tiled=True)]
    all_to_all x1, blocking collectives: 10.6 us -> 11.6 us  [on_device(): got = lax.all_to_all(mixed, RAD, 0, 0, tiled=True)]
  transfers between devices with their start and end apart: 3 -> 4, of which waited for: 1 -> 2; matrix products, arithmetic and copies ran while one was open for 0% -> 0% of each run, Pallas kernels for 11% -> 14%
where the time goes in v5:
time: 77.4 us; the launch traced here: 77 us
  blocking collectives  37.5 us (48%)
  starting transfers between devices  18.6 us (24%)
  Pallas kernels  14.6 us (19%)
  waiting for transfers between devices  5.51 us (7%)
    all_to_all x1, blocking collectives, on_device(): g = lax.all_to_all(g, LAT, 0, 0, tiled=True)  15.2 us
    all_to_all x1, blocking collectives, on_device(): got = lax.all_to_all(mixed, RAD, 0, 0, tiled=True)  11.6 us
    all_to_all x1, blocking collectives, on_device(): z2 = lax.all_to_all(sent, RAD, 0, 0, tiled=True)  10.7 us
    ppermute x1, starting transfers between devices, on_device(): right = lax.ppermute(down, LAT, [((i + 1) % lat, i) for i in range(lat)])  6.48 us
    all_to_all x1, starting transfers between devices, on_device(): z0 = lax.all_to_all(dealt, RAD, 0, 0, tiled=True)  5.26 us
    pallas_call x1, Pallas kernels, on_device(): call(outer_kernel, f32(PARTS, FLAT, LANES), [VMEM] * 7, [pltpu.VMEM((EXT1...  4.8 us
    all_to_all x1, starting transfers between devices, on_device(): z1 = lax.all_to_all(first, RAD, 0, 0, tiled=True)  4.35 us
    all_to_all x1, waiting for transfers between devices, on_device(): z0 = lax.all_to_all(dealt, RAD, 0, 0, tiled=True)  3.79 us
  transfers between devices with their start and end apart: 4, of which 2 were waited for; matrix products, arithmetic and copies ran while one was open for 0% of the time, Pallas kernels for 14%

profile of v5, /device:TPU:1, one launch (start us, length us, event | category | flops | bytes accessed | tf_op | source)
XLA Modules:
  0.0 77.0 jit_solution(1332575072077803581)
XLA Ops:
  0.6 0.0 copy-start
  0.6 0.0 copy-start.1
  0.7 1.4 %shard_map.86 = (f32[32,2176]{1,0:T(8,128)S(1)}, f32[32,2176]{1,0:T(8,128)S(1)}, f32[8,128]{1,0:T(8,128)S(1)}, s32[31,32]{1,0:T(8,128)S(1)}, f32[1,4096]{1,0:T(1,128)S(1)}) custom-call(f32[16,4096]{1,0:T(8,128)} %src.5, f32[31,4096]{1,0:T(8,128)} %weights.7, f32[1,4096]{1,0:T(1,128)} %bitcast.3, s32[31,32]{1,0:T(8,128)} %neighbors.1, f32[1,128]{1,0:T(1,128)} %bitcast.4), custom_call_target="tpu_custom_call" | custom-call | tf_op jit(solution)/shard_map/pallas_call | solution.py:305
  2.0 2.5 %collective-permute-start = (f32[32,2176]{1,0:T(8,128)S(1)}, f32[32,2176]{1,0:T(8,128)S(1)}, u32[]{:S(2)}, u32[]{:S(2)}) collective-permute-start(f32[32,2176]{1,0:T(8,128)S(1)} %get-tuple-element.25), channel_id=1, source_target_pairs={{0,8},{8,16},{16,24},{24,32},{32,40},{40,48},{48,56},{56,64},{64,7... | collective-permute-start | bytes 835592 | tf_op jit(solution)/shard_map/ppermute | solution.py:316
  4.6 6.5 %collective-permute-start.1 = (f32[32,2176]{1,0:T(8,128)S(1)}, f32[32,2176]{1,0:T(8,128)S(1)}, u32[]{:S(2)}, u32[]{:S(2)}) collective-permute-start(f32[32,2176]{1,0:T(8,128)S(1)} %get-tuple-element.26), channel_id=1, source_target_pairs={{8,0},{16,8},{24,16},{32,24},{40,32},{48,40},{56,48},{64,56},{72,6... | collective-permute-start | bytes 835592 | tf_op jit(solution)/shard_map/ppermute | solution.py:317
  11.0 0.0 copy-done
  11.0 0.0 copy-done.1
  11.0 2.9 %shard_map.87 = (f32[16,16,128]{2,1,0:T(8,128)S(1)}, f32[32,1,128]{2,1,0:T(1,128)S(1)}, f32[8,128]{1,0:T(8,128)S(1)}, f32[8,16,512]{2,1,0:T(8,128)}) custom-call(f32[16,4096]{1,0:T(8,128)S(1)} %copy-done.1, f32[31,4096]{1,0:T(8,128)S(1)} %copy-done, f32[1,4096]{1,0:T(1,128)S(1)} %get-tuple-element.22.shifts, s32[31,32]{1,0:T(8,128)S(1)} %get-tuple-element.23.nb_in, ...), custom_call_target="tpu_custom_call" | custom-call | tf_op jit(solution)/shard_map/pallas_call | solution.py:318
  14.0 5.3 %all-to-all-start = ((f32[8,16,512]{2,1,0:T(8,128)}), f32[8,16,512]{2,1,0:T(8,128)S(1)}, u32[]{:S(2)}, u32[]{:S(2)}) async-start(f32[8,16,512]{2,1,0:T(8,128)} %get-tuple-element.24), calls=%async_computation | async-start | bytes 524288 | tf_op jit(solution)/shard_map/all_to_all | solution.py:329
  19.2 0.0 collective-permute-done.left
  19.2 0.0 collective-permute-done.1.right
  19.2 2.7 %shard_map.88 = (f32[8,16,512]{2,1,0:T(8,128)}, f32[64,16,128]{2,1,0:T(8,128)S(1)}, f32[32,16,128]{2,1,0:T(8,128)S(1)}) custom-call(f32[16,4096]{1,0:T(8,128)S(1)} %copy-done.1, f32[32,2176]{1,0:T(8,128)S(1)} %collective-permute-done.left, f32[32,2176]{1,0:T(8,128)S(1)} %collective-permute-done.1.right, f32[31,4096]{1,0:T(8,128)S(1)} %copy-done, ...), custom_call_target="tpu_custom_call" | custom-call | tf_op jit(solution)/shard_map/pallas_call | solution.py:330
  21.9 3.8 %all-to-all-done.z0 = f32[8,16,512]{2,1,0:T(8,128)S(1)} async-done(((f32[8,16,512]{2,1,0:T(8,128)}), f32[8,16,512]{2,1,0:T(8,128)S(1)}, u32[]{:S(2)}, u32[]{:S(2)}) %all-to-all-start) | async-done | bytes 262176 | tf_op jit(solution)/shard_map/all_to_all | solution.py:329
  25.7 4.4 %all-to-all-start.1 = ((f32[8,16,512]{2,1,0:T(8,128)}), f32[8,16,512]{2,1,0:T(8,128)S(1)}, u32[]{:S(2)}, u32[]{:S(2)}) async-start(f32[8,16,512]{2,1,0:T(8,128)} %get-tuple-element.29), calls=%async_computation.1 | async-start | bytes 524288 | tf_op jit(solution)/shard_map/all_to_all | solution.py:336
  30.1 0.0 copy-start.2
  30.1 4.8 %shard_map.89.second = f32[8,64,128]{2,1,0:T(8,128)S(1)} custom-call(f32[64,16,128]{2,1,0:T(8,128)S(1)} %get-tuple-element.30.x0, f32[32,16,128]{2,1,0:T(8,128)S(1)} %get-tuple-element.31.x1_own, f32[32,2176]{1,0:T(8,128)S(1)} %collective-permute-done.left, f32[32,2176]{1,0:T(8,128)S(1)} %collective-permute-done.1.right, f32[31,4096]{1,0:T(8,128)S(1)} %copy-done, ...), custom_call_target="tpu_custom_call" | custom-call | tf_op jit(solution)/shard_map/pallas_call | solution.py:337
  34.9 1.7 %all-to-all-done.1.z1 = f32[8,16,512]{2,1,0:T(8,128)S(1)} async-done(((f32[8,16,512]{2,1,0:T(8,128)}), f32[8,16,512]{2,1,0:T(8,128)S(1)}, u32[]{:S(2)}, u32[]{:S(2)}) %all-to-all-start.1) | async-done | bytes 262176 | tf_op jit(solution)/shard_map/all_to_all | solution.py:336
  36.6 0.0 copy-done.2
  36.6 1.0 %shard_map.90 = (f32[8,72,128]{2,1,0:T(8,128)S(1)}, f32[128,512]{1,0:T(8,128)S(1)}, f32[128,512]{1,0:T(8,128)S(1)}, f32[128,512]{1,0:T(8,128)S(1)}) custom-call(f32[8,16,512]{2,1,0:T(8,128)S(1)} %all-to-all-done.z0, f32[8,16,512]{2,1,0:T(8,128)S(1)} %all-to-all-done.1.z1, f32[8,64,128]{2,1,0:T(8,128)S(1)} %shard_map.89.second, f32[128,128]{1,0:T(8,128)S(1)} %copy-done.2, ...), custom_call_target="tpu_custom_call" | custom-call | tf_op jit(solution)/shard_map/pallas_call | solution.py:349
  37.6 10.7 %all_to_all.25.z2 = f32[8,72,128]{2,1,0:T(8,128)S(1)} all-to-all(f32[8,72,128]{2,1,0:T(8,128)S(1)} %get-tuple-element.33), channel_id=1, replica_groups=mesh['y'=4,'z'=8,'x'=4,'core'=2] {'x','core'}, dimensions={0} | all-to-all | bytes 589824 | tf_op jit(solution)/shard_map/all_to_all | solution.py:355
  48.3 0.6 shard_map.91
  48.9 0.0 copy-start.3
  49.0 15.2 %all_to_all.26.got = f32[32,8,128]{2,1,0:T(8,128)S(1)} all-to-all(f32[32,8,128]{2,1,0:T(8,128)S(1)} %shard_map.91), channel_id=1, replica_groups=mesh['y'=4,'z'=8,'x'=4,'core'=2] {'y','z'}, dimensions={0} | all-to-all | bytes 262144 | tf_op jit(solution)/shard_map/all_to_all | solution.py:362
  64.2 0.0 copy-done.3
  64.2 0.5 shard_map.92
  64.7 11.6 %all_to_all.27.got = f32[8,72,128]{2,1,0:T(8,128)S(1)} all-to-all(f32[8,72,128]{2,1,0:T(8,128)S(1)} %get-tuple-element.37), channel_id=1, replica_groups=mesh['y'=4,'z'=8,'x'=4,'core'=2] {'x','core'}, dimensions={0} | all-to-all | bytes 589824 | tf_op jit(solution)/shard_map/all_to_all | solution.py:369
  76.3 0.7 shard_map.93
  (1 shorter events, 0.0 us)
Async XLA Ops:
  0.6 10.4 %copy-start = (f32[31,4096]{1,0:T(8,128)S(1)}, f32[31,4096]{1,0:T(8,128)}, u32[]{:S(2)}) copy-start(f32[31,4096]{1,0:T(8,128)} %weights.7) | copy-start | bytes 1523716
  0.6 10.4 %copy-start.1 = (f32[16,4096]{1,0:T(8,128)S(1)}, f32[16,4096]{1,0:T(8,128)}, u32[]{:S(2)}) copy-start(f32[16,4096]{1,0:T(8,128)} %src.5) | copy-start | bytes 786436
  2.0 17.2 %collective-permute-start = (f32[32,2176]{1,0:T(8,128)S(1)}, f32[32,2176]{1,0:T(8,128)S(1)}, u32[]{:S(2)}, u32[]{:S(2)}) collective-permute-start(f32[32,2176]{1,0:T(8,128)S(1)} %get-tuple-element.25), channel_id=1, source_target_pairs={{0,8},{8,16},{16,24},{24,32},{32,40},{40,48},{48,56},{56,64},{64,7... | collective-permute-start | bytes 835592 | tf_op jit(solution)/shard_map/ppermute | solution.py:316
  4.6 14.7 %collective-permute-start.1 = (f32[32,2176]{1,0:T(8,128)S(1)}, f32[32,2176]{1,0:T(8,128)S(1)}, u32[]{:S(2)}, u32[]{:S(2)}) collective-permute-start(f32[32,2176]{1,0:T(8,128)S(1)} %get-tuple-element.26), channel_id=1, source_target_pairs={{8,0},{16,8},{24,16},{32,24},{40,32},{48,40},{56,48},{64,56},{72,6... | collective-permute-start | bytes 835592 | tf_op jit(solution)/shard_map/ppermute | solution.py:317
  14.0 11.8 %all-to-all-start = ((f32[8,16,512]{2,1,0:T(8,128)}), f32[8,16,512]{2,1,0:T(8,128)S(1)}, u32[]{:S(2)}, u32[]{:S(2)}) async-start(f32[8,16,512]{2,1,0:T(8,128)} %get-tuple-element.24), calls=%async_computation | async-start | bytes 524288 | tf_op jit(solution)/shard_map/all_to_all | solution.py:329
  25.7 10.9 %all-to-all-start.1 = ((f32[8,16,512]{2,1,0:T(8,128)}), f32[8,16,512]{2,1,0:T(8,128)S(1)}, u32[]{:S(2)}, u32[]{:S(2)}) async-start(f32[8,16,512]{2,1,0:T(8,128)} %get-tuple-element.29), calls=%async_computation.1 | async-start | bytes 524288 | tf_op jit(solution)/shard_map/all_to_all | solution.py:336
  30.1 6.5 %copy-start.2 = (f32[128,128]{1,0:T(8,128)S(1)}, f32[128,128]{1,0:T(8,128)}, u32[]{:S(2)}) copy-start(f32[128,128]{1,0:T(8,128)} %to_modes.5) | copy-start | bytes 196612
  48.9 15.2 %copy-start.3 = (f32[128,128]{1,0:T(8,128)S(1)}, f32[128,128]{1,0:T(8,128)}, u32[]{:S(2)}) copy-start(f32[128,128]{1,0:T(8,128)} %from_modes.1) | copy-start | bytes 196612

commit v6 on v5

--- a/solution.py
+++ b/solution.py
@@ -23,11 +23,24 @@
 FLAT = SLAB * PART // LANES
 WIDE = 2 * HALO * LANES
 NEAR = HALO * LANES
+HALF = NEAR // 2
+TAIL = HALF + NEAR
 LAT = ("y", "z")
 RAD = ("x", "core")
+
+
+def work(microseconds):
+    return pl.CostEstimate(
+        flops=int(microseconds * 1e9), transcendentals=0, bytes_accessed=0
+    )
+
+
 VMEM = pl.BlockSpec(memory_space=pltpu.VMEM)
 SMEM = pl.BlockSpec(memory_space=pltpu.SMEM)
 HBM = pl.BlockSpec(memory_space=pltpu.HBM)
+COST_0 = work(3)
+COST_1 = work(3)
+COST_2 = work(10)
 HIGHEST = lax.Precision.HIGHEST
 
 
@@ -58,24 +71,25 @@
         copy.wait()
 
 
-def pack_kernel(src, weights, shifts, neighbors, eig, up, down, own, nb_in, sh_in, w_in, eig_in, sems):
+def pack_kernel(src, weights, shifts, neighbors, eig, up, down, up_far, down_far, own, nb_in, sh_in, w_in, eig_in, sems):
     last = BLOCKS * LANES
-    ends = ((up, last - WIDE, last - NEAR), (down, 0, 0))
+    ends = ((up, up_far, last - NEAR, last - WIDE), (down, down_far, 0, NEAR))
     pairs = [(neighbors, nb_in), (eig, eig_in), (shifts, sh_in)]
-    for k, (out, start, near) in enumerate(ends):
+    for k, (near_out, far_out, near, far) in enumerate(ends):
         pairs += [
+            (src.at[:, pl.ds(near, NEAR)], near_out),
             (weights.at[:, pl.ds(near, NEAR)], w_in.at[k]),
-            (src.at[:, pl.ds(start, NEAR)], out.at[0:SLAB, 0:NEAR]),
-            (src.at[:, pl.ds(start + NEAR, NEAR)], out.at[SLAB : 2 * SLAB, 0:NEAR]),
+            (src.at[:, pl.ds(far, HALF)], far_out.at[0:SLAB, 0:HALF]),
+            (src.at[:, pl.ds(far + HALF, HALF)], far_out.at[SLAB : 2 * SLAB, 0:HALF]),
         ]
     wait_all(start_all(sems, pairs))
     nb = nb_in[...].astype(jnp.float32)
-    for k, (out, first) in enumerate(((up, BLOCKS - HALO), (down, 0))):
-        near = first * LANES
-        out[0:STENCIL, NEAR:WIDE] = w_in[k]
-        out[STENCIL:ROWS, NEAR:WIDE] = sh_in[:, near : near + NEAR]
-        out[:, WIDE:] = jnp.zeros((ROWS, LANES), jnp.float32)
-        out[0:STENCIL, WIDE : WIDE + HALO] = nb[:, first : first + HALO]
+    for k, (_, out, near, _) in enumerate(ends):
+        block = near // LANES
+        out[0:STENCIL, HALF:TAIL] = w_in[k]
+        out[STENCIL:ROWS, HALF:TAIL] = sh_in[:, near : near + NEAR]
+        out[:, TAIL:] = jnp.zeros((ROWS, LANES), jnp.float32)
+        out[0:STENCIL, TAIL : TAIL + HALO] = nb[:, block : block + HALO]
     own[...] = jnp.broadcast_to(eig_in[...], own.shape)
 
 
@@ -93,11 +107,9 @@
     return acc
 
 
-def inner_kernel(src, weights, shifts, nb_in, place_in, x1, diag, place, dealt, nb, sems):
+def inner_kernel(src, weights, shifts, nb_in, place_in, x1, diag, place, nb, sems):
     copies = start_all(sems, [(nb_in, nb)])
     place[...] = place_in[...]
-    for r in range(PARTS):
-        dealt[r] = src[:, r * PART : (r + 1) * PART]
     for j in range(BLOCKS):
         cols = slice(j * LANES, (j + 1) * LANES)
         diag[j] = jnp.sum(weights[:, cols], axis=0, keepdims=True) + shifts[:, cols]
@@ -120,18 +132,18 @@
 
 def edge_kernel(src, left, right, weights, diag, inner, nb_in, out, x0, x1, nb, sems):
     copies = start_all(sems, [(nb_in, nb)])
-    for half in range(2):
-        rows = slice(half * SLAB, half * SLAB + SLAB)
-        for j in range(HALO):
-            cols = slice(j * LANES, (j + 1) * LANES)
-            x0[half * HALO + j] = left[rows, cols]
-            x0[2 * HALO + BLOCKS + half * HALO + j] = right[rows, cols]
+    for j in range(HALO):
+        cols = slice(j * LANES, (j + 1) * LANES)
+        x0[j] = left[:, cols]
+        x0[HALO + BLOCKS + j] = right[:, cols]
     for j in range(BLOCKS):
-        x0[2 * HALO + j] = src[:, j * LANES : (j + 1) * LANES]
+        x0[HALO + j] = src[:, j * LANES : (j + 1) * LANES]
+    for r in range(PARTS):
+        out[r, 0:SLAB, :] = src[:, r * PART : (r + 1) * PART]
     for j in range(HALO, BLOCKS - HALO):
         x1[j] = inner[j - HALO]
         part, place = divmod(j, PART // LANES)
-        out[part, :, place * LANES : (place + 1) * LANES] = inner[j - HALO]
+        out[part, SLAB:, place * LANES : (place + 1) * LANES] = inner[j - HALO]
     wait_all(copies)
 
     def step(i, _):
@@ -139,29 +151,37 @@
             b = i * (BLOCKS - HALO) + u
             value = apply(
                 lambda c: x0[c],
-                b + 2 * HALO,
+                b + HALO,
                 diag[b],
                 lambda s: weights[s : s + 1, column(0, b)],
                 lambda s: nb[s, b],
             )
             x1[b] = value
-            out[lax.div(b, PART // LANES), :, column(0, lax.rem(b, PART // LANES))] = value
+            out[lax.div(b, PART // LANES), SLAB:, column(0, lax.rem(b, PART // LANES))] = value
         return 0
 
     lax.fori_loop(0, 2, step, 0)
 
 
-def outer_kernel(x0, x1_own, left, right, weights, diag, nb_in, out, x1, nbv, nbs, nb, sems):
-    nbv[0] = left[:, WIDE:].astype(jnp.int32)
-    nbv[1] = right[:, WIDE:].astype(jnp.int32)
+def outer_kernel(x0_near, x1_own, left, right, weights, diag, nb_in, out, x0, x1, nbv, nbs, nb, sems):
+    nbv[0] = left[:, TAIL:].astype(jnp.int32)
+    nbv[1] = right[:, TAIL:].astype(jnp.int32)
     copies = start_all(sems, [(nbv.at[k], nbs.at[k]) for k in range(2)] + [(nb_in, nb)])
+    for half in range(2):
+        rows = slice(half * SLAB, half * SLAB + SLAB)
+        for j in range(HALO // 2):
+            cols = slice(j * LANES, (j + 1) * LANES)
+            x0[half * HALO // 2 + j] = left[rows, cols]
+            x0[3 * HALO + BLOCKS + half * HALO // 2 + j] = right[rows, cols]
+    for j in range(EXT1):
+        x0[HALO + j] = x0_near[j]
     for j in range(BLOCKS):
         x1[HALO + j] = x1_own[j]
     wait_all(copies)
     for side, ref in ((0, left), (1, right)):
         for j in range(HALO):
             e = j + side * (HALO + BLOCKS)
-            cols = slice(NEAR + j * LANES, NEAR + (j + 1) * LANES)
+            cols = slice(HALF + j * LANES, HALF + (j + 1) * LANES)
             x1[e] = apply(
                 lambda c: x0[c],
                 e + HALO,
@@ -200,11 +220,11 @@
     )
 
 
-def gram_kernel(z0, z1, second, to_modes, own, out, modal, image, partial, s):
+def gram_kernel(z01, second, to_modes, own, out, modal, image, partial, s):
     for r in range(PARTS):
         rows = slice(r * SLAB, (r + 1) * SLAB)
-        s[rows, 0:PART] = z0[r]
-        s[rows, PART : 2 * PART] = z1[r]
+        s[rows, 0:PART] = z01[r, 0:SLAB, :]
+        s[rows, PART : 2 * PART] = z01[r, SLAB:, :]
     m = mm(to_modes[...], s[...])
     row = lax.broadcasted_iota(jnp.int32, (MODES, MODES), 0)
     col = lax.broadcasted_iota(jnp.int32, (MODES, MODES), 1)
@@ -231,7 +251,7 @@
     out[...] = jnp.broadcast_to(g[None], out.shape)
 
 
-def finish_kernel(got, z0, z1, to_modes, from_modes, own, out, side, s):
+def finish_kernel(got, z01, to_modes, from_modes, own, out, side, s):
     g = jnp.sum(got[...], axis=0)
     mm_, mi, ii, mj, ij, jj = (g[k : k + 1, :] for k in range(6))
     e = own[0:1, :]
@@ -253,8 +273,8 @@
     side[1:2, :] = scale
     ours = jnp.broadcast_to(b * (2.0 * (mj + a * ij) + b * jj), (8, LANES))
     for r in range(PARTS):
-        s[r * SLAB : (r + 1) * SLAB, :] = z0[r]
-        s[MODES + r * SLAB : MODES + (r + 1) * SLAB, :] = z1[r]
+        s[r * SLAB : (r + 1) * SLAB, :] = z01[r, 0:SLAB, :]
+        s[MODES + r * SLAB : MODES + (r + 1) * SLAB, :] = z01[r, SLAB:, :]
     from_m = from_modes[...]
     to_m = to_modes[...]
     mix = jnp.concatenate([mm(from_m * (over + u0 + u1 * e), to_m), mm(from_m * u1, to_m)], axis=1)
@@ -280,7 +300,7 @@
     mine[...] = picked
 
 
-def call(kernel, out_shape, in_specs, scratch=(), out_specs=None):
+def call(kernel, out_shape, in_specs, scratch=(), out_specs=None, cost=None):
     if out_specs is None:
         out_specs = (VMEM,) * len(out_shape) if isinstance(out_shape, tuple) else VMEM
     return pl.pallas_call(
@@ -289,6 +309,7 @@
         in_specs=in_specs,
         out_specs=out_specs,
         scratch_shapes=scratch,
+        cost_estimate=cost,
         compiler_params=pltpu.CompilerParams(vmem_limit_bytes=32 * 1024 * 1024),
     )
 
@@ -302,56 +323,58 @@
     place = jnp.full((8, LANES), lax.axis_index(RAD).astype(jnp.float32))
     shift_row = shifts.reshape(1, -1)
     eig = eigenvalue.reshape(1, -1)
-    up, down, own, nb, shift_row = call(
+    nears, fars = f32(SLAB, NEAR), f32(ROWS, TAIL + LANES)
+    offsets = jax.ShapeDtypeStruct(neighbors.shape, neighbors.dtype)
+    up, down, up_far, down_far, own, nb, shift_row = call(
         pack_kernel,
-        (f32(ROWS, WIDE + LANES), f32(ROWS, WIDE + LANES), f32(8, LANES),
-         jax.ShapeDtypeStruct(neighbors.shape, neighbors.dtype), f32(1, BLOCKS * LANES)),
+        (nears, nears, fars, fars, f32(8, LANES), offsets, f32(1, BLOCKS * LANES)),
         [HBM] * 5,
         [
             pltpu.VMEM((2, STENCIL, NEAR), jnp.float32),
             pltpu.VMEM((1, LANES), jnp.float32),
-            pltpu.SemaphoreType.DMA((9,)),
+            pltpu.SemaphoreType.DMA((11,)),
         ],
     )(*(pinned(v) for v in (source, weights, shift_row, neighbors, eig)))
-    left = lax.ppermute(up, LAT, [(i, (i + 1) % lat) for i in range(lat)])
-    right = lax.ppermute(down, LAT, [((i + 1) % lat, i) for i in range(lat)])
-    inner, diag, place, dealt = call(
+    onward = [(i, (i + 1) % lat) for i in range(lat)]
+    back = [(j, i) for i, j in onward]
+    left, right = lax.ppermute(up, LAT, onward), lax.ppermute(down, LAT, back)
+    left_far, right_far = lax.ppermute(up_far, LAT, onward), lax.ppermute(down_far, LAT, back)
+    smem_offsets = pltpu.SMEM((STENCIL, BLOCKS), jnp.int32)
+    inner, diag, place = call(
         inner_kernel,
-        (
-            f32(BLOCKS - 2 * HALO, SLAB, LANES),
-            f32(BLOCKS, 1, LANES),
-            f32(8, LANES),
-            f32(PARTS, SLAB, PART),
-        ),
+        (f32(BLOCKS - 2 * HALO, SLAB, LANES), f32(BLOCKS, 1, LANES), f32(8, LANES)),
         [VMEM] * 5,
-        [pltpu.SMEM((STENCIL, BLOCKS), jnp.int32), pltpu.SemaphoreType.DMA((1,))],
+        [smem_offsets, pltpu.SemaphoreType.DMA((1,))],
+        cost=COST_0,
     )(source, weights, shift_row, nb, place)
-    z0 = lax.all_to_all(dealt, RAD, 0, 0, tiled=True)
     first, x0, x1 = call(
         edge_kernel,
-        (f32(PARTS, SLAB, PART), f32(EXT2, SLAB, LANES), f32(BLOCKS, SLAB, LANES)),
+        (f32(PARTS, 2 * SLAB, PART), f32(EXT1, SLAB, LANES), f32(BLOCKS, SLAB, LANES)),
         [VMEM] * 7,
-        [pltpu.SMEM((STENCIL, BLOCKS), jnp.int32), pltpu.SemaphoreType.DMA((1,))],
+        [smem_offsets, pltpu.SemaphoreType.DMA((1,))],
+        cost=COST_1,
     )(source, left, right, weights, diag, inner, nb)
-    z1 = lax.all_to_all(first, RAD, 0, 0, tiled=True)
+    z01 = lax.all_to_all(first, RAD, 0, 0, tiled=True)
     second = call(
         outer_kernel,
         f32(PARTS, FLAT, LANES),
         [VMEM] * 7,
         [
+            pltpu.VMEM((EXT2, SLAB, LANES), jnp.float32),
             pltpu.VMEM((EXT1, SLAB, LANES), jnp.float32),
             pltpu.VMEM((2, ROWS, LANES), jnp.int32),
             pltpu.SMEM((2, ROWS, LANES), jnp.int32),
-            pltpu.SMEM((STENCIL, BLOCKS), jnp.int32),
+            smem_offsets,
             pltpu.SemaphoreType.DMA((3,)),
         ],
-    )(x0, x1, left, right, weights, diag, nb)
+        cost=COST_2,
+    )(x0, x1, left_far, right_far, weights, diag, nb)
     sent, modal, image, partial = call(
         gram_kernel,
         (f32(PARTS, FLAT + 8, LANES),) + (f32(MODES, PART),) * 3,
-        [VMEM] * 5,
+        [VMEM] * 4,
         [pltpu.VMEM((MODES, 2 * PART), jnp.float32)],
-    )(z0, z1, second, to_modes, own)
+    )(z01, second, to_modes, own)
     z2 = lax.all_to_all(sent, RAD, 0, 0, tiled=True)
     g = call(
         again_kernel,
@@ -363,9 +386,9 @@
     mixed, side = call(
         finish_kernel,
         (f32(PARTS, FLAT + 8, LANES), f32(8, LANES)),
-        [VMEM] * 6,
+        [VMEM] * 5,
         [pltpu.VMEM((2 * MODES, PART), jnp.float32)],
-    )(g, z0, z1, to_modes, from_modes, own)
+    )(g, z01, to_modes, from_modes, own)
     got = lax.all_to_all(mixed, RAD, 0, 0, tiled=True)
     smoothed, residual_norm = call(
         unpack_kernel, (f32(SLAB, BLOCKS * LANES), f32(1, SLAB)), [VMEM] * 3

time: 77.4 us -> 74.7 us (0.965)
  blocking collectives: 37.5 us -> 35.3 us
  starting transfers between devices: 18.6 us -> 19.6 us
  waiting for transfers between devices: 5.51 us -> 4.65 us
    ppermute x2 -> x4, starting transfers between devices: 9.02 us -> 13.8 us  [the longest x2 9.02 us: on_device(): left, right = (lax.ppermute(up, LAT, onward), lax.ppermute(down, LAT, back))]
    all_to_all x2 -> x1, starting transfers between devices: 9.62 us -> 5.82 us  [on_device(): z01 = lax.all_to_all(first, RAD, 0, 0, tiled=True)]
    all_to_all x1, blocking collectives: 15.2 us -> 13.1 us  [on_device(): g = lax.all_to_all(g, LAT, 0, 0, tiled=True)]
    all_to_all x2 -> x1, waiting for transfers between devices: 5.5 us -> 4.64 us  [on_device(): z01 = lax.all_to_all(first, RAD, 0, 0, tiled=True)]
  transfers between devices with their start and end apart: 4 -> 5, of which waited for: 2 -> 1; matrix products, arithmetic and copies ran while one was open for 0% -> 0% of each run, Pallas kernels for 14% -> 13%
where the time goes in v6:
time: 74.7 us; the launch traced here: 74.3 us
  blocking collectives  35.3 us (47%)
  starting transfers between devices  19.6 us (26%)
  Pallas kernels  14 us (19%)
  waiting for transfers between devices  4.65 us (6%)
    all_to_all x1, blocking collectives, on_device(): g = lax.all_to_all(g, LAT, 0, 0, tiled=True)  13.1 us
    all_to_all x1, blocking collectives, on_device(): got = lax.all_to_all(mixed, RAD, 0, 0, tiled=True)  11.6 us
    all_to_all x1, blocking collectives, on_device(): z2 = lax.all_to_all(sent, RAD, 0, 0, tiled=True)  10.6 us
    ppermute x2, starting transfers between devices, on_device(): left, right = (lax.ppermute(up, LAT, onward), lax.ppermute(down, LAT, back))  9.02 us
    all_to_all x1, starting transfers between devices, on_device(): z01 = lax.all_to_all(first, RAD, 0, 0, tiled=True)  5.82 us
    pallas_call x1, Pallas kernels, on_device(): call(outer_kernel, f32(PARTS, FLAT, LANES), [VMEM] * 7, [pltpu.VMEM((EXT2...  4.81 us
    ppermute x1, starting transfers between devices, on_device(): lax.ppermute(down_far, LAT, back)  4.78 us
    all_to_all x1, waiting for transfers between devices, on_device(): z01 = lax.all_to_all(first, RAD, 0, 0, tiled=True)  4.64 us
  transfers between devices with their start and end apart: 5, of which 1 were waited for; matrix products, arithmetic and copies ran while one was open for 0% of the time, Pallas kernels for 13%

profile of v6, /device:TPU:1, one launch (start us, length us, event | category | flops | bytes accessed | tf_op | source)
XLA Modules:
  0.0 74.3 jit_solution(9848489214576455289)
XLA Ops:
  0.6 0.0 copy-start.1
  0.6 0.0 copy-start.2
  0.7 1.4 %shard_map.86 = (f32[16,1024]{1,0:T(8,128)S(1)}, f32[16,1024]{1,0:T(8,128)S(1)}, f32[32,1664]{1,0:T(8,128)S(1)}, f32[32,1664]{1,0:T(8,128)S(1)}, f32[8,128]{1,0:...) custom-call(f32[16,4096]{1,0:T(8,128)} %src.5, f32[31,4096]{1,0:T(8,128)} %weights.7, f32[1,4096]{1,0:T(1,128)} %bitcast.3, ...), custom_call_target="tpu_custom_call" | custom-call | tf_op jit(solution)/shard_map/pallas_call | solution.py:328
  2.0 2.5 %collective-permute-start = (f32[16,1024]{1,0:T(8,128)S(1)}, f32[16,1024]{1,0:T(8,128)S(1)}, u32[]{:S(2)}, u32[]{:S(2)}) collective-permute-start(f32[16,1024]{1,0:T(8,128)S(1)} %get-tuple-element.23), channel_id=1, source_target_pairs={{0,8},{8,16},{16,24},{24,32},{32,40},{40,48},{48,56},{56,64},{64,7... | collective-permute-start | bytes 196616 | tf_op jit(solution)/shard_map/ppermute | solution.py:340
  4.6 6.5 %collective-permute-start.1 = (f32[16,1024]{1,0:T(8,128)S(1)}, f32[16,1024]{1,0:T(8,128)S(1)}, u32[]{:S(2)}, u32[]{:S(2)}) collective-permute-start(f32[16,1024]{1,0:T(8,128)S(1)} %get-tuple-element.24), channel_id=1, source_target_pairs={{8,0},{16,8},{24,16},{32,24},{40,32},{48,40},{56,48},{64,56},{72,6... | collective-permute-start | bytes 196616 | tf_op jit(solution)/shard_map/ppermute | solution.py:340
  11.1 0.0 collective-permute-start.2
  11.1 4.8 %collective-permute-start.3 = (f32[32,1664]{1,0:T(8,128)S(1)}, f32[32,1664]{1,0:T(8,128)S(1)}, u32[]{:S(2)}, u32[]{:S(2)}) collective-permute-start(f32[32,1664]{1,0:T(8,128)S(1)} %get-tuple-element.33), channel_id=1, source_target_pairs={{8,0},{16,8},{24,16},{32,24},{40,32},{48,40},{56,48},{64,56},{72,6... | collective-permute-start | bytes 638984 | tf_op jit(solution)/shard_map/ppermute | solution.py:341
  15.8 0.0 copy-done.1
  15.8 0.0 copy-done.2
  15.9 2.2 %shard_map.87 = (f32[16,16,128]{2,1,0:T(8,128)S(1)}, f32[32,1,128]{2,1,0:T(1,128)S(1)}, f32[8,128]{1,0:T(8,128)S(1)}) custom-call(f32[16,4096]{1,0:T(8,128)S(1)} %copy-done.2, f32[31,4096]{1,0:T(8,128)S(1)} %copy-done.1, f32[1,4096]{1,0:T(1,128)S(1)} %get-tuple-element.25.shifts, s32[31,32]{1,0:T(8,128)S(1)} %get-tuple-element.26.nb_in, ...), custom_call_target="tpu_custom_call" | custom-call | flops 3000000000 | tf_op jit(solution)/shard_map/pallas_call | solution.py:343
  18.1 0.0 collective-permute-done.left
  18.1 0.0 collective-permute-done.1.right
  18.1 2.8 %shard_map.88 = (f32[8,32,512]{2,1,0:T(8,128)}, f32[48,16,128]{2,1,0:T(8,128)S(1)}, f32[32,16,128]{2,1,0:T(8,128)S(1)}) custom-call(f32[16,4096]{1,0:T(8,128)S(1)} %copy-done.2, f32[16,1024]{1,0:T(8,128)S(1)} %collective-permute-done.left, f32[16,1024]{1,0:T(8,128)S(1)} %collective-permute-done.1.right, f32[31,4096]{1,0:T(8,128)S(1)} %copy-done.1, ...), custom_call_target="tpu_custom_call" | custom-call | flops 3000000000 | tf_op jit(solution)/shard_map/pallas_call | solution.py:350
  20.9 5.8 %all-to-all-start = ((f32[8,32,512]{2,1,0:T(8,128)}), f32[8,32,512]{2,1,0:T(8,128)S(1)}, u32[]{:S(2)}, u32[]{:S(2)}) async-start(f32[8,32,512]{2,1,0:T(8,128)} %get-tuple-element.29), calls=%async_computation | async-start | bytes 1048576 | tf_op jit(solution)/shard_map/all_to_all | solution.py:357
  26.7 0.0 collective-permute-done.2.left
  26.7 0.0 collective-permute-done.3.right
  26.7 0.0 copy-start
  26.8 4.8 %shard_map.89.second = f32[8,64,128]{2,1,0:T(8,128)S(1)} custom-call(f32[48,16,128]{2,1,0:T(8,128)S(1)} %get-tuple-element.30.x0_near, f32[32,16,128]{2,1,0:T(8,128)S(1)} %get-tuple-element.31.x1_own, f32[32,1664]{1,0:T(8,128)S(1)} %collective-permute-done.2.left, f32[32,1664]{1,0:T(8,128)S(1)} %collective-permute-done.3.right, f32[31,4096]{1,0:T(8,128)S(1)} %copy-done.1, ...), custom_call_target="tpu_custom_call" | custom-call | flops 10000000000 | tf_op jit(solution)/shard_map/pallas_call | solution.py:358
  31.6 4.6 %all-to-all-done.z01 = f32[8,32,512]{2,1,0:T(8,128)S(1)} async-done(((f32[8,32,512]{2,1,0:T(8,128)}), f32[8,32,512]{2,1,0:T(8,128)S(1)}, u32[]{:S(2)}, u32[]{:S(2)}) %all-to-all-start) | async-done | bytes 524320 | tf_op jit(solution)/shard_map/all_to_all | solution.py:357
  36.2 0.0 copy-done
  36.2 1.0 %shard_map.90 = (f32[8,72,128]{2,1,0:T(8,128)S(1)}, f32[128,512]{1,0:T(8,128)S(1)}, f32[128,512]{1,0:T(8,128)S(1)}, f32[128,512]{1,0:T(8,128)S(1)}) custom-call(f32[8,32,512]{2,1,0:T(8,128)S(1)} %all-to-all-done.z01, f32[8,64,128]{2,1,0:T(8,128)S(1)} %shard_map.89.second, f32[128,128]{1,0:T(8,128)S(1)} %copy-done, f32[8,128]{1,0:T(8,128)S(1)} %get-tuple-element.34.own), custom_call_target="tpu_custom_call" | custom-call | tf_op jit(solution)/shard_map/pallas_call | solution.py:372
  37.2 10.6 %all_to_all.20.z2 = f32[8,72,128]{2,1,0:T(8,128)S(1)} all-to-all(f32[8,72,128]{2,1,0:T(8,128)S(1)} %get-tuple-element.35), channel_id=1, replica_groups=mesh['y'=4,'z'=8,'x'=4,'core'=2] {'x','core'}, dimensions={0} | all-to-all | bytes 589824 | tf_op jit(solution)/shard_map/all_to_all | solution.py:378
  47.8 0.6 shard_map.91
  48.4 0.0 copy-start.3
  48.4 13.1 %all_to_all.21.got = f32[32,8,128]{2,1,0:T(8,128)S(1)} all-to-all(f32[32,8,128]{2,1,0:T(8,128)S(1)} %shard_map.91), channel_id=1, replica_groups=mesh['y'=4,'z'=8,'x'=4,'core'=2] {'y','z'}, dimensions={0} | all-to-all | bytes 262144 | tf_op jit(solution)/shard_map/all_to_all | solution.py:385
  61.5 0.0 copy-done.3
  61.5 0.5 shard_map.92
  62.0 11.6 %all_to_all.22.got = f32[8,72,128]{2,1,0:T(8,128)S(1)} all-to-all(f32[8,72,128]{2,1,0:T(8,128)S(1)} %get-tuple-element.39), channel_id=1, replica_groups=mesh['y'=4,'z'=8,'x'=4,'core'=2] {'x','core'}, dimensions={0} | all-to-all | bytes 589824 | tf_op jit(solution)/shard_map/all_to_all | solution.py:392
  73.6 0.7 shard_map.93
  (1 shorter events, 0.0 us)
Async XLA Ops:
  0.6 15.2 %copy-start.1 = (f32[31,4096]{1,0:T(8,128)S(1)}, f32[31,4096]{1,0:T(8,128)}, u32[]{:S(2)}) copy-start(f32[31,4096]{1,0:T(8,128)} %weights.7) | copy-start | bytes 1523716
  0.6 15.2 %copy-start.2 = (f32[16,4096]{1,0:T(8,128)S(1)}, f32[16,4096]{1,0:T(8,128)}, u32[]{:S(2)}) copy-start(f32[16,4096]{1,0:T(8,128)} %src.5) | copy-start | bytes 786436
  2.0 16.1 %collective-permute-start = (f32[16,1024]{1,0:T(8,128)S(1)}, f32[16,1024]{1,0:T(8,128)S(1)}, u32[]{:S(2)}, u32[]{:S(2)}) collective-permute-start(f32[16,1024]{1,0:T(8,128)S(1)} %get-tuple-element.23), channel_id=1, source_target_pairs={{0,8},{8,16},{16,24},{24,32},{32,40},{40,48},{48,56},{56,64},{64,7... | collective-permute-start | bytes 196616 | tf_op jit(solution)/shard_map/ppermute | solution.py:340
  4.6 13.5 %collective-permute-start.1 = (f32[16,1024]{1,0:T(8,128)S(1)}, f32[16,1024]{1,0:T(8,128)S(1)}, u32[]{:S(2)}, u32[]{:S(2)}) collective-permute-start(f32[16,1024]{1,0:T(8,128)S(1)} %get-tuple-element.24), channel_id=1, source_target_pairs={{8,0},{16,8},{24,16},{32,24},{40,32},{48,40},{56,48},{64,56},{72,6... | collective-permute-start | bytes 196616 | tf_op jit(solution)/shard_map/ppermute | solution.py:340
  11.1 15.7 %collective-permute-start.2 = (f32[32,1664]{1,0:T(8,128)S(1)}, f32[32,1664]{1,0:T(8,128)S(1)}, u32[]{:S(2)}, u32[]{:S(2)}) collective-permute-start(f32[32,1664]{1,0:T(8,128)S(1)} %get-tuple-element.32), channel_id=1, source_target_pairs={{0,8},{8,16},{16,24},{24,32},{32,40},{40,48},{48,56},{56,64},{64,7... | collective-permute-start | bytes 638984 | tf_op jit(solution)/shard_map/ppermute | solution.py:341
  11.1 15.7 %collective-permute-start.3 = (f32[32,1664]{1,0:T(8,128)S(1)}, f32[32,1664]{1,0:T(8,128)S(1)}, u32[]{:S(2)}, u32[]{:S(2)}) collective-permute-start(f32[32,1664]{1,0:T(8,128)S(1)} %get-tuple-element.33), channel_id=1, source_target_pairs={{8,0},{16,8},{24,16},{32,24},{40,32},{48,40},{56,48},{64,56},{72,6... | collective-permute-start | bytes 638984 | tf_op jit(solution)/shard_map/ppermute | solution.py:341
  20.9 15.3 %all-to-all-start = ((f32[8,32,512]{2,1,0:T(8,128)}), f32[8,32,512]{2,1,0:T(8,128)S(1)}, u32[]{:S(2)}, u32[]{:S(2)}) async-start(f32[8,32,512]{2,1,0:T(8,128)} %get-tuple-element.29), calls=%async_computation | async-start | bytes 1048576 | tf_op jit(solution)/shard_map/all_to_all | solution.py:357
  26.7 9.5 %copy-start = (f32[128,128]{1,0:T(8,128)S(1)}, f32[128,128]{1,0:T(8,128)}, u32[]{:S(2)}) copy-start(f32[128,128]{1,0:T(8,128)} %to_modes.5) | copy-start | bytes 196612
  48.4 13.1 %copy-start.3 = (f32[128,128]{1,0:T(8,128)S(1)}, f32[128,128]{1,0:T(8,128)}, u32[]{:S(2)}) copy-start(f32[128,128]{1,0:T(8,128)} %from_modes.1) | copy-start | bytes 196612

commit v7 on v6

--- a/solution.py
+++ b/solution.py
@@ -20,7 +20,7 @@
 PARTS = 8
 PART = BLOCKS * LANES // PARTS
 MODES = 128
-FLAT = SLAB * PART // LANES
+FLAT = SLAB * PART // 8
 WIDE = 2 * HALO * LANES
 NEAR = HALO * LANES
 HALF = NEAR // 2
@@ -71,25 +71,37 @@
         copy.wait()
 
 
-def pack_kernel(src, weights, shifts, neighbors, eig, up, down, up_far, down_far, own, nb_in, sh_in, w_in, eig_in, sems):
+def odd():
+    return lax.rem(lax.axis_index("z"), 2)
+
+
+def aligned(start):
+    return pl.multiple_of(start, LANES)
+
+
+def pack_kernel(src, weights, shifts, neighbors, eig, *refs):
+    nears, fars, (own, nb_in, sh_in, w_in, eig_in, sems) = refs[0:2], refs[2:4], refs[4:]
     last = BLOCKS * LANES
-    ends = ((up, up_far, last - NEAR, last - WIDE), (down, down_far, 0, NEAR))
     pairs = [(neighbors, nb_in), (eig, eig_in), (shifts, sh_in)]
-    for k, (near_out, far_out, near, far) in enumerate(ends):
+    rightward = [odd() == k for k in range(2)]
+    starts = [aligned(jnp.where(up, last - NEAR, 0)) for up in rightward]
+    for k in range(2):
+        far = aligned(jnp.where(rightward[k], last - WIDE, NEAR))
         pairs += [
-            (src.at[:, pl.ds(near, NEAR)], near_out),
-            (weights.at[:, pl.ds(near, NEAR)], w_in.at[k]),
-            (src.at[:, pl.ds(far, HALF)], far_out.at[0:SLAB, 0:HALF]),
-            (src.at[:, pl.ds(far + HALF, HALF)], far_out.at[SLAB : 2 * SLAB, 0:HALF]),
+            (src.at[:, pl.ds(starts[k], NEAR)], nears[k]),
+            (weights.at[:, pl.ds(starts[k], NEAR)], w_in.at[k]),
+            (src.at[:, pl.ds(far, HALF)], fars[k].at[0:SLAB, 0:HALF]),
+            (src.at[:, pl.ds(aligned(far + HALF), HALF)], fars[k].at[SLAB : 2 * SLAB, 0:HALF]),
         ]
     wait_all(start_all(sems, pairs))
     nb = nb_in[...].astype(jnp.float32)
-    for k, (_, out, near, _) in enumerate(ends):
-        block = near // LANES
-        out[0:STENCIL, HALF:TAIL] = w_in[k]
-        out[STENCIL:ROWS, HALF:TAIL] = sh_in[:, near : near + NEAR]
-        out[:, TAIL:] = jnp.zeros((ROWS, LANES), jnp.float32)
-        out[0:STENCIL, TAIL : TAIL + HALO] = nb[:, block : block + HALO]
+    for k in range(2):
+        fars[k][0:STENCIL, HALF:TAIL] = w_in[k]
+        fars[k][STENCIL:ROWS, HALF:TAIL] = sh_in[:, pl.ds(starts[k], NEAR)]
+        fars[k][:, TAIL:] = jnp.zeros((ROWS, LANES), jnp.float32)
+        fars[k][0:STENCIL, TAIL : TAIL + HALO] = jnp.where(
+            rightward[k], nb[:, BLOCKS - HALO :], nb[:, :HALO]
+        )
     own[...] = jnp.broadcast_to(eig_in[...], own.shape)
 
 
@@ -130,12 +142,12 @@
     lax.fori_loop(0, (BLOCKS - 2 * HALO) // UNROLL, step, 0)
 
 
-def edge_kernel(src, left, right, weights, diag, inner, nb_in, out, x0, x1, nb, sems):
+def edge_kernel(src, near_0, near_1, weights, diag, inner, nb_in, out, x0, x1, nb, sems):
     copies = start_all(sems, [(nb_in, nb)])
-    for j in range(HALO):
-        cols = slice(j * LANES, (j + 1) * LANES)
-        x0[j] = left[:, cols]
-        x0[HALO + BLOCKS + j] = right[:, cols]
+    for k, near in enumerate((near_0, near_1)):
+        base = jnp.where(odd() == k, HALO + BLOCKS, 0)
+        for j in range(HALO):
+            x0[base + j] = near[:, j * LANES : (j + 1) * LANES]
     for j in range(BLOCKS):
         x0[HALO + j] = src[:, j * LANES : (j + 1) * LANES]
     for r in range(PARTS):
@@ -163,24 +175,24 @@
     lax.fori_loop(0, 2, step, 0)
 
 
-def outer_kernel(x0_near, x1_own, left, right, weights, diag, nb_in, out, x0, x1, nbv, nbs, nb, sems):
-    nbv[0] = left[:, TAIL:].astype(jnp.int32)
-    nbv[1] = right[:, TAIL:].astype(jnp.int32)
+def outer_kernel(x0_near, x1_own, far_0, far_1, weights, diag, nb_in, out, x0, x1, nbv, nbs, nb, sems):
+    nbv[0] = far_0[:, TAIL:].astype(jnp.int32)
+    nbv[1] = far_1[:, TAIL:].astype(jnp.int32)
     copies = start_all(sems, [(nbv.at[k], nbs.at[k]) for k in range(2)] + [(nb_in, nb)])
-    for half in range(2):
-        rows = slice(half * SLAB, half * SLAB + SLAB)
-        for j in range(HALO // 2):
-            cols = slice(j * LANES, (j + 1) * LANES)
-            x0[half * HALO // 2 + j] = left[rows, cols]
-            x0[3 * HALO + BLOCKS + half * HALO // 2 + j] = right[rows, cols]
+    for k, far in enumerate((far_0, far_1)):
+        base = jnp.where(odd() == k, 3 * HALO + BLOCKS, 0)
+        for j in range(HALO):
+            half, place = divmod(j, HALO // 2)
+            x0[base + j] = far[half * SLAB : (half + 1) * SLAB, place * LANES : (place + 1) * LANES]
     for j in range(EXT1):
         x0[HALO + j] = x0_near[j]
     for j in range(BLOCKS):
         x1[HALO + j] = x1_own[j]
     wait_all(copies)
-    for side, ref in ((0, left), (1, right)):
+    for side, ref in ((0, far_0), (1, far_1)):
+        base = jnp.where(odd() == side, HALO + BLOCKS, 0)
         for j in range(HALO):
-            e = j + side * (HALO + BLOCKS)
+            e = base + j
             cols = slice(HALF + j * LANES, HALF + (j + 1) * LANES)
             x1[e] = apply(
                 lambda c: x0[c],
@@ -193,14 +205,16 @@
     def step(i, _):
         for u in range(UNROLL):
             b = i * UNROLL + u
-            rows = pl.ds(pl.multiple_of(lax.rem(b, PART // LANES) * SLAB, SLAB), SLAB)
-            out[lax.div(b, PART // LANES), rows, :] = apply(
+            value = apply(
                 lambda c: x1[c],
                 b + HALO,
                 diag[b],
                 lambda s: weights[s : s + 1, column(0, b)],
                 lambda s: nb[s, b],
             )
+            place = lax.rem(b, PART // LANES)
+            for half in range(SLAB // 8):
+                out[lax.div(b, PART // LANES), :, column(half * PART, place)] = value[half * 8 : half * 8 + 8]
         return 0
 
     lax.fori_loop(0, BLOCKS // UNROLL, step, 0)
@@ -236,18 +250,18 @@
     partial[...] = e * (m1 + i0)
     g = sums(((m0, m0), (m0, i0), (i0, i0)), 0)
     for r in range(PARTS):
-        out[r, 0:FLAT, :] = second[r]
-        out[r, FLAT:, :] = g
+        out[r, :, 0:FLAT] = second[r]
+        out[r, :, FLAT:] = g
 
 
 def again_kernel(z2, modal, image, partial, to_modes, out, s):
     for r in range(PARTS):
-        for j in range(PART // LANES):
-            cols = slice(j * LANES, (j + 1) * LANES)
-            s[r * SLAB : (r + 1) * SLAB, cols] = z2[r, j * SLAB : (j + 1) * SLAB, :]
+        for half in range(SLAB // 8):
+            row = r * SLAB + half * 8
+            s[row : row + 8, :] = z2[r, :, half * PART : (half + 1) * PART]
     again = mm(to_modes[...], s[...]) + partial[...]
     m0, i0 = modal[...], image[...]
-    g = jnp.sum(z2[:, FLAT:, :], axis=0) + sums(((m0, again), (i0, again), (again, again)), 3)
+    g = jnp.sum(z2[:, :, FLAT:], axis=0) + sums(((m0, again), (i0, again), (again, again)), 3)
     out[...] = jnp.broadcast_to(g[None], out.shape)
 
 
@@ -280,18 +294,18 @@
     mix = jnp.concatenate([mm(from_m * (over + u0 + u1 * e), to_m), mm(from_m * u1, to_m)], axis=1)
     value = mm(mix, s[...])
     for r in range(PARTS):
-        for j in range(PART // LANES):
-            cols = slice(j * LANES, (j + 1) * LANES)
-            out[r, j * SLAB : (j + 1) * SLAB, :] = value[r * SLAB : (r + 1) * SLAB, cols]
-        out[r, FLAT:, :] = ours
+        for half in range(SLAB // 8):
+            row = r * SLAB + half * 8
+            out[r, :, half * PART : (half + 1) * PART] = value[row : row + 8, :]
+        out[r, :, FLAT:] = ours
 
 
 def unpack_kernel(got, side, place, out, mine):
     for r in range(PARTS):
-        for j in range(PART // LANES):
-            start = r * PART + j * LANES
-            out[:, start : start + LANES] = got[r, j * SLAB : (j + 1) * SLAB, :]
-    squares = side[0:1, :] + sum(got[r, FLAT : FLAT + 1, :] for r in range(PARTS))
+        for half in range(SLAB // 8):
+            rows = slice(half * 8, half * 8 + 8)
+            out[rows, r * PART : (r + 1) * PART] = got[r, :, half * PART : (half + 1) * PART]
+    squares = side[0:1, :] + sum(got[r, 0:1, FLAT:] for r in range(PARTS))
     norm = jnp.sqrt(jnp.maximum(squares, 0.0) / side[1:2, :])
     here = place[0:1, 0:SLAB]
     picked = norm[:, 0:SLAB]
@@ -325,7 +339,7 @@
     eig = eigenvalue.reshape(1, -1)
     nears, fars = f32(SLAB, NEAR), f32(ROWS, TAIL + LANES)
     offsets = jax.ShapeDtypeStruct(neighbors.shape, neighbors.dtype)
-    up, down, up_far, down_far, own, nb, shift_row = call(
+    near_0, near_1, far_0, far_1, own, nb, shift_row = call(
         pack_kernel,
         (nears, nears, fars, fars, f32(8, LANES), offsets, f32(1, BLOCKS * LANES)),
         [HBM] * 5,
@@ -335,10 +349,12 @@
             pltpu.SemaphoreType.DMA((11,)),
         ],
     )(*(pinned(v) for v in (source, weights, shift_row, neighbors, eig)))
-    onward = [(i, (i + 1) % lat) for i in range(lat)]
-    back = [(j, i) for i, j in onward]
-    left, right = lax.ppermute(up, LAT, onward), lax.ppermute(down, LAT, back)
-    left_far, right_far = lax.ppermute(up_far, LAT, onward), lax.ppermute(down_far, LAT, back)
+    swaps = [
+        [(i, (i + turn) % lat) for i, turn in ((i, 1 if i % 2 == k else -1) for i in range(lat))]
+        for k in range(2)
+    ]
+    near_0, near_1 = lax.ppermute(near_0, LAT, swaps[0]), lax.ppermute(near_1, LAT, swaps[1])
+    far_0, far_1 = lax.ppermute(far_0, LAT, swaps[0]), lax.ppermute(far_1, LAT, swaps[1])
     smem_offsets = pltpu.SMEM((STENCIL, BLOCKS), jnp.int32)
     inner, diag, place = call(
         inner_kernel,
@@ -353,11 +369,11 @@
         [VMEM] * 7,
         [smem_offsets, pltpu.SemaphoreType.DMA((1,))],
         cost=COST_1,
-    )(source, left, right, weights, diag, inner, nb)
+    )(source, near_0, near_1, weights, diag, inner, nb)
     z01 = lax.all_to_all(first, RAD, 0, 0, tiled=True)
     second = call(
         outer_kernel,
-        f32(PARTS, FLAT, LANES),
+        f32(PARTS, 8, FLAT),
         [VMEM] * 7,
         [
             pltpu.VMEM((EXT2, SLAB, LANES), jnp.float32),
@@ -368,10 +384,10 @@
             pltpu.SemaphoreType.DMA((3,)),
         ],
         cost=COST_2,
-    )(x0, x1, left_far, right_far, weights, diag, nb)
+    )(x0, x1, far_0, far_1, weights, diag, nb)
     sent, modal, image, partial = call(
         gram_kernel,
-        (f32(PARTS, FLAT + 8, LANES),) + (f32(MODES, PART),) * 3,
+        (f32(PARTS, 8, FLAT + LANES),) + (f32(MODES, PART),) * 3,
         [VMEM] * 4,
         [pltpu.VMEM((MODES, 2 * PART), jnp.float32)],
     )(z01, second, to_modes, own)
@@ -385,7 +401,7 @@
     g = lax.all_to_all(g, LAT, 0, 0, tiled=True)
     mixed, side = call(
         finish_kernel,
-        (f32(PARTS, FLAT + 8, LANES), f32(8, LANES)),
+        (f32(PARTS, 8, FLAT + LANES), f32(8, LANES)),
         [VMEM] * 5,
         [pltpu.VMEM((2 * MODES, PART), jnp.float32)],
     )(g, z01, to_modes, from_modes, own)

time: 74.7 us -> 73.7 us (0.987)
  starting transfers between devices: 19.6 us -> 17.2 us
  blocking collectives: 35.3 us -> 36.6 us
    ppermute x4, starting transfers between devices: 13.8 us -> 11.1 us  [the longest x1 7.12 us: on_device(): lax.ppermute(near_1, LAT, swaps[1])]
    all_to_all x1, blocking collectives: 13.1 us -> 14.5 us  [on_device(): g = lax.all_to_all(g, LAT, 0, 0, tiled=True)]
where the time goes in v7:
time: 73.7 us; the launch traced here: 73.4 us
  blocking collectives  36.6 us (50%)
  starting transfers between devices  17.2 us (23%)
  Pallas kernels  14.1 us (19%)
  waiting for transfers between devices  4.64 us (6%)
  between operations  0.74 us (1%)
    all_to_all x1, blocking collectives, on_device(): g = lax.all_to_all(g, LAT, 0, 0, tiled=True)  14.5 us
    all_to_all x1, blocking collectives, on_device(): got = lax.all_to_all(mixed, RAD, 0, 0, tiled=True)  11.6 us
    all_to_all x1, blocking collectives, on_device(): z2 = lax.all_to_all(sent, RAD, 0, 0, tiled=True)  10.6 us
    ppermute x1, starting transfers between devices, on_device(): lax.ppermute(near_1, LAT, swaps[1])  7.12 us
    all_to_all x1, starting transfers between devices, on_device(): z01 = lax.all_to_all(first, RAD, 0, 0, tiled=True)  6.1 us
    pallas_call x1, Pallas kernels, on_device(): call(outer_kernel, f32(PARTS, 8, FLAT), [VMEM] * 7, [pltpu.VMEM((EXT2, SL...  4.83 us
    all_to_all x1, waiting for transfers between devices, on_device(): z01 = lax.all_to_all(first, RAD, 0, 0, tiled=True)  4.63 us
    pallas_call x1, Pallas kernels, on_device(): call(edge_kernel, (f32(PARTS, 2 * SLAB, PART), f32(EXT1, SLAB, LANES), f3...  2.79 us
  transfers between devices with their start and end apart: 5, of which 1 were waited for; matrix products, arithmetic and copies ran while one was open for 0% of the time, Pallas kernels for 13%

profile of v7, /device:TPU:1, one launch (start us, length us, event | category | flops | bytes accessed | tf_op | source)
XLA Modules:
  0.0 73.4 jit_solution(9561090316719748646)
XLA Ops:
  0.6 0.0 copy-start.1
  0.6 0.0 copy-start.2
  0.7 1.4 %shard_map.86 = (f32[16,1024]{1,0:T(8,128)S(1)}, f32[16,1024]{1,0:T(8,128)S(1)}, f32[32,1664]{1,0:T(8,128)S(1)}, f32[32,1664]{1,0:T(8,128)S(1)}, f32[8,128]{1,0:...) custom-call(f32[16,4096]{1,0:T(8,128)} %src.5, f32[31,4096]{1,0:T(8,128)} %weights.7, f32[1,4096]{1,0:T(1,128)} %bitcast.3, ...), custom_call_target="tpu_custom_call" | custom-call | tf_op jit(solution)/shard_map/pallas_call | solution.py:342
  2.1 2.6 %collective-permute-start = (f32[16,1024]{1,0:T(8,128)S(1)}, f32[16,1024]{1,0:T(8,128)S(1)}, u32[]{:S(2)}, u32[]{:S(2)}) collective-permute-start(f32[16,1024]{1,0:T(8,128)S(1)} %get-tuple-element.23), channel_id=1, source_target_pairs={{0,8},{8,0},{16,24},{24,16},{32,40},{40,32},{48,56},{56,48},{64,72... | collective-permute-start | bytes 196616 | tf_op jit(solution)/shard_map/ppermute | solution.py:356
  4.7 7.1 %collective-permute-start.1 = (f32[16,1024]{1,0:T(8,128)S(1)}, f32[16,1024]{1,0:T(8,128)S(1)}, u32[]{:S(2)}, u32[]{:S(2)}) collective-permute-start(f32[16,1024]{1,0:T(8,128)S(1)} %get-tuple-element.24), channel_id=1, source_target_pairs={{0,248},{8,16},{16,8},{24,32},{32,24},{40,48},{48,40},{56,64},{64,... | collective-permute-start | bytes 196616 | tf_op jit(solution)/shard_map/ppermute | solution.py:356
  11.8 0.0 collective-permute-start.2
  11.8 1.5 %collective-permute-start.3 = (f32[32,1664]{1,0:T(8,128)S(1)}, f32[32,1664]{1,0:T(8,128)S(1)}, u32[]{:S(2)}, u32[]{:S(2)}) collective-permute-start(f32[32,1664]{1,0:T(8,128)S(1)} %get-tuple-element.33), channel_id=1, source_target_pairs={{0,248},{8,16},{16,8},{24,32},{32,24},{40,48},{48,40},{56,64},{64,... | collective-permute-start | bytes 638984 | tf_op jit(solution)/shard_map/ppermute | solution.py:357
  13.2 0.0 copy-done.1
  13.2 0.0 copy-done.2
  13.2 2.2 %shard_map.87 = (f32[16,16,128]{2,1,0:T(8,128)S(1)}, f32[32,1,128]{2,1,0:T(1,128)S(1)}, f32[8,128]{1,0:T(8,128)S(1)}) custom-call(f32[16,4096]{1,0:T(8,128)S(1)} %copy-done.2, f32[31,4096]{1,0:T(8,128)S(1)} %copy-done.1, f32[1,4096]{1,0:T(1,128)S(1)} %get-tuple-element.25.shifts, s32[31,32]{1,0:T(8,128)S(1)} %get-tuple-element.26.nb_in, ...), custom_call_target="tpu_custom_call" | custom-call | flops 3000000000 | tf_op jit(solution)/shard_map/pallas_call | solution.py:359
  15.5 0.0 collective-permute-done.near_0
  15.5 0.0 collective-permute-done.1.near_1
  15.5 2.8 %shard_map.88 = (f32[8,32,512]{2,1,0:T(8,128)}, f32[48,16,128]{2,1,0:T(8,128)S(1)}, f32[32,16,128]{2,1,0:T(8,128)S(1)}) custom-call(f32[16,4096]{1,0:T(8,128)S(1)} %copy-done.2, f32[16,1024]{1,0:T(8,128)S(1)} %collective-permute-done.near_0, f32[16,1024]{1,0:T(8,128)S(1)} %collective-permute-done.1.near_1, f32[31,4096]{1,0:T(8,128)S(1)} %copy-done.1, ...), custom_call_target="tpu_custom_call" | custom-call | flops 3000000000 | tf_op jit(solution)/shard_map/pallas_call | solution.py:366
  18.3 6.1 %all-to-all-start = ((f32[8,32,512]{2,1,0:T(8,128)}), f32[8,32,512]{2,1,0:T(8,128)S(1)}, u32[]{:S(2)}, u32[]{:S(2)}) async-start(f32[8,32,512]{2,1,0:T(8,128)} %get-tuple-element.29), calls=%async_computation | async-start | bytes 1048576 | tf_op jit(solution)/shard_map/all_to_all | solution.py:373
  24.4 0.0 collective-permute-done.2.far_0
  24.4 0.0 collective-permute-done.3.far_1
  24.4 0.0 copy-start
  24.4 4.8 %shard_map.89.second = f32[8,8,1024]{2,1,0:T(8,128)S(1)} custom-call(f32[48,16,128]{2,1,0:T(8,128)S(1)} %get-tuple-element.30.x0_near, f32[32,16,128]{2,1,0:T(8,128)S(1)} %get-tuple-element.31.x1_own, f32[32,1664]{1,0:T(8,128)S(1)} %collective-permute-done.2.far_0, f32[32,1664]{1,0:T(8,128)S(1)} %collective-permute-done.3.far_1, f32[31,4096]{1,0:T(8,128)S(1)} %copy-done.1, ...), custom_call_target="tpu_custom_call" | custom-call | flops 10000000000 | tf_op jit(solution)/shard_map/pallas_call | solution.py:374
  29.3 4.6 %all-to-all-done.z01 = f32[8,32,512]{2,1,0:T(8,128)S(1)} async-done(((f32[8,32,512]{2,1,0:T(8,128)}), f32[8,32,512]{2,1,0:T(8,128)S(1)}, u32[]{:S(2)}, u32[]{:S(2)}) %all-to-all-start) | async-done | bytes 524320 | tf_op jit(solution)/shard_map/all_to_all | solution.py:373
  33.9 0.0 copy-done
  33.9 1.0 %shard_map.90 = (f32[8,8,1152]{2,1,0:T(8,128)S(1)}, f32[128,512]{1,0:T(8,128)S(1)}, f32[128,512]{1,0:T(8,128)S(1)}, f32[128,512]{1,0:T(8,128)S(1)}) custom-call(f32[8,32,512]{2,1,0:T(8,128)S(1)} %all-to-all-done.z01, f32[8,8,1024]{2,1,0:T(8,128)S(1)} %shard_map.89.second, f32[128,128]{1,0:T(8,128)S(1)} %copy-done, f32[8,128]{1,0:T(8,128)S(1)} %get-tuple-element.34.own), custom_call_target="tpu_custom_call" | custom-call | tf_op jit(solution)/shard_map/pallas_call | solution.py:388
  34.9 10.6 %all_to_all.20.z2 = f32[8,8,1152]{2,1,0:T(8,128)S(1)} all-to-all(f32[8,8,1152]{2,1,0:T(8,128)S(1)} %get-tuple-element.35), channel_id=1, replica_groups=mesh['y'=4,'z'=8,'x'=4,'core'=2] {'x','core'}, dimensions={0} | all-to-all | bytes 589824 | tf_op jit(solution)/shard_map/all_to_all | solution.py:394
  45.4 0.6 shard_map.91
  46.1 0.0 copy-start.3
  46.1 14.5 %all_to_all.21.got = f32[32,8,128]{2,1,0:T(8,128)S(1)} all-to-all(f32[32,8,128]{2,1,0:T(8,128)S(1)} %shard_map.91), channel_id=1, replica_groups=mesh['y'=4,'z'=8,'x'=4,'core'=2] {'y','z'}, dimensions={0} | all-to-all | bytes 262144 | tf_op jit(solution)/shard_map/all_to_all | solution.py:401
  60.6 0.0 copy-done.3
  60.6 0.5 shard_map.92
  61.1 11.6 %all_to_all.22.got = f32[8,8,1152]{2,1,0:T(8,128)S(1)} all-to-all(f32[8,8,1152]{2,1,0:T(8,128)S(1)} %get-tuple-element.39), channel_id=1, replica_groups=mesh['y'=4,'z'=8,'x'=4,'core'=2] {'x','core'}, dimensions={0} | all-to-all | bytes 589824 | tf_op jit(solution)/shard_map/all_to_all | solution.py:408
  72.7 0.7 shard_map.93
  (1 shorter events, 0.0 us)
Async XLA Ops:
  0.6 12.6 %copy-start.1 = (f32[31,4096]{1,0:T(8,128)S(1)}, f32[31,4096]{1,0:T(8,128)}, u32[]{:S(2)}) copy-start(f32[31,4096]{1,0:T(8,128)} %weights.7) | copy-start | bytes 1523716
  0.6 12.6 %copy-start.2 = (f32[16,4096]{1,0:T(8,128)S(1)}, f32[16,4096]{1,0:T(8,128)}, u32[]{:S(2)}) copy-start(f32[16,4096]{1,0:T(8,128)} %src.5) | copy-start | bytes 786436
  2.1 13.4 %collective-permute-start = (f32[16,1024]{1,0:T(8,128)S(1)}, f32[16,1024]{1,0:T(8,128)S(1)}, u32[]{:S(2)}, u32[]{:S(2)}) collective-permute-start(f32[16,1024]{1,0:T(8,128)S(1)} %get-tuple-element.23), channel_id=1, source_target_pairs={{0,8},{8,0},{16,24},{24,16},{32,40},{40,32},{48,56},{56,48},{64,72... | collective-permute-start | bytes 196616 | tf_op jit(solution)/shard_map/ppermute | solution.py:356
  4.7 10.8 %collective-permute-start.1 = (f32[16,1024]{1,0:T(8,128)S(1)}, f32[16,1024]{1,0:T(8,128)S(1)}, u32[]{:S(2)}, u32[]{:S(2)}) collective-permute-start(f32[16,1024]{1,0:T(8,128)S(1)} %get-tuple-element.24), channel_id=1, source_target_pairs={{0,248},{8,16},{16,8},{24,32},{32,24},{40,48},{48,40},{56,64},{64,... | collective-permute-start | bytes 196616 | tf_op jit(solution)/shard_map/ppermute | solution.py:356
  11.8 12.6 %collective-permute-start.2 = (f32[32,1664]{1,0:T(8,128)S(1)}, f32[32,1664]{1,0:T(8,128)S(1)}, u32[]{:S(2)}, u32[]{:S(2)}) collective-permute-start(f32[32,1664]{1,0:T(8,128)S(1)} %get-tuple-element.32), channel_id=1, source_target_pairs={{0,8},{8,0},{16,24},{24,16},{32,40},{40,32},{48,56},{56,48},{64,72... | collective-permute-start | bytes 638984 | tf_op jit(solution)/shard_map/ppermute | solution.py:357
  11.8 12.6 %collective-permute-start.3 = (f32[32,1664]{1,0:T(8,128)S(1)}, f32[32,1664]{1,0:T(8,128)S(1)}, u32[]{:S(2)}, u32[]{:S(2)}) collective-permute-start(f32[32,1664]{1,0:T(8,128)S(1)} %get-tuple-element.33), channel_id=1, source_target_pairs={{0,248},{8,16},{16,8},{24,32},{32,24},{40,48},{48,40},{56,64},{64,... | collective-permute-start | bytes 638984 | tf_op jit(solution)/shard_map/ppermute | solution.py:357
  18.3 15.6 %all-to-all-start = ((f32[8,32,512]{2,1,0:T(8,128)}), f32[8,32,512]{2,1,0:T(8,128)S(1)}, u32[]{:S(2)}, u32[]{:S(2)}) async-start(f32[8,32,512]{2,1,0:T(8,128)} %get-tuple-element.29), calls=%async_computation | async-start | bytes 1048576 | tf_op jit(solution)/shard_map/all_to_all | solution.py:373
  24.4 9.5 %copy-start = (f32[128,128]{1,0:T(8,128)S(1)}, f32[128,128]{1,0:T(8,128)}, u32[]{:S(2)}) copy-start(f32[128,128]{1,0:T(8,128)} %to_modes.5) | copy-start | bytes 196612
  46.1 14.5 %copy-start.3 = (f32[128,128]{1,0:T(8,128)S(1)}, f32[128,128]{1,0:T(8,128)}, u32[]{:S(2)}) copy-start(f32[128,128]{1,0:T(8,128)} %from_modes.1) | copy-start | bytes 196612

commit v8 on v7

--- a/solution.py
+++ b/solution.py
@@ -79,29 +79,16 @@
     return pl.multiple_of(start, LANES)
 
 
-def pack_kernel(src, weights, shifts, neighbors, eig, *refs):
-    nears, fars, (own, nb_in, sh_in, w_in, eig_in, sems) = refs[0:2], refs[2:4], refs[4:]
-    last = BLOCKS * LANES
-    pairs = [(neighbors, nb_in), (eig, eig_in), (shifts, sh_in)]
-    rightward = [odd() == k for k in range(2)]
-    starts = [aligned(jnp.where(up, last - NEAR, 0)) for up in rightward]
-    for k in range(2):
-        far = aligned(jnp.where(rightward[k], last - WIDE, NEAR))
-        pairs += [
-            (src.at[:, pl.ds(starts[k], NEAR)], nears[k]),
-            (weights.at[:, pl.ds(starts[k], NEAR)], w_in.at[k]),
-            (src.at[:, pl.ds(far, HALF)], fars[k].at[0:SLAB, 0:HALF]),
-            (src.at[:, pl.ds(aligned(far + HALF), HALF)], fars[k].at[SLAB : 2 * SLAB, 0:HALF]),
-        ]
+def rightward(swap):
+    return odd() == swap
+
+
+def pack_kernel(src, weights, shifts, neighbors, eig, near_0, near_1, own, nb, shift_row, eig_in, sems):
+    pairs = [(neighbors, nb), (eig, eig_in), (shifts, shift_row)]
+    for k, near in enumerate((near_0, near_1)):
+        start = aligned(jnp.where(rightward(k), BLOCKS * LANES - NEAR, 0))
+        pairs.append((src.at[:, pl.ds(start, NEAR)], near))
     wait_all(start_all(sems, pairs))
-    nb = nb_in[...].astype(jnp.float32)
-    for k in range(2):
-        fars[k][0:STENCIL, HALF:TAIL] = w_in[k]
-        fars[k][STENCIL:ROWS, HALF:TAIL] = sh_in[:, pl.ds(starts[k], NEAR)]
-        fars[k][:, TAIL:] = jnp.zeros((ROWS, LANES), jnp.float32)
-        fars[k][0:STENCIL, TAIL : TAIL + HALO] = jnp.where(
-            rightward[k], nb[:, BLOCKS - HALO :], nb[:, :HALO]
-        )
     own[...] = jnp.broadcast_to(eig_in[...], own.shape)
 
 
@@ -119,9 +106,22 @@
     return acc
 
 
-def inner_kernel(src, weights, shifts, nb_in, place_in, x1, diag, place, nb, sems):
+def inner_kernel(src, weights, shifts, nb_in, place_in, x1, diag, place, far_0, far_1, nb, sems):
     copies = start_all(sems, [(nb_in, nb)])
     place[...] = place_in[...]
+    offsets = nb_in[...].astype(jnp.float32)
+    for k, out in enumerate((far_0, far_1)):
+        up = rightward(k)
+        near = aligned(jnp.where(up, BLOCKS * LANES - NEAR, 0))
+        far = aligned(jnp.where(up, BLOCKS * LANES - WIDE, NEAR))
+        out[0:SLAB, 0:HALF] = src[:, pl.ds(far, HALF)]
+        out[SLAB : 2 * SLAB, 0:HALF] = src[:, pl.ds(aligned(far + HALF), HALF)]
+        out[0:STENCIL, HALF:TAIL] = weights[:, pl.ds(near, NEAR)]
+        out[STENCIL:ROWS, HALF:TAIL] = shifts[:, pl.ds(near, NEAR)]
+        out[:, TAIL:] = jnp.zeros((ROWS, LANES), jnp.float32)
+        out[0:STENCIL, TAIL : TAIL + HALO] = jnp.where(
+            up, offsets[:, BLOCKS - HALO :], offsets[:, :HALO]
+        )
     for j in range(BLOCKS):
         cols = slice(j * LANES, (j + 1) * LANES)
         diag[j] = jnp.sum(weights[:, cols], axis=0, keepdims=True) + shifts[:, cols]
@@ -339,30 +339,26 @@
     eig = eigenvalue.reshape(1, -1)
     nears, fars = f32(SLAB, NEAR), f32(ROWS, TAIL + LANES)
     offsets = jax.ShapeDtypeStruct(neighbors.shape, neighbors.dtype)
-    near_0, near_1, far_0, far_1, own, nb, shift_row = call(
+    near_0, near_1, own, nb, shift_row = call(
         pack_kernel,
-        (nears, nears, fars, fars, f32(8, LANES), offsets, f32(1, BLOCKS * LANES)),
+        (nears, nears, f32(8, LANES), offsets, f32(1, BLOCKS * LANES)),
         [HBM] * 5,
-        [
-            pltpu.VMEM((2, STENCIL, NEAR), jnp.float32),
-            pltpu.VMEM((1, LANES), jnp.float32),
-            pltpu.SemaphoreType.DMA((11,)),
-        ],
+        [pltpu.VMEM((1, LANES), jnp.float32), pltpu.SemaphoreType.DMA((5,))],
     )(*(pinned(v) for v in (source, weights, shift_row, neighbors, eig)))
     swaps = [
         [(i, (i + turn) % lat) for i, turn in ((i, 1 if i % 2 == k else -1) for i in range(lat))]
         for k in range(2)
     ]
     near_0, near_1 = lax.ppermute(near_0, LAT, swaps[0]), lax.ppermute(near_1, LAT, swaps[1])
-    far_0, far_1 = lax.ppermute(far_0, LAT, swaps[0]), lax.ppermute(far_1, LAT, swaps[1])
     smem_offsets = pltpu.SMEM((STENCIL, BLOCKS), jnp.int32)
-    inner, diag, place = call(
+    inner, diag, place, far_0, far_1 = call(
         inner_kernel,
-        (f32(BLOCKS - 2 * HALO, SLAB, LANES), f32(BLOCKS, 1, LANES), f32(8, LANES)),
+        (f32(BLOCKS - 2 * HALO, SLAB, LANES), f32(BLOCKS, 1, LANES), f32(8, LANES), fars, fars),
         [VMEM] * 5,
         [smem_offsets, pltpu.SemaphoreType.DMA((1,))],
         cost=COST_0,
     )(source, weights, shift_row, nb, place)
+    far_0, far_1 = lax.ppermute(far_0, LAT, swaps[0]), lax.ppermute(far_1, LAT, swaps[1])
     first, x0, x1 = call(
         edge_kernel,
         (f32(PARTS, 2 * SLAB, PART), f32(EXT1, SLAB, LANES), f32(BLOCKS, SLAB, LANES)),

time: 73.7 us -> 72.9 us (0.989)
  transfers between devices with their start and end apart: 5 -> 5, of which waited for: 1 -> 1; matrix products, arithmetic and copies ran while one was open for 0% -> 0% of each run, Pallas kernels for 13% -> 14%
where the time goes in v8:
time: 72.9 us; the launch traced here: 72.6 us
  blocking collectives  36.1 us (50%)
  starting transfers between devices  17.3 us (24%)
  Pallas kernels  13.8 us (19%)
  waiting for transfers between devices  4.63 us (6%)
  between operations  0.73 us (1%)
    all_to_all x1, blocking collectives, on_device(): g = lax.all_to_all(g, LAT, 0, 0, tiled=True)  14 us
    all_to_all x1, blocking collectives, on_device(): got = lax.all_to_all(mixed, RAD, 0, 0, tiled=True)  11.6 us
    all_to_all x1, blocking collectives, on_device(): z2 = lax.all_to_all(sent, RAD, 0, 0, tiled=True)  10.6 us
    ppermute x1, starting transfers between devices, on_device(): lax.ppermute(near_1, LAT, swaps[1])  7.12 us
    all_to_all x1, starting transfers between devices, on_device(): z01 = lax.all_to_all(first, RAD, 0, 0, tiled=True)  6.1 us
    pallas_call x1, Pallas kernels, on_device(): call(outer_kernel, f32(PARTS, 8, FLAT), [VMEM] * 7, [pltpu.VMEM((EXT2, SL...  4.83 us
    all_to_all x1, waiting for transfers between devices, on_device(): z01 = lax.all_to_all(first, RAD, 0, 0, tiled=True)  4.62 us
    pallas_call x1, Pallas kernels, on_device(): call(edge_kernel, (f32(PARTS, 2 * SLAB, PART), f32(EXT1, SLAB, LANES), f3...  2.78 us
  transfers between devices with their start and end apart: 5, of which 1 were waited for; matrix products, arithmetic and copies ran while one was open for 0% of the time, Pallas kernels for 14%

profile of v8, /device:TPU:1, one launch (start us, length us, event | category | flops | bytes accessed | tf_op | source)
XLA Modules:
  0.0 72.6 jit_solution(6362657830254414657)
XLA Ops:
  0.6 0.0 copy-start.1
  0.6 0.0 copy-start.2
  0.7 1.0 %shard_map.86 = (f32[16,1024]{1,0:T(8,128)S(1)}, f32[16,1024]{1,0:T(8,128)S(1)}, f32[8,128]{1,0:T(8,128)S(1)}, s32[31,32]{1,0:T(8,128)S(1)}, f32[1,4096]{1,0:T(1,128)S(1)}) custom-call(f32[16,4096]{1,0:T(8,128)} %src.5, f32[31,4096]{1,0:T(8,128)} %weights.7, f32[1,4096]{1,0:T(1,128)} %bitcast.3, s32[31,32]{1,0:T(8,128)} %neighbors.1, f32[1,128]{1,0:T(1,128)} %bitcast.4), custom_call_target="tpu_custom_call" | custom-call | tf_op jit(solution)/shard_map/pallas_call | solution.py:342
  1.7 2.6 %collective-permute-start = (f32[16,1024]{1,0:T(8,128)S(1)}, f32[16,1024]{1,0:T(8,128)S(1)}, u32[]{:S(2)}, u32[]{:S(2)}) collective-permute-start(f32[16,1024]{1,0:T(8,128)S(1)} %get-tuple-element.23), channel_id=1, source_target_pairs={{0,8},{8,0},{16,24},{24,16},{32,40},{40,32},{48,56},{56,48},{64,72... | collective-permute-start | bytes 196616 | tf_op jit(solution)/shard_map/ppermute | solution.py:352
  4.2 7.1 %collective-permute-start.1 = (f32[16,1024]{1,0:T(8,128)S(1)}, f32[16,1024]{1,0:T(8,128)S(1)}, u32[]{:S(2)}, u32[]{:S(2)}) collective-permute-start(f32[16,1024]{1,0:T(8,128)S(1)} %get-tuple-element.24), channel_id=1, source_target_pairs={{0,248},{8,16},{16,8},{24,32},{32,24},{40,48},{48,40},{56,64},{64,... | collective-permute-start | bytes 196616 | tf_op jit(solution)/shard_map/ppermute | solution.py:352
  11.4 0.0 copy-done.1
  11.4 0.0 copy-done.2
  11.4 2.3 %shard_map.87 = (f32[16,16,128]{2,1,0:T(8,128)S(1)}, f32[32,1,128]{2,1,0:T(1,128)S(1)}, f32[8,128]{1,0:T(8,128)S(1)}, f32[32,1664]{1,0:T(8,128)S(1)}, f32[32,1664]{1,0:T(8,128)S(1)}) custom-call(f32[16,4096]{1,0:T(8,128)S(1)} %copy-done.2, f32[31,4096]{1,0:T(8,128)S(1)} %copy-done.1, f32[1,4096]{1,0:T(1,128)S(1)} %get-tuple-element.25.shifts, ...), custom_call_target="tpu_custom_call" | custom-call | flops 3000000000 | tf_op jit(solution)/shard_map/pallas_call | solution.py:354
  13.7 0.1 collective-permute-start.2
  13.8 1.4 %collective-permute-start.3 = (f32[32,1664]{1,0:T(8,128)S(1)}, f32[32,1664]{1,0:T(8,128)S(1)}, u32[]{:S(2)}, u32[]{:S(2)}) collective-permute-start(f32[32,1664]{1,0:T(8,128)S(1)} %get-tuple-element.33), channel_id=1, source_target_pairs={{0,248},{8,16},{16,8},{24,32},{32,24},{40,48},{48,40},{56,64},{64,... | collective-permute-start | bytes 638984 | tf_op jit(solution)/shard_map/ppermute | solution.py:361
  15.2 0.0 collective-permute-done.near_0
  15.2 0.0 collective-permute-done.1.near_1
  15.2 2.8 %shard_map.88 = (f32[8,32,512]{2,1,0:T(8,128)}, f32[48,16,128]{2,1,0:T(8,128)S(1)}, f32[32,16,128]{2,1,0:T(8,128)S(1)}) custom-call(f32[16,4096]{1,0:T(8,128)S(1)} %copy-done.2, f32[16,1024]{1,0:T(8,128)S(1)} %collective-permute-done.near_0, f32[16,1024]{1,0:T(8,128)S(1)} %collective-permute-done.1.near_1, f32[31,4096]{1,0:T(8,128)S(1)} %copy-done.1, ...), custom_call_target="tpu_custom_call" | custom-call | flops 3000000000 | tf_op jit(solution)/shard_map/pallas_call | solution.py:362
  18.0 6.1 %all-to-all-start = ((f32[8,32,512]{2,1,0:T(8,128)}), f32[8,32,512]{2,1,0:T(8,128)S(1)}, u32[]{:S(2)}, u32[]{:S(2)}) async-start(f32[8,32,512]{2,1,0:T(8,128)} %get-tuple-element.29), calls=%async_computation | async-start | bytes 1048576 | tf_op jit(solution)/shard_map/all_to_all | solution.py:369
  24.1 0.0 collective-permute-done.2.far_0
  24.1 0.0 collective-permute-done.3.far_1
  24.1 0.0 copy-start
  24.2 4.8 %shard_map.89.second = f32[8,8,1024]{2,1,0:T(8,128)S(1)} custom-call(f32[48,16,128]{2,1,0:T(8,128)S(1)} %get-tuple-element.30.x0_near, f32[32,16,128]{2,1,0:T(8,128)S(1)} %get-tuple-element.31.x1_own, f32[32,1664]{1,0:T(8,128)S(1)} %collective-permute-done.2.far_0, f32[32,1664]{1,0:T(8,128)S(1)} %collective-permute-done.3.far_1, f32[31,4096]{1,0:T(8,128)S(1)} %copy-done.1, ...), custom_call_target="tpu_custom_call" | custom-call | flops 10000000000 | tf_op jit(solution)/shard_map/pallas_call | solution.py:370
  29.0 4.6 %all-to-all-done.z01 = f32[8,32,512]{2,1,0:T(8,128)S(1)} async-done(((f32[8,32,512]{2,1,0:T(8,128)}), f32[8,32,512]{2,1,0:T(8,128)S(1)}, u32[]{:S(2)}, u32[]{:S(2)}) %all-to-all-start) | async-done | bytes 524320 | tf_op jit(solution)/shard_map/all_to_all | solution.py:369
  33.6 0.0 copy-done
  33.6 1.0 %shard_map.90 = (f32[8,8,1152]{2,1,0:T(8,128)S(1)}, f32[128,512]{1,0:T(8,128)S(1)}, f32[128,512]{1,0:T(8,128)S(1)}, f32[128,512]{1,0:T(8,128)S(1)}) custom-call(f32[8,32,512]{2,1,0:T(8,128)S(1)} %all-to-all-done.z01, f32[8,8,1024]{2,1,0:T(8,128)S(1)} %shard_map.89.second, f32[128,128]{1,0:T(8,128)S(1)} %copy-done, f32[8,128]{1,0:T(8,128)S(1)} %get-tuple-element.34.own), custom_call_target="tpu_custom_call" | custom-call | tf_op jit(solution)/shard_map/pallas_call | solution.py:384
  34.6 10.6 %all_to_all.20.z2 = f32[8,8,1152]{2,1,0:T(8,128)S(1)} all-to-all(f32[8,8,1152]{2,1,0:T(8,128)S(1)} %get-tuple-element.35), channel_id=1, replica_groups=mesh['y'=4,'z'=8,'x'=4,'core'=2] {'x','core'}, dimensions={0} | all-to-all | bytes 589824 | tf_op jit(solution)/shard_map/all_to_all | solution.py:390
  45.2 0.6 shard_map.91
  45.8 0.0 copy-start.3
  45.8 14.0 %all_to_all.21.got = f32[32,8,128]{2,1,0:T(8,128)S(1)} all-to-all(f32[32,8,128]{2,1,0:T(8,128)S(1)} %shard_map.91), channel_id=1, replica_groups=mesh['y'=4,'z'=8,'x'=4,'core'=2] {'y','z'}, dimensions={0} | all-to-all | bytes 262144 | tf_op jit(solution)/shard_map/all_to_all | solution.py:397
  59.8 0.0 copy-done.3
  59.8 0.5 shard_map.92
  60.3 11.6 %all_to_all.22.got = f32[8,8,1152]{2,1,0:T(8,128)S(1)} all-to-all(f32[8,8,1152]{2,1,0:T(8,128)S(1)} %get-tuple-element.39), channel_id=1, replica_groups=mesh['y'=4,'z'=8,'x'=4,'core'=2] {'x','core'}, dimensions={0} | all-to-all | bytes 589824 | tf_op jit(solution)/shard_map/all_to_all | solution.py:404
  71.9 0.7 shard_map.93
  (1 shorter events, 0.0 us)
Async XLA Ops:
  0.6 10.7 %copy-start.1 = (f32[31,4096]{1,0:T(8,128)S(1)}, f32[31,4096]{1,0:T(8,128)}, u32[]{:S(2)}) copy-start(f32[31,4096]{1,0:T(8,128)} %weights.7) | copy-start | bytes 1523716
  0.6 10.7 %copy-start.2 = (f32[16,4096]{1,0:T(8,128)S(1)}, f32[16,4096]{1,0:T(8,128)}, u32[]{:S(2)}) copy-start(f32[16,4096]{1,0:T(8,128)} %src.5) | copy-start | bytes 786436
  1.7 13.5 %collective-permute-start = (f32[16,1024]{1,0:T(8,128)S(1)}, f32[16,1024]{1,0:T(8,128)S(1)}, u32[]{:S(2)}, u32[]{:S(2)}) collective-permute-start(f32[16,1024]{1,0:T(8,128)S(1)} %get-tuple-element.23), channel_id=1, source_target_pairs={{0,8},{8,0},{16,24},{24,16},{32,40},{40,32},{48,56},{56,48},{64,72... | collective-permute-start | bytes 196616 | tf_op jit(solution)/shard_map/ppermute | solution.py:352
  4.2 11.0 %collective-permute-start.1 = (f32[16,1024]{1,0:T(8,128)S(1)}, f32[16,1024]{1,0:T(8,128)S(1)}, u32[]{:S(2)}, u32[]{:S(2)}) collective-permute-start(f32[16,1024]{1,0:T(8,128)S(1)} %get-tuple-element.24), channel_id=1, source_target_pairs={{0,248},{8,16},{16,8},{24,32},{32,24},{40,48},{48,40},{56,64},{64,... | collective-permute-start | bytes 196616 | tf_op jit(solution)/shard_map/ppermute | solution.py:352
  13.7 10.4 %collective-permute-start.2 = (f32[32,1664]{1,0:T(8,128)S(1)}, f32[32,1664]{1,0:T(8,128)S(1)}, u32[]{:S(2)}, u32[]{:S(2)}) collective-permute-start(f32[32,1664]{1,0:T(8,128)S(1)} %get-tuple-element.32), channel_id=1, source_target_pairs={{0,8},{8,0},{16,24},{24,16},{32,40},{40,32},{48,56},{56,48},{64,72... | collective-permute-start | bytes 638984 | tf_op jit(solution)/shard_map/ppermute | solution.py:361
  13.8 10.3 %collective-permute-start.3 = (f32[32,1664]{1,0:T(8,128)S(1)}, f32[32,1664]{1,0:T(8,128)S(1)}, u32[]{:S(2)}, u32[]{:S(2)}) collective-permute-start(f32[32,1664]{1,0:T(8,128)S(1)} %get-tuple-element.33), channel_id=1, source_target_pairs={{0,248},{8,16},{16,8},{24,32},{32,24},{40,48},{48,40},{56,64},{64,... | collective-permute-start | bytes 638984 | tf_op jit(solution)/shard_map/ppermute | solution.py:361
  18.0 15.6 %all-to-all-start = ((f32[8,32,512]{2,1,0:T(8,128)}), f32[8,32,512]{2,1,0:T(8,128)S(1)}, u32[]{:S(2)}, u32[]{:S(2)}) async-start(f32[8,32,512]{2,1,0:T(8,128)} %get-tuple-element.29), calls=%async_computation | async-start | bytes 1048576 | tf_op jit(solution)/shard_map/all_to_all | solution.py:369
  24.1 9.5 %copy-start = (f32[128,128]{1,0:T(8,128)S(1)}, f32[128,128]{1,0:T(8,128)}, u32[]{:S(2)}) copy-start(f32[128,128]{1,0:T(8,128)} %to_modes.5) | copy-start | bytes 196612
  45.8 14.0 %copy-start.3 = (f32[128,128]{1,0:T(8,128)S(1)}, f32[128,128]{1,0:T(8,128)}, u32[]{:S(2)}) copy-start(f32[128,128]{1,0:T(8,128)} %from_modes.1) | copy-start | bytes 196612

commit v9 on v8

--- a/solution.py
+++ b/solution.py
@@ -106,22 +106,9 @@
     return acc
 
 
-def inner_kernel(src, weights, shifts, nb_in, place_in, x1, diag, place, far_0, far_1, nb, sems):
+def inner_kernel(src, weights, shifts, nb_in, place_in, x1, diag, place, nb, sems):
     copies = start_all(sems, [(nb_in, nb)])
     place[...] = place_in[...]
-    offsets = nb_in[...].astype(jnp.float32)
-    for k, out in enumerate((far_0, far_1)):
-        up = rightward(k)
-        near = aligned(jnp.where(up, BLOCKS * LANES - NEAR, 0))
-        far = aligned(jnp.where(up, BLOCKS * LANES - WIDE, NEAR))
-        out[0:SLAB, 0:HALF] = src[:, pl.ds(far, HALF)]
-        out[SLAB : 2 * SLAB, 0:HALF] = src[:, pl.ds(aligned(far + HALF), HALF)]
-        out[0:STENCIL, HALF:TAIL] = weights[:, pl.ds(near, NEAR)]
-        out[STENCIL:ROWS, HALF:TAIL] = shifts[:, pl.ds(near, NEAR)]
-        out[:, TAIL:] = jnp.zeros((ROWS, LANES), jnp.float32)
-        out[0:STENCIL, TAIL : TAIL + HALO] = jnp.where(
-            up, offsets[:, BLOCKS - HALO :], offsets[:, :HALO]
-        )
     for j in range(BLOCKS):
         cols = slice(j * LANES, (j + 1) * LANES)
         diag[j] = jnp.sum(weights[:, cols], axis=0, keepdims=True) + shifts[:, cols]
@@ -142,8 +129,21 @@
     lax.fori_loop(0, (BLOCKS - 2 * HALO) // UNROLL, step, 0)
 
 
-def edge_kernel(src, near_0, near_1, weights, diag, inner, nb_in, out, x0, x1, nb, sems):
+def edge_kernel(src, near_0, near_1, weights, shifts, diag, inner, nb_in, out, x0, x1, far_0, far_1, nb, sems):
     copies = start_all(sems, [(nb_in, nb)])
+    offsets = nb_in[...].astype(jnp.float32)
+    for k, far_out in enumerate((far_0, far_1)):
+        up = rightward(k)
+        near = aligned(jnp.where(up, BLOCKS * LANES - NEAR, 0))
+        far = aligned(jnp.where(up, BLOCKS * LANES - WIDE, NEAR))
+        far_out[0:SLAB, 0:HALF] = src[:, pl.ds(far, HALF)]
+        far_out[SLAB : 2 * SLAB, 0:HALF] = src[:, pl.ds(aligned(far + HALF), HALF)]
+        far_out[0:STENCIL, HALF:TAIL] = weights[:, pl.ds(near, NEAR)]
+        far_out[STENCIL:ROWS, HALF:TAIL] = shifts[:, pl.ds(near, NEAR)]
+        far_out[:, TAIL:] = jnp.zeros((ROWS, LANES), jnp.float32)
+        far_out[0:STENCIL, TAIL : TAIL + HALO] = jnp.where(
+            up, offsets[:, BLOCKS - HALO :], offsets[:, :HALO]
+        )
     for k, near in enumerate((near_0, near_1)):
         base = jnp.where(odd() == k, HALO + BLOCKS, 0)
         for j in range(HALO):
@@ -351,21 +351,27 @@
     ]
     near_0, near_1 = lax.ppermute(near_0, LAT, swaps[0]), lax.ppermute(near_1, LAT, swaps[1])
     smem_offsets = pltpu.SMEM((STENCIL, BLOCKS), jnp.int32)
-    inner, diag, place, far_0, far_1 = call(
+    inner, diag, place = call(
         inner_kernel,
-        (f32(BLOCKS - 2 * HALO, SLAB, LANES), f32(BLOCKS, 1, LANES), f32(8, LANES), fars, fars),
+        (f32(BLOCKS - 2 * HALO, SLAB, LANES), f32(BLOCKS, 1, LANES), f32(8, LANES)),
         [VMEM] * 5,
         [smem_offsets, pltpu.SemaphoreType.DMA((1,))],
         cost=COST_0,
     )(source, weights, shift_row, nb, place)
-    far_0, far_1 = lax.ppermute(far_0, LAT, swaps[0]), lax.ppermute(far_1, LAT, swaps[1])
-    first, x0, x1 = call(
+    first, x0, x1, far_0, far_1 = call(
         edge_kernel,
-        (f32(PARTS, 2 * SLAB, PART), f32(EXT1, SLAB, LANES), f32(BLOCKS, SLAB, LANES)),
-        [VMEM] * 7,
+        (
+            f32(PARTS, 2 * SLAB, PART),
+            f32(EXT1, SLAB, LANES),
+            f32(BLOCKS, SLAB, LANES),
+            fars,
+            fars,
+        ),
+        [VMEM] * 8,
         [smem_offsets, pltpu.SemaphoreType.DMA((1,))],
         cost=COST_1,
-    )(source, near_0, near_1, weights, diag, inner, nb)
+    )(source, near_0, near_1, weights, shift_row, diag, inner, nb)
+    far_0, far_1 = lax.ppermute(far_0, LAT, swaps[0]), lax.ppermute(far_1, LAT, swaps[1])
     z01 = lax.all_to_all(first, RAD, 0, 0, tiled=True)
     second = call(
         outer_kernel,

time: 72.9 us -> 75.7 us (1.038)
  starting transfers between devices: 17.3 us -> 20.7 us
    ppermute x1, starting transfers between devices: 1.44 us -> 4.22 us  [on_device(): lax.ppermute(far_1, LAT, swaps[1])]
  transfers between devices with their start and end apart: 5 -> 5, of which waited for: 1 -> 1; matrix products, arithmetic and copies ran while one was open for 0% -> 0% of each run, Pallas kernels for 14% -> 9%
where the time goes in v9:
time: 75.7 us; the launch traced here: 75.4 us
  blocking collectives  35.5 us (47%)
  starting transfers between devices  20.7 us (27%)
  Pallas kernels  13.7 us (18%)
  waiting for transfers between devices  4.63 us (6%)
    all_to_all x1, blocking collectives, on_device(): g = lax.all_to_all(g, LAT, 0, 0, tiled=True)  13.4 us
    all_to_all x1, blocking collectives, on_device(): got = lax.all_to_all(mixed, RAD, 0, 0, tiled=True)  11.6 us
    all_to_all x1, blocking collectives, on_device(): z2 = lax.all_to_all(sent, RAD, 0, 0, tiled=True)  10.6 us
    ppermute x1, starting transfers between devices, on_device(): lax.ppermute(near_1, LAT, swaps[1])  7.12 us
    all_to_all x1, starting transfers between devices, on_device(): z01 = lax.all_to_all(first, RAD, 0, 0, tiled=True)  6.68 us
    pallas_call x1, Pallas kernels, on_device(): call(outer_kernel, f32(PARTS, 8, FLAT), [VMEM] * 7, [pltpu.VMEM((EXT2, SL...  4.83 us
    all_to_all x1, waiting for transfers between devices, on_device(): z01 = lax.all_to_all(first, RAD, 0, 0, tiled=True)  4.62 us
    ppermute x1, starting transfers between devices, on_device(): lax.ppermute(far_1, LAT, swaps[1])  4.22 us
  transfers between devices with their start and end apart: 5, of which 1 were waited for; matrix products, arithmetic and copies ran while one was open for 0% of the time, Pallas kernels for 9%

profile of v9, /device:TPU:1, one launch (start us, length us, event | category | flops | bytes accessed | tf_op | source)
XLA Modules:
  0.0 75.4 jit_solution(3555131756144457736)
XLA Ops:
  0.6 0.0 copy-start.1
  0.6 0.0 copy-start.2
  0.7 1.0 %shard_map.86 = (f32[16,1024]{1,0:T(8,128)S(1)}, f32[16,1024]{1,0:T(8,128)S(1)}, f32[8,128]{1,0:T(8,128)S(1)}, s32[31,32]{1,0:T(8,128)S(1)}, f32[1,4096]{1,0:T(1,128)S(1)}) custom-call(f32[16,4096]{1,0:T(8,128)} %src.5, f32[31,4096]{1,0:T(8,128)} %weights.7, f32[1,4096]{1,0:T(1,128)} %bitcast.3, s32[31,32]{1,0:T(8,128)} %neighbors.1, f32[1,128]{1,0:T(1,128)} %bitcast.4), custom_call_target="tpu_custom_call" | custom-call | tf_op jit(solution)/shard_map/pallas_call | solution.py:342
  1.7 2.6 %collective-permute-start = (f32[16,1024]{1,0:T(8,128)S(1)}, f32[16,1024]{1,0:T(8,128)S(1)}, u32[]{:S(2)}, u32[]{:S(2)}) collective-permute-start(f32[16,1024]{1,0:T(8,128)S(1)} %get-tuple-element.23), channel_id=1, source_target_pairs={{0,8},{8,0},{16,24},{24,16},{32,40},{40,32},{48,56},{56,48},{64,72... | collective-permute-start | bytes 196616 | tf_op jit(solution)/shard_map/ppermute | solution.py:352
  4.2 7.1 %collective-permute-start.1 = (f32[16,1024]{1,0:T(8,128)S(1)}, f32[16,1024]{1,0:T(8,128)S(1)}, u32[]{:S(2)}, u32[]{:S(2)}) collective-permute-start(f32[16,1024]{1,0:T(8,128)S(1)} %get-tuple-element.24), channel_id=1, source_target_pairs={{0,248},{8,16},{16,8},{24,32},{32,24},{40,48},{48,40},{56,64},{64,... | collective-permute-start | bytes 196616 | tf_op jit(solution)/shard_map/ppermute | solution.py:352
  11.4 0.0 copy-done.1
  11.4 0.0 copy-done.2
  11.4 2.2 %shard_map.87 = (f32[16,16,128]{2,1,0:T(8,128)S(1)}, f32[32,1,128]{2,1,0:T(1,128)S(1)}, f32[8,128]{1,0:T(8,128)S(1)}) custom-call(f32[16,4096]{1,0:T(8,128)S(1)} %copy-done.2, f32[31,4096]{1,0:T(8,128)S(1)} %copy-done.1, f32[1,4096]{1,0:T(1,128)S(1)} %get-tuple-element.25.shifts, s32[31,32]{1,0:T(8,128)S(1)} %get-tuple-element.26.nb_in, ...), custom_call_target="tpu_custom_call" | custom-call | flops 3000000000 | tf_op jit(solution)/shard_map/pallas_call | solution.py:354
  13.6 0.0 collective-permute-done.near_0
  13.6 0.0 collective-permute-done.1.near_1
  13.6 2.8 %shard_map.88 = (f32[8,32,512]{2,1,0:T(8,128)}, f32[48,16,128]{2,1,0:T(8,128)S(1)}, f32[32,16,128]{2,1,0:T(8,128)S(1)}, f32[32,1664]{1,0:T(8,128)S(1)}, f32[32,1664]{1,0:T(8,128)S(1)}) custom-call(f32[16,4096]{1,0:T(8,128)S(1)} %copy-done.2, f32[16,1024]{1,0:T(8,128)S(1)} %collective-permute-done.near_0, f32[16,1024]{1,0:T(8,128)S(1)} %collective-permute-done.1.near_1, ...), custom_call_target="tpu_custom_call" | custom-call | flops 3000000000 | tf_op jit(solution)/shard_map/pallas_call | solution.py:361
  16.5 0.1 collective-permute-start.2
  16.6 4.2 %collective-permute-start.3 = (f32[32,1664]{1,0:T(8,128)S(1)}, f32[32,1664]{1,0:T(8,128)S(1)}, u32[]{:S(2)}, u32[]{:S(2)}) collective-permute-start(f32[32,1664]{1,0:T(8,128)S(1)} %get-tuple-element.33), channel_id=1, source_target_pairs={{0,248},{8,16},{16,8},{24,32},{32,24},{40,48},{48,40},{56,64},{64,... | collective-permute-start | bytes 638984 | tf_op jit(solution)/shard_map/ppermute | solution.py:374
  20.8 6.7 %all-to-all-start = ((f32[8,32,512]{2,1,0:T(8,128)}), f32[8,32,512]{2,1,0:T(8,128)S(1)}, u32[]{:S(2)}, u32[]{:S(2)}) async-start(f32[8,32,512]{2,1,0:T(8,128)} %get-tuple-element.29), calls=%async_computation | async-start | bytes 1048576 | tf_op jit(solution)/shard_map/all_to_all | solution.py:375
  27.5 0.0 collective-permute-done.2.far_0
  27.5 0.0 collective-permute-done.3.far_1
  27.5 0.0 copy-start
  27.5 4.8 %shard_map.89.second = f32[8,8,1024]{2,1,0:T(8,128)S(1)} custom-call(f32[48,16,128]{2,1,0:T(8,128)S(1)} %get-tuple-element.30.x0_near, f32[32,16,128]{2,1,0:T(8,128)S(1)} %get-tuple-element.31.x1_own, f32[32,1664]{1,0:T(8,128)S(1)} %collective-permute-done.2.far_0, f32[32,1664]{1,0:T(8,128)S(1)} %collective-permute-done.3.far_1, f32[31,4096]{1,0:T(8,128)S(1)} %copy-done.1, ...), custom_call_target="tpu_custom_call" | custom-call | flops 10000000000 | tf_op jit(solution)/shard_map/pallas_call | solution.py:376
  32.3 4.6 %all-to-all-done.z01 = f32[8,32,512]{2,1,0:T(8,128)S(1)} async-done(((f32[8,32,512]{2,1,0:T(8,128)}), f32[8,32,512]{2,1,0:T(8,128)S(1)}, u32[]{:S(2)}, u32[]{:S(2)}) %all-to-all-start) | async-done | bytes 524320 | tf_op jit(solution)/shard_map/all_to_all | solution.py:375
  37.0 0.0 copy-done
  37.0 1.0 %shard_map.90 = (f32[8,8,1152]{2,1,0:T(8,128)S(1)}, f32[128,512]{1,0:T(8,128)S(1)}, f32[128,512]{1,0:T(8,128)S(1)}, f32[128,512]{1,0:T(8,128)S(1)}) custom-call(f32[8,32,512]{2,1,0:T(8,128)S(1)} %all-to-all-done.z01, f32[8,8,1024]{2,1,0:T(8,128)S(1)} %shard_map.89.second, f32[128,128]{1,0:T(8,128)S(1)} %copy-done, f32[8,128]{1,0:T(8,128)S(1)} %get-tuple-element.34.own), custom_call_target="tpu_custom_call" | custom-call | tf_op jit(solution)/shard_map/pallas_call | solution.py:390
  37.9 10.6 %all_to_all.20.z2 = f32[8,8,1152]{2,1,0:T(8,128)S(1)} all-to-all(f32[8,8,1152]{2,1,0:T(8,128)S(1)} %get-tuple-element.35), channel_id=1, replica_groups=mesh['y'=4,'z'=8,'x'=4,'core'=2] {'x','core'}, dimensions={0} | all-to-all | bytes 589824 | tf_op jit(solution)/shard_map/all_to_all | solution.py:396
  48.5 0.6 shard_map.91
  49.1 0.0 copy-start.3
  49.1 13.4 %all_to_all.21.got = f32[32,8,128]{2,1,0:T(8,128)S(1)} all-to-all(f32[32,8,128]{2,1,0:T(8,128)S(1)} %shard_map.91), channel_id=1, replica_groups=mesh['y'=4,'z'=8,'x'=4,'core'=2] {'y','z'}, dimensions={0} | all-to-all | bytes 262144 | tf_op jit(solution)/shard_map/all_to_all | solution.py:403
  62.5 0.0 copy-done.3
  62.5 0.5 shard_map.92
  63.1 11.6 %all_to_all.22.got = f32[8,8,1152]{2,1,0:T(8,128)S(1)} all-to-all(f32[8,8,1152]{2,1,0:T(8,128)S(1)} %get-tuple-element.39), channel_id=1, replica_groups=mesh['y'=4,'z'=8,'x'=4,'core'=2] {'x','core'}, dimensions={0} | all-to-all | bytes 589824 | tf_op jit(solution)/shard_map/all_to_all | solution.py:410
  74.6 0.7 shard_map.93
  (1 shorter events, 0.0 us)
Async XLA Ops:
  0.6 10.7 %copy-start.1 = (f32[31,4096]{1,0:T(8,128)S(1)}, f32[31,4096]{1,0:T(8,128)}, u32[]{:S(2)}) copy-start(f32[31,4096]{1,0:T(8,128)} %weights.7) | copy-start | bytes 1523716
  0.6 10.7 %copy-start.2 = (f32[16,4096]{1,0:T(8,128)S(1)}, f32[16,4096]{1,0:T(8,128)}, u32[]{:S(2)}) copy-start(f32[16,4096]{1,0:T(8,128)} %src.5) | copy-start | bytes 786436
  1.7 11.9 %collective-permute-start = (f32[16,1024]{1,0:T(8,128)S(1)}, f32[16,1024]{1,0:T(8,128)S(1)}, u32[]{:S(2)}, u32[]{:S(2)}) collective-permute-start(f32[16,1024]{1,0:T(8,128)S(1)} %get-tuple-element.23), channel_id=1, source_target_pairs={{0,8},{8,0},{16,24},{24,16},{32,40},{40,32},{48,56},{56,48},{64,72... | collective-permute-start | bytes 196616 | tf_op jit(solution)/shard_map/ppermute | solution.py:352
  4.2 9.4 %collective-permute-start.1 = (f32[16,1024]{1,0:T(8,128)S(1)}, f32[16,1024]{1,0:T(8,128)S(1)}, u32[]{:S(2)}, u32[]{:S(2)}) collective-permute-start(f32[16,1024]{1,0:T(8,128)S(1)} %get-tuple-element.24), channel_id=1, source_target_pairs={{0,248},{8,16},{16,8},{24,32},{32,24},{40,48},{48,40},{56,64},{64,... | collective-permute-start | bytes 196616 | tf_op jit(solution)/shard_map/ppermute | solution.py:352
  16.5 11.0 %collective-permute-start.2 = (f32[32,1664]{1,0:T(8,128)S(1)}, f32[32,1664]{1,0:T(8,128)S(1)}, u32[]{:S(2)}, u32[]{:S(2)}) collective-permute-start(f32[32,1664]{1,0:T(8,128)S(1)} %get-tuple-element.32), channel_id=1, source_target_pairs={{0,8},{8,0},{16,24},{24,16},{32,40},{40,32},{48,56},{56,48},{64,72... | collective-permute-start | bytes 638984 | tf_op jit(solution)/shard_map/ppermute | solution.py:374
  16.6 10.9 %collective-permute-start.3 = (f32[32,1664]{1,0:T(8,128)S(1)}, f32[32,1664]{1,0:T(8,128)S(1)}, u32[]{:S(2)}, u32[]{:S(2)}) collective-permute-start(f32[32,1664]{1,0:T(8,128)S(1)} %get-tuple-element.33), channel_id=1, source_target_pairs={{0,248},{8,16},{16,8},{24,32},{32,24},{40,48},{48,40},{56,64},{64,... | collective-permute-start | bytes 638984 | tf_op jit(solution)/shard_map/ppermute | solution.py:374
  20.8 16.2 %all-to-all-start = ((f32[8,32,512]{2,1,0:T(8,128)}), f32[8,32,512]{2,1,0:T(8,128)S(1)}, u32[]{:S(2)}, u32[]{:S(2)}) async-start(f32[8,32,512]{2,1,0:T(8,128)} %get-tuple-element.29), calls=%async_computation | async-start | bytes 1048576 | tf_op jit(solution)/shard_map/all_to_all | solution.py:375
  27.5 9.5 %copy-start = (f32[128,128]{1,0:T(8,128)S(1)}, f32[128,128]{1,0:T(8,128)}, u32[]{:S(2)}) copy-start(f32[128,128]{1,0:T(8,128)} %to_modes.5) | copy-start | bytes 196612
  49.1 13.4 %copy-start.3 = (f32[128,128]{1,0:T(8,128)S(1)}, f32[128,128]{1,0:T(8,128)}, u32[]{:S(2)}) copy-start(f32[128,128]{1,0:T(8,128)} %from_modes.1) | copy-start | bytes 196612

commit v10 on v8

--- a/solution.py
+++ b/solution.py
@@ -80,7 +80,7 @@
 
 
 def rightward(swap):
-    return odd() == swap
+    return odd() != swap
 
 
 def pack_kernel(src, weights, shifts, neighbors, eig, near_0, near_1, own, nb, shift_row, eig_in, sems):
@@ -127,25 +127,20 @@
         diag[j] = jnp.sum(weights[:, cols], axis=0, keepdims=True) + shifts[:, cols]
     wait_all(copies)
 
-    def step(i, _):
-        for u in range(UNROLL):
-            b = HALO + i * UNROLL + u
-            x1[b - HALO] = apply(
-                lambda c: src[:, column(0, c)],
-                b,
-                diag[b],
-                lambda s: weights[s : s + 1, column(0, b)],
-                lambda s: nb[s, b],
-            )
-        return 0
-
-    lax.fori_loop(0, (BLOCKS - 2 * HALO) // UNROLL, step, 0)
+    for b in range(HALO, BLOCKS - HALO):
+        x1[b - HALO] = apply(
+            lambda c: src[:, column(0, c)],
+            b,
+            diag[b],
+            lambda s: weights[s : s + 1, column(0, b)],
+            lambda s: nb[s, b],
+        )
 
 
 def edge_kernel(src, near_0, near_1, weights, diag, inner, nb_in, out, x0, x1, nb, sems):
     copies = start_all(sems, [(nb_in, nb)])
     for k, near in enumerate((near_0, near_1)):
-        base = jnp.where(odd() == k, HALO + BLOCKS, 0)
+        base = jnp.where(rightward(k), HALO + BLOCKS, 0)
         for j in range(HALO):
             x0[base + j] = near[:, j * LANES : (j + 1) * LANES]
     for j in range(BLOCKS):
@@ -158,21 +153,17 @@
         out[part, SLAB:, place * LANES : (place + 1) * LANES] = inner[j - HALO]
     wait_all(copies)
 
-    def step(i, _):
-        for u in range(UNROLL):
-            b = i * (BLOCKS - HALO) + u
-            value = apply(
-                lambda c: x0[c],
-                b + HALO,
-                diag[b],
-                lambda s: weights[s : s + 1, column(0, b)],
-                lambda s: nb[s, b],
-            )
-            x1[b] = value
-            out[lax.div(b, PART // LANES), SLAB:, column(0, lax.rem(b, PART // LANES))] = value
-        return 0
-
-    lax.fori_loop(0, 2, step, 0)
+    for b in (*range(HALO), *range(BLOCKS - HALO, BLOCKS)):
+        value = apply(
+            lambda c: x0[c],
+            b + HALO,
+            diag[b],
+            lambda s: weights[s : s + 1, column(0, b)],
+            lambda s: nb[s, b],
+        )
+        x1[b] = value
+        part, place = divmod(b, PART // LANES)
+        out[part, SLAB:, place * LANES : (place + 1) * LANES] = value
 
 
 def outer_kernel(x0_near, x1_own, far_0, far_1, weights, diag, nb_in, out, x0, x1, nbv, nbs, nb, sems):
@@ -180,7 +171,7 @@
     nbv[1] = far_1[:, TAIL:].astype(jnp.int32)
     copies = start_all(sems, [(nbv.at[k], nbs.at[k]) for k in range(2)] + [(nb_in, nb)])
     for k, far in enumerate((far_0, far_1)):
-        base = jnp.where(odd() == k, 3 * HALO + BLOCKS, 0)
+        base = jnp.where(rightward(k), 3 * HALO + BLOCKS, 0)
         for j in range(HALO):
             half, place = divmod(j, HALO // 2)
             x0[base + j] = far[half * SLAB : (half + 1) * SLAB, place * LANES : (place + 1) * LANES]
@@ -190,7 +181,7 @@
         x1[HALO + j] = x1_own[j]
     wait_all(copies)
     for side, ref in ((0, far_0), (1, far_1)):
-        base = jnp.where(odd() == side, HALO + BLOCKS, 0)
+        base = jnp.where(rightward(side), HALO + BLOCKS, 0)
         for j in range(HALO):
             e = base + j
             cols = slice(HALF + j * LANES, HALF + (j + 1) * LANES)
@@ -346,7 +337,7 @@
         [pltpu.VMEM((1, LANES), jnp.float32), pltpu.SemaphoreType.DMA((5,))],
     )(*(pinned(v) for v in (source, weights, shift_row, neighbors, eig)))
     swaps = [
-        [(i, (i + turn) % lat) for i, turn in ((i, 1 if i % 2 == k else -1) for i in range(lat))]
+        [(i, (i + turn) % lat) for i, turn in ((i, 1 if i % 2 != k else -1) for i in range(lat))]
         for k in range(2)
     ]
     near_0, near_1 = lax.ppermute(near_0, LAT, swaps[0]), lax.ppermute(near_1, LAT, swaps[1])

time: 72.9 us -> 72.9 us (level)
  blocking collectives: 36.1 us -> 37.3 us
  starting transfers between devices: 17.3 us -> 16.5 us
    ppermute x1, starting transfers between devices: 7.12 us -> 0.01 us  [on_device(): lax.ppermute(near_1, LAT, swaps[1])]
    ppermute x1, starting transfers between devices: 2.55 us -> 8.94 us  [on_device(): lax.ppermute(near_0, LAT, swaps[0])]
    ppermute x1, starting transfers between devices: 0.09 us -> 1.53 us  [on_device(): lax.ppermute(far_0, LAT, swaps[0])]
    ppermute x1, starting transfers between devices: 1.44 us -> 0.12 us  [on_device(): lax.ppermute(far_1, LAT, swaps[1])]
    all_to_all x1, blocking collectives: 14 us -> 15.2 us  [on_device(): g = lax.all_to_all(g, LAT, 0, 0, tiled=True)]
  transfers between devices with their start and end apart: 5 -> 5, of which waited for: 1 -> 1; matrix products, arithmetic and copies ran while one was open for 0% -> 0% of each run, Pallas kernels for 14% -> 13%
where the time goes in v10:
time: 72.9 us; the launch traced here: 72.5 us
  blocking collectives  37.3 us (51%)
  starting transfers between devices  16.5 us (23%)
  Pallas kernels  13.4 us (18%)
  waiting for transfers between devices  4.63 us (6%)
  between operations  0.73 us (1%)
    all_to_all x1, blocking collectives, on_device(): g = lax.all_to_all(g, LAT, 0, 0, tiled=True)  15.2 us
    all_to_all x1, blocking collectives, on_device(): got = lax.all_to_all(mixed, RAD, 0, 0, tiled=True)  11.6 us
    all_to_all x1, blocking collectives, on_device(): z2 = lax.all_to_all(sent, RAD, 0, 0, tiled=True)  10.6 us
    ppermute x1, starting transfers between devices, on_device(): lax.ppermute(near_0, LAT, swaps[0])  8.94 us
    all_to_all x1, starting transfers between devices, on_device(): z01 = lax.all_to_all(first, RAD, 0, 0, tiled=True)  5.87 us
    pallas_call x1, Pallas kernels, on_device(): call(outer_kernel, f32(PARTS, 8, FLAT), [VMEM] * 7, [pltpu.VMEM((EXT2, SL...  4.83 us
    all_to_all x1, waiting for transfers between devices, on_device(): z01 = lax.all_to_all(first, RAD, 0, 0, tiled=True)  4.62 us
    pallas_call x1, Pallas kernels, on_device(): call(edge_kernel, (f32(PARTS, 2 * SLAB, PART), f32(EXT1, SLAB, LANES), f3...  2.69 us
  transfers between devices with their start and end apart: 5, of which 1 were waited for; matrix products, arithmetic and copies ran while one was open for 0% of the time, Pallas kernels for 13%

profile of v10, /device:TPU:1, one launch (start us, length us, event | category | flops | bytes accessed | tf_op | source)
XLA Modules:
  0.0 72.5 jit_solution(8407592276082551926)
XLA Ops:
  0.6 0.0 copy-start.1
  0.6 0.0 copy-start.2
  0.7 1.0 %shard_map.86 = (f32[16,1024]{1,0:T(8,128)S(1)}, f32[16,1024]{1,0:T(8,128)S(1)}, f32[8,128]{1,0:T(8,128)S(1)}, s32[31,32]{1,0:T(8,128)S(1)}, f32[1,4096]{1,0:T(1,128)S(1)}) custom-call(f32[16,4096]{1,0:T(8,128)} %src.5, f32[31,4096]{1,0:T(8,128)} %weights.7, f32[1,4096]{1,0:T(1,128)} %bitcast.3, s32[31,32]{1,0:T(8,128)} %neighbors.1, f32[1,128]{1,0:T(1,128)} %bitcast.4), custom_call_target="tpu_custom_call" | custom-call | tf_op jit(solution)/shard_map/pallas_call | solution.py:333
  1.7 8.9 %collective-permute-start = (f32[16,1024]{1,0:T(8,128)S(1)}, f32[16,1024]{1,0:T(8,128)S(1)}, u32[]{:S(2)}, u32[]{:S(2)}) collective-permute-start(f32[16,1024]{1,0:T(8,128)S(1)} %get-tuple-element.23), channel_id=1, source_target_pairs={{0,248},{8,16},{16,8},{24,32},{32,24},{40,48},{48,40},{56,64},{64,... | collective-permute-start | bytes 196616 | tf_op jit(solution)/shard_map/ppermute | solution.py:343
  10.6 0.0 collective-permute-start.1
  10.6 0.0 copy-done.1
  10.6 0.0 copy-done.2
  10.7 2.0 %shard_map.87 = (f32[16,16,128]{2,1,0:T(8,128)S(1)}, f32[32,1,128]{2,1,0:T(1,128)S(1)}, f32[8,128]{1,0:T(8,128)S(1)}, f32[32,1664]{1,0:T(8,128)S(1)}, f32[32,1664]{1,0:T(8,128)S(1)}) custom-call(f32[16,4096]{1,0:T(8,128)S(1)} %copy-done.2, f32[31,4096]{1,0:T(8,128)S(1)} %copy-done.1, f32[1,4096]{1,0:T(1,128)S(1)} %get-tuple-element.25.shifts, ...), custom_call_target="tpu_custom_call" | custom-call | flops 3000000000 | tf_op jit(solution)/shard_map/pallas_call | solution.py:345
  12.6 1.5 %collective-permute-start.2 = (f32[32,1664]{1,0:T(8,128)S(1)}, f32[32,1664]{1,0:T(8,128)S(1)}, u32[]{:S(2)}, u32[]{:S(2)}) collective-permute-start(f32[32,1664]{1,0:T(8,128)S(1)} %get-tuple-element.32), channel_id=1, source_target_pairs={{0,248},{8,16},{16,8},{24,32},{32,24},{40,48},{48,40},{56,64},{64,... | collective-permute-start | bytes 638984 | tf_op jit(solution)/shard_map/ppermute | solution.py:352
  14.2 0.1 collective-permute-start.3
  14.3 0.0 collective-permute-done.near_0
  14.3 0.0 collective-permute-done.1.near_1
  14.3 2.7 %shard_map.88 = (f32[8,32,512]{2,1,0:T(8,128)}, f32[48,16,128]{2,1,0:T(8,128)S(1)}, f32[32,16,128]{2,1,0:T(8,128)S(1)}) custom-call(f32[16,4096]{1,0:T(8,128)S(1)} %copy-done.2, f32[16,1024]{1,0:T(8,128)S(1)} %collective-permute-done.near_0, f32[16,1024]{1,0:T(8,128)S(1)} %collective-permute-done.1.near_1, f32[31,4096]{1,0:T(8,128)S(1)} %copy-done.1, ...), custom_call_target="tpu_custom_call" | custom-call | flops 3000000000 | tf_op jit(solution)/shard_map/pallas_call | solution.py:353
  17.0 5.9 %all-to-all-start = ((f32[8,32,512]{2,1,0:T(8,128)}), f32[8,32,512]{2,1,0:T(8,128)S(1)}, u32[]{:S(2)}, u32[]{:S(2)}) async-start(f32[8,32,512]{2,1,0:T(8,128)} %get-tuple-element.29), calls=%async_computation | async-start | bytes 1048576 | tf_op jit(solution)/shard_map/all_to_all | solution.py:360
  22.9 0.0 collective-permute-done.2.far_0
  22.9 0.0 collective-permute-done.3.far_1
  22.9 0.0 copy-start
  22.9 4.8 %shard_map.89.second = f32[8,8,1024]{2,1,0:T(8,128)S(1)} custom-call(f32[48,16,128]{2,1,0:T(8,128)S(1)} %get-tuple-element.30.x0_near, f32[32,16,128]{2,1,0:T(8,128)S(1)} %get-tuple-element.31.x1_own, f32[32,1664]{1,0:T(8,128)S(1)} %collective-permute-done.2.far_0, f32[32,1664]{1,0:T(8,128)S(1)} %collective-permute-done.3.far_1, f32[31,4096]{1,0:T(8,128)S(1)} %copy-done.1, ...), custom_call_target="tpu_custom_call" | custom-call | flops 10000000000 | tf_op jit(solution)/shard_map/pallas_call | solution.py:361
  27.7 4.6 %all-to-all-done.z01 = f32[8,32,512]{2,1,0:T(8,128)S(1)} async-done(((f32[8,32,512]{2,1,0:T(8,128)}), f32[8,32,512]{2,1,0:T(8,128)S(1)}, u32[]{:S(2)}, u32[]{:S(2)}) %all-to-all-start) | async-done | bytes 524320 | tf_op jit(solution)/shard_map/all_to_all | solution.py:360
  32.3 0.0 copy-done
  32.4 1.0 %shard_map.90 = (f32[8,8,1152]{2,1,0:T(8,128)S(1)}, f32[128,512]{1,0:T(8,128)S(1)}, f32[128,512]{1,0:T(8,128)S(1)}, f32[128,512]{1,0:T(8,128)S(1)}) custom-call(f32[8,32,512]{2,1,0:T(8,128)S(1)} %all-to-all-done.z01, f32[8,8,1024]{2,1,0:T(8,128)S(1)} %shard_map.89.second, f32[128,128]{1,0:T(8,128)S(1)} %copy-done, f32[8,128]{1,0:T(8,128)S(1)} %get-tuple-element.34.own), custom_call_target="tpu_custom_call" | custom-call | tf_op jit(solution)/shard_map/pallas_call | solution.py:375
  33.3 10.6 %all_to_all.20.z2 = f32[8,8,1152]{2,1,0:T(8,128)S(1)} all-to-all(f32[8,8,1152]{2,1,0:T(8,128)S(1)} %get-tuple-element.35), channel_id=1, replica_groups=mesh['y'=4,'z'=8,'x'=4,'core'=2] {'x','core'}, dimensions={0} | all-to-all | bytes 589824 | tf_op jit(solution)/shard_map/all_to_all | solution.py:381
  43.9 0.6 shard_map.91
  44.5 0.0 copy-start.3
  44.5 15.2 %all_to_all.21.got = f32[32,8,128]{2,1,0:T(8,128)S(1)} all-to-all(f32[32,8,128]{2,1,0:T(8,128)S(1)} %shard_map.91), channel_id=1, replica_groups=mesh['y'=4,'z'=8,'x'=4,'core'=2] {'y','z'}, dimensions={0} | all-to-all | bytes 262144 | tf_op jit(solution)/shard_map/all_to_all | solution.py:388
  59.7 0.0 copy-done.3
  59.7 0.5 shard_map.92
  60.3 11.6 %all_to_all.22.got = f32[8,8,1152]{2,1,0:T(8,128)S(1)} all-to-all(f32[8,8,1152]{2,1,0:T(8,128)S(1)} %get-tuple-element.39), channel_id=1, replica_groups=mesh['y'=4,'z'=8,'x'=4,'core'=2] {'x','core'}, dimensions={0} | all-to-all | bytes 589824 | tf_op jit(solution)/shard_map/all_to_all | solution.py:395
  71.8 0.7 %shard_map.93 = (f32[16,4096]{1,0:T(8,128)}, f32[1,16]{1,0:T(1,128)}) custom-call(f32[8,8,1152]{2,1,0:T(8,128)S(1)} %all_to_all.22.got, f32[8,128]{1,0:T(8,128)S(1)} %get-tuple-element.40.side, f32[8,128]{1,0:T(8,128)S(1)} %get-tuple-element.41.place), custom_call_target="tpu_custom_call" | custom-call | tf_op jit(solution)/shard_map/pallas_call | solution.py:396
  (1 shorter events, 0.0 us)
Async XLA Ops:
  0.6 10.0 %copy-start.1 = (f32[31,4096]{1,0:T(8,128)S(1)}, f32[31,4096]{1,0:T(8,128)}, u32[]{:S(2)}) copy-start(f32[31,4096]{1,0:T(8,128)} %weights.7) | copy-start | bytes 1523716
  0.6 10.0 %copy-start.2 = (f32[16,4096]{1,0:T(8,128)S(1)}, f32[16,4096]{1,0:T(8,128)}, u32[]{:S(2)}) copy-start(f32[16,4096]{1,0:T(8,128)} %src.5) | copy-start | bytes 786436
  1.7 12.6 %collective-permute-start = (f32[16,1024]{1,0:T(8,128)S(1)}, f32[16,1024]{1,0:T(8,128)S(1)}, u32[]{:S(2)}, u32[]{:S(2)}) collective-permute-start(f32[16,1024]{1,0:T(8,128)S(1)} %get-tuple-element.23), channel_id=1, source_target_pairs={{0,248},{8,16},{16,8},{24,32},{32,24},{40,48},{48,40},{56,64},{64,... | collective-permute-start | bytes 196616 | tf_op jit(solution)/shard_map/ppermute | solution.py:343
  10.6 3.7 %collective-permute-start.1 = (f32[16,1024]{1,0:T(8,128)S(1)}, f32[16,1024]{1,0:T(8,128)S(1)}, u32[]{:S(2)}, u32[]{:S(2)}) collective-permute-start(f32[16,1024]{1,0:T(8,128)S(1)} %get-tuple-element.24), channel_id=1, source_target_pairs={{0,8},{8,0},{16,24},{24,16},{32,40},{40,32},{48,56},{56,48},{64,72... | collective-permute-start | bytes 196616 | tf_op jit(solution)/shard_map/ppermute | solution.py:343
  12.6 10.2 %collective-permute-start.2 = (f32[32,1664]{1,0:T(8,128)S(1)}, f32[32,1664]{1,0:T(8,128)S(1)}, u32[]{:S(2)}, u32[]{:S(2)}) collective-permute-start(f32[32,1664]{1,0:T(8,128)S(1)} %get-tuple-element.32), channel_id=1, source_target_pairs={{0,248},{8,16},{16,8},{24,32},{32,24},{40,48},{48,40},{56,64},{64,... | collective-permute-start | bytes 638984 | tf_op jit(solution)/shard_map/ppermute | solution.py:352
  14.2 8.7 %collective-permute-start.3 = (f32[32,1664]{1,0:T(8,128)S(1)}, f32[32,1664]{1,0:T(8,128)S(1)}, u32[]{:S(2)}, u32[]{:S(2)}) collective-permute-start(f32[32,1664]{1,0:T(8,128)S(1)} %get-tuple-element.33), channel_id=1, source_target_pairs={{0,8},{8,0},{16,24},{24,16},{32,40},{40,32},{48,56},{56,48},{64,72... | collective-permute-start | bytes 638984 | tf_op jit(solution)/shard_map/ppermute | solution.py:352
  17.0 15.4 %all-to-all-start = ((f32[8,32,512]{2,1,0:T(8,128)}), f32[8,32,512]{2,1,0:T(8,128)S(1)}, u32[]{:S(2)}, u32[]{:S(2)}) async-start(f32[8,32,512]{2,1,0:T(8,128)} %get-tuple-element.29), calls=%async_computation | async-start | bytes 1048576 | tf_op jit(solution)/shard_map/all_to_all | solution.py:360
  22.9 9.5 %copy-start = (f32[128,128]{1,0:T(8,128)S(1)}, f32[128,128]{1,0:T(8,128)}, u32[]{:S(2)}) copy-start(f32[128,128]{1,0:T(8,128)} %to_modes.5) | copy-start | bytes 196612
  44.5 15.2 %copy-start.3 = (f32[128,128]{1,0:T(8,128)S(1)}, f32[128,128]{1,0:T(8,128)}, u32[]{:S(2)}) copy-start(f32[128,128]{1,0:T(8,128)} %from_modes.1) | copy-start | bytes 196612

commit v11 on v10

--- a/solution.py
+++ b/solution.py
@@ -137,8 +137,9 @@
         )
 
 
-def edge_kernel(src, near_0, near_1, weights, diag, inner, nb_in, out, x0, x1, nb, sems):
-    copies = start_all(sems, [(nb_in, nb)])
+def edge_kernel(src, near_0, near_1, weights, diag, inner, nb_in, out, x0, x1, nb, buffer, sems):
+    offsets = pltpu.make_async_copy(nb_in, nb, sems.at[PARTS])
+    offsets.start()
     for k, near in enumerate((near_0, near_1)):
         base = jnp.where(rightward(k), HALO + BLOCKS, 0)
         for j in range(HALO):
@@ -146,12 +147,16 @@
     for j in range(BLOCKS):
         x0[HALO + j] = src[:, j * LANES : (j + 1) * LANES]
     for r in range(PARTS):
-        out[r, 0:SLAB, :] = src[:, r * PART : (r + 1) * PART]
+        buffer[r, 0:SLAB, :] = src[:, r * PART : (r + 1) * PART]
     for j in range(HALO, BLOCKS - HALO):
         x1[j] = inner[j - HALO]
         part, place = divmod(j, PART // LANES)
-        out[part, SLAB:, place * LANES : (place + 1) * LANES] = inner[j - HALO]
-    wait_all(copies)
+        buffer[part, SLAB:, place * LANES : (place + 1) * LANES] = inner[j - HALO]
+    parts = [pltpu.make_async_copy(buffer.at[r], out.at[r], sems.at[r]) for r in range(PARTS)]
+    per_part = PART // LANES
+    for r in range(HALO // per_part, (BLOCKS - HALO) // per_part):
+        parts[r].start()
+    offsets.wait()
 
     for b in (*range(HALO), *range(BLOCKS - HALO, BLOCKS)):
         value = apply(
@@ -162,8 +167,11 @@
             lambda s: nb[s, b],
         )
         x1[b] = value
-        part, place = divmod(b, PART // LANES)
-        out[part, SLAB:, place * LANES : (place + 1) * LANES] = value
+        part, place = divmod(b, per_part)
+        buffer[part, SLAB:, place * LANES : (place + 1) * LANES] = value
+        if place == per_part - 1:
+            parts[part].start()
+    wait_all(parts)
 
 
 def outer_kernel(x0_near, x1_own, far_0, far_1, weights, diag, nb_in, out, x0, x1, nbv, nbs, nb, sems):
@@ -253,12 +261,13 @@
     again = mm(to_modes[...], s[...]) + partial[...]
     m0, i0 = modal[...], image[...]
     g = jnp.sum(z2[:, :, FLAT:], axis=0) + sums(((m0, again), (i0, again), (again, again)), 3)
-    out[...] = jnp.broadcast_to(g[None], out.shape)
+    row = jnp.concatenate([g[k : k + 1, :] for k in range(6)], axis=1)
+    out[...] = jnp.broadcast_to(row[None], out.shape)
 
 
 def finish_kernel(got, z01, to_modes, from_modes, own, out, side, s):
     g = jnp.sum(got[...], axis=0)
-    mm_, mi, ii, mj, ij, jj = (g[k : k + 1, :] for k in range(6))
+    mm_, mi, ii, mj, ij, jj = (g[:, k * LANES : (k + 1) * LANES] for k in range(6))
     e = own[0:1, :]
     scale = mm_ + 1e-06
     upper = 1.5 * jnp.sqrt(ii / scale)
@@ -354,7 +363,12 @@
         edge_kernel,
         (f32(PARTS, 2 * SLAB, PART), f32(EXT1, SLAB, LANES), f32(BLOCKS, SLAB, LANES)),
         [VMEM] * 7,
-        [smem_offsets, pltpu.SemaphoreType.DMA((1,))],
+        [
+            smem_offsets,
+            pltpu.VMEM((PARTS, 2 * SLAB, PART), jnp.float32),
+            pltpu.SemaphoreType.DMA((PARTS + 1,)),
+        ],
+        out_specs=(HBM, VMEM, VMEM),
         cost=COST_1,
     )(source, near_0, near_1, weights, diag, inner, nb)
     z01 = lax.all_to_all(first, RAD, 0, 0, tiled=True)
@@ -381,7 +395,7 @@
     z2 = lax.all_to_all(sent, RAD, 0, 0, tiled=True)
     g = call(
         again_kernel,
-        f32(lat, 8, LANES),
+        f32(lat, 1, 6 * LANES),
         [VMEM] * 5,
         [pltpu.VMEM((MODES, PART), jnp.float32)],
     )(z2, modal, image, partial, to_modes)

time: 72.9 us -> 72.6 us (level)
  no operation moved by 1% of the time
where the time goes in v11:
time: 72.6 us; the launch traced here: 72.3 us
  blocking collectives  37.2 us (51%)
  starting transfers between devices  16.5 us (23%)
  Pallas kernels  13.3 us (18%)
  waiting for transfers between devices  4.64 us (6%)
  between operations  0.73 us (1%)
    all_to_all x1, blocking collectives, on_device(): g = lax.all_to_all(g, LAT, 0, 0, tiled=True)  15 us
    all_to_all x1, blocking collectives, on_device(): got = lax.all_to_all(mixed, RAD, 0, 0, tiled=True)  11.7 us
    all_to_all x1, blocking collectives, on_device(): z2 = lax.all_to_all(sent, RAD, 0, 0, tiled=True)  10.6 us
    ppermute x1, starting transfers between devices, on_device(): lax.ppermute(near_0, LAT, swaps[0])  8.94 us
    all_to_all x1, starting transfers between devices, on_device(): z01 = lax.all_to_all(first, RAD, 0, 0, tiled=True)  5.88 us
    pallas_call x1, Pallas kernels, on_device(): call(outer_kernel, f32(PARTS, 8, FLAT), [VMEM] * 7, [pltpu.VMEM((EXT2, SL...  4.82 us
    all_to_all x1, waiting for transfers between devices, on_device(): z01 = lax.all_to_all(first, RAD, 0, 0, tiled=True)  4.63 us
    pallas_call x1, Pallas kernels, on_device(): call(edge_kernel, (f32(PARTS, 2 * SLAB, PART), f32(EXT1, SLAB, LANES), f3...  2.59 us
  transfers between devices with their start and end apart: 5, of which 1 were waited for; matrix products, arithmetic and copies ran while one was open for 0% of the time, Pallas kernels for 13%

profile of v11, /device:TPU:1, one launch (start us, length us, event | category | flops | bytes accessed | tf_op | source)
XLA Modules:
  0.0 72.3 jit_solution(16760458360423371215)
XLA Ops:
  0.6 0.0 copy-start.1
  0.6 0.0 copy-start.2
  0.7 1.0 %shard_map.86 = (f32[16,1024]{1,0:T(8,128)S(1)}, f32[16,1024]{1,0:T(8,128)S(1)}, f32[8,128]{1,0:T(8,128)S(1)}, s32[31,32]{1,0:T(8,128)S(1)}, f32[1,4096]{1,0:T(1,128)S(1)}) custom-call(f32[16,4096]{1,0:T(8,128)} %src.5, f32[31,4096]{1,0:T(8,128)} %weights.7, f32[1,4096]{1,0:T(1,128)} %bitcast.3, s32[31,32]{1,0:T(8,128)} %neighbors.1, f32[1,128]{1,0:T(1,128)} %bitcast.4), custom_call_target="tpu_custom_call" | custom-call | tf_op jit(solution)/shard_map/pallas_call | solution.py:342
  1.7 8.9 %collective-permute-start = (f32[16,1024]{1,0:T(8,128)S(1)}, f32[16,1024]{1,0:T(8,128)S(1)}, u32[]{:S(2)}, u32[]{:S(2)}) collective-permute-start(f32[16,1024]{1,0:T(8,128)S(1)} %get-tuple-element.23), channel_id=1, source_target_pairs={{0,248},{8,16},{16,8},{24,32},{32,24},{40,48},{48,40},{56,64},{64,... | collective-permute-start | bytes 196616 | tf_op jit(solution)/shard_map/ppermute | solution.py:352
  10.6 0.0 collective-permute-start.1
  10.6 0.0 copy-done.1
  10.6 0.0 copy-done.2
  10.7 2.0 %shard_map.87 = (f32[16,16,128]{2,1,0:T(8,128)S(1)}, f32[32,1,128]{2,1,0:T(1,128)S(1)}, f32[8,128]{1,0:T(8,128)S(1)}, f32[32,1664]{1,0:T(8,128)S(1)}, f32[32,1664]{1,0:T(8,128)S(1)}) custom-call(f32[16,4096]{1,0:T(8,128)S(1)} %copy-done.2, f32[31,4096]{1,0:T(8,128)S(1)} %copy-done.1, f32[1,4096]{1,0:T(1,128)S(1)} %get-tuple-element.25.shifts, ...), custom_call_target="tpu_custom_call" | custom-call | flops 3000000000 | tf_op jit(solution)/shard_map/pallas_call | solution.py:354
  12.6 1.5 %collective-permute-start.2 = (f32[32,1664]{1,0:T(8,128)S(1)}, f32[32,1664]{1,0:T(8,128)S(1)}, u32[]{:S(2)}, u32[]{:S(2)}) collective-permute-start(f32[32,1664]{1,0:T(8,128)S(1)} %get-tuple-element.32), channel_id=1, source_target_pairs={{0,248},{8,16},{16,8},{24,32},{32,24},{40,48},{48,40},{56,64},{64,... | collective-permute-start | bytes 638984 | tf_op jit(solution)/shard_map/ppermute | solution.py:361
  14.2 0.1 collective-permute-start.3
  14.3 0.0 collective-permute-done.near_0
  14.3 0.0 collective-permute-done.1.near_1
  14.3 2.6 %shard_map.88 = (f32[8,32,512]{2,1,0:T(8,128)}, f32[48,16,128]{2,1,0:T(8,128)S(1)}, f32[32,16,128]{2,1,0:T(8,128)S(1)}) custom-call(f32[16,4096]{1,0:T(8,128)S(1)} %copy-done.2, f32[16,1024]{1,0:T(8,128)S(1)} %collective-permute-done.near_0, f32[16,1024]{1,0:T(8,128)S(1)} %collective-permute-done.1.near_1, f32[31,4096]{1,0:T(8,128)S(1)} %copy-done.1, ...), custom_call_target="tpu_custom_call" | custom-call | flops 3000000000 | tf_op jit(solution)/shard_map/pallas_call | solution.py:362
  16.9 5.9 %all-to-all-start = ((f32[8,32,512]{2,1,0:T(8,128)}), f32[8,32,512]{2,1,0:T(8,128)S(1)}, u32[]{:S(2)}, u32[]{:S(2)}) async-start(f32[8,32,512]{2,1,0:T(8,128)} %get-tuple-element.29), calls=%async_computation | async-start | bytes 1048576 | tf_op jit(solution)/shard_map/all_to_all | solution.py:374
  22.8 0.0 collective-permute-done.2.far_0
  22.8 0.0 collective-permute-done.3.far_1
  22.8 0.0 copy-start
  22.8 4.8 %shard_map.89.second = f32[8,8,1024]{2,1,0:T(8,128)S(1)} custom-call(f32[48,16,128]{2,1,0:T(8,128)S(1)} %get-tuple-element.30.x0_near, f32[32,16,128]{2,1,0:T(8,128)S(1)} %get-tuple-element.31.x1_own, f32[32,1664]{1,0:T(8,128)S(1)} %collective-permute-done.2.far_0, f32[32,1664]{1,0:T(8,128)S(1)} %collective-permute-done.3.far_1, f32[31,4096]{1,0:T(8,128)S(1)} %copy-done.1, ...), custom_call_target="tpu_custom_call" | custom-call | flops 10000000000 | tf_op jit(solution)/shard_map/pallas_call | solution.py:375
  27.6 4.6 %all-to-all-done.z01 = f32[8,32,512]{2,1,0:T(8,128)S(1)} async-done(((f32[8,32,512]{2,1,0:T(8,128)}), f32[8,32,512]{2,1,0:T(8,128)S(1)}, u32[]{:S(2)}, u32[]{:S(2)}) %all-to-all-start) | async-done | bytes 524320 | tf_op jit(solution)/shard_map/all_to_all | solution.py:374
  32.2 0.0 copy-done
  32.2 1.0 %shard_map.90 = (f32[8,8,1152]{2,1,0:T(8,128)S(1)}, f32[128,512]{1,0:T(8,128)S(1)}, f32[128,512]{1,0:T(8,128)S(1)}, f32[128,512]{1,0:T(8,128)S(1)}) custom-call(f32[8,32,512]{2,1,0:T(8,128)S(1)} %all-to-all-done.z01, f32[8,8,1024]{2,1,0:T(8,128)S(1)} %shard_map.89.second, f32[128,128]{1,0:T(8,128)S(1)} %copy-done, f32[8,128]{1,0:T(8,128)S(1)} %get-tuple-element.34.own), custom_call_target="tpu_custom_call" | custom-call | tf_op jit(solution)/shard_map/pallas_call | solution.py:389
  33.2 10.6 %all_to_all.20.z2 = f32[8,8,1152]{2,1,0:T(8,128)S(1)} all-to-all(f32[8,8,1152]{2,1,0:T(8,128)S(1)} %get-tuple-element.35), channel_id=1, replica_groups=mesh['y'=4,'z'=8,'x'=4,'core'=2] {'x','core'}, dimensions={0} | all-to-all | bytes 589824 | tf_op jit(solution)/shard_map/all_to_all | solution.py:395
  43.8 0.6 shard_map.91
  44.4 0.0 copy-start.3
  44.4 15.0 %all_to_all.21.got = f32[32,1,768]{2,1,0:T(1,128)S(1)} all-to-all(f32[32,1,768]{2,1,0:T(1,128)S(1)} %shard_map.91), channel_id=1, replica_groups=mesh['y'=4,'z'=8,'x'=4,'core'=2] {'y','z'}, dimensions={0} | all-to-all | bytes 196608 | tf_op jit(solution)/shard_map/all_to_all | solution.py:402
  59.4 0.0 copy-done.3
  59.4 0.5 shard_map.92
  59.9 11.7 %all_to_all.22.got = f32[8,8,1152]{2,1,0:T(8,128)S(1)} all-to-all(f32[8,8,1152]{2,1,0:T(8,128)S(1)} %get-tuple-element.39), channel_id=1, replica_groups=mesh['y'=4,'z'=8,'x'=4,'core'=2] {'x','core'}, dimensions={0} | all-to-all | bytes 589824 | tf_op jit(solution)/shard_map/all_to_all | solution.py:409
  71.6 0.7 %shard_map.93 = (f32[16,4096]{1,0:T(8,128)}, f32[1,16]{1,0:T(1,128)}) custom-call(f32[8,8,1152]{2,1,0:T(8,128)S(1)} %all_to_all.22.got, f32[8,128]{1,0:T(8,128)S(1)} %get-tuple-element.40.side, f32[8,128]{1,0:T(8,128)S(1)} %get-tuple-element.41.place), custom_call_target="tpu_custom_call" | custom-call | tf_op jit(solution)/shard_map/pallas_call | solution.py:410
  (1 shorter events, 0.0 us)
Async XLA Ops:
  0.6 10.0 %copy-start.1 = (f32[31,4096]{1,0:T(8,128)S(1)}, f32[31,4096]{1,0:T(8,128)}, u32[]{:S(2)}) copy-start(f32[31,4096]{1,0:T(8,128)} %weights.7) | copy-start | bytes 1523716
  0.6 10.0 %copy-start.2 = (f32[16,4096]{1,0:T(8,128)S(1)}, f32[16,4096]{1,0:T(8,128)}, u32[]{:S(2)}) copy-start(f32[16,4096]{1,0:T(8,128)} %src.5) | copy-start | bytes 786436
  1.7 12.6 %collective-permute-start = (f32[16,1024]{1,0:T(8,128)S(1)}, f32[16,1024]{1,0:T(8,128)S(1)}, u32[]{:S(2)}, u32[]{:S(2)}) collective-permute-start(f32[16,1024]{1,0:T(8,128)S(1)} %get-tuple-element.23), channel_id=1, source_target_pairs={{0,248},{8,16},{16,8},{24,32},{32,24},{40,48},{48,40},{56,64},{64,... | collective-permute-start | bytes 196616 | tf_op jit(solution)/shard_map/ppermute | solution.py:352
  10.6 3.7 %collective-permute-start.1 = (f32[16,1024]{1,0:T(8,128)S(1)}, f32[16,1024]{1,0:T(8,128)S(1)}, u32[]{:S(2)}, u32[]{:S(2)}) collective-permute-start(f32[16,1024]{1,0:T(8,128)S(1)} %get-tuple-element.24), channel_id=1, source_target_pairs={{0,8},{8,0},{16,24},{24,16},{32,40},{40,32},{48,56},{56,48},{64,72... | collective-permute-start | bytes 196616 | tf_op jit(solution)/shard_map/ppermute | solution.py:352
  12.6 10.1 %collective-permute-start.2 = (f32[32,1664]{1,0:T(8,128)S(1)}, f32[32,1664]{1,0:T(8,128)S(1)}, u32[]{:S(2)}, u32[]{:S(2)}) collective-permute-start(f32[32,1664]{1,0:T(8,128)S(1)} %get-tuple-element.32), channel_id=1, source_target_pairs={{0,248},{8,16},{16,8},{24,32},{32,24},{40,48},{48,40},{56,64},{64,... | collective-permute-start | bytes 638984 | tf_op jit(solution)/shard_map/ppermute | solution.py:361
  14.2 8.6 %collective-permute-start.3 = (f32[32,1664]{1,0:T(8,128)S(1)}, f32[32,1664]{1,0:T(8,128)S(1)}, u32[]{:S(2)}, u32[]{:S(2)}) collective-permute-start(f32[32,1664]{1,0:T(8,128)S(1)} %get-tuple-element.33), channel_id=1, source_target_pairs={{0,8},{8,0},{16,24},{24,16},{32,40},{40,32},{48,56},{56,48},{64,72... | collective-permute-start | bytes 638984 | tf_op jit(solution)/shard_map/ppermute | solution.py:361
  16.9 15.4 %all-to-all-start = ((f32[8,32,512]{2,1,0:T(8,128)}), f32[8,32,512]{2,1,0:T(8,128)S(1)}, u32[]{:S(2)}, u32[]{:S(2)}) async-start(f32[8,32,512]{2,1,0:T(8,128)} %get-tuple-element.29), calls=%async_computation | async-start | bytes 1048576 | tf_op jit(solution)/shard_map/all_to_all | solution.py:374
  22.8 9.5 %copy-start = (f32[128,128]{1,0:T(8,128)S(1)}, f32[128,128]{1,0:T(8,128)}, u32[]{:S(2)}) copy-start(f32[128,128]{1,0:T(8,128)} %to_modes.5) | copy-start | bytes 196612
  44.4 15.0 %copy-start.3 = (f32[128,128]{1,0:T(8,128)S(1)}, f32[128,128]{1,0:T(8,128)}, u32[]{:S(2)}) copy-start(f32[128,128]{1,0:T(8,128)} %from_modes.1) | copy-start | bytes 196612

commit v12 on v11

--- a/solution.py
+++ b/solution.py
@@ -219,6 +219,21 @@
     lax.fori_loop(0, BLOCKS // UNROLL, step, 0)
 
 
+def tile(t):
+    return slice(8 * (t // 3), 8 * (t // 3) + 8), slice(LANES * (t % 3), LANES * (t % 3) + LANES)
+
+
+def tiles(r):
+    per_half = PART // LANES
+    for t in range(SLAB // 8 * per_half):
+        half, j = divmod(t, per_half)
+        row = r * SLAB + half * 8
+        yield t, slice(row, row + 8), slice(j * LANES, (j + 1) * LANES)
+
+
+RIDE = slice(16, 24), slice(2 * LANES, 3 * LANES)
+
+
 def sums(pairs, first):
     folded = []
     for a, b in pairs:
@@ -249,18 +264,18 @@
     partial[...] = e * (m1 + i0)
     g = sums(((m0, m0), (m0, i0), (i0, i0)), 0)
     for r in range(PARTS):
-        out[r, :, 0:FLAT] = second[r]
-        out[r, :, FLAT:] = g
+        for t, _, _ in tiles(r):
+            out[(r, *tile(t))] = second[r, :, t * LANES : (t + 1) * LANES]
+        out[(r, *RIDE)] = g
 
 
 def again_kernel(z2, modal, image, partial, to_modes, out, s):
     for r in range(PARTS):
-        for half in range(SLAB // 8):
-            row = r * SLAB + half * 8
-            s[row : row + 8, :] = z2[r, :, half * PART : (half + 1) * PART]
+        for t, rows, cols in tiles(r):
+            s[rows, cols] = z2[(r, *tile(t))]
     again = mm(to_modes[...], s[...]) + partial[...]
     m0, i0 = modal[...], image[...]
-    g = jnp.sum(z2[:, :, FLAT:], axis=0) + sums(((m0, again), (i0, again), (again, again)), 3)
+    g = sum(z2[(r, *RIDE)] for r in range(PARTS)) + sums(((m0, again), (i0, again), (again, again)), 3)
     row = jnp.concatenate([g[k : k + 1, :] for k in range(6)], axis=1)
     out[...] = jnp.broadcast_to(row[None], out.shape)
 
@@ -294,18 +309,16 @@
     mix = jnp.concatenate([mm(from_m * (over + u0 + u1 * e), to_m), mm(from_m * u1, to_m)], axis=1)
     value = mm(mix, s[...])
     for r in range(PARTS):
-        for half in range(SLAB // 8):
-            row = r * SLAB + half * 8
-            out[r, :, half * PART : (half + 1) * PART] = value[row : row + 8, :]
-        out[r, :, FLAT:] = ours
+        for t, rows, cols in tiles(r):
+            out[(r, *tile(t))] = value[rows, cols]
+        out[(r, *RIDE)] = ours
 
 
 def unpack_kernel(got, side, place, out, mine):
     for r in range(PARTS):
-        for half in range(SLAB // 8):
-            rows = slice(half * 8, half * 8 + 8)
-            out[rows, r * PART : (r + 1) * PART] = got[r, :, half * PART : (half + 1) * PART]
-    squares = side[0:1, :] + sum(got[r, 0:1, FLAT:] for r in range(PARTS))
+        for t, rows, cols in tiles(0):
+            out[rows, r * PART + cols.start : r * PART + cols.stop] = got[(r, *tile(t))]
+    squares = side[0:1, :] + sum(got[r, 16:17, RIDE[1]] for r in range(PARTS))
     norm = jnp.sqrt(jnp.maximum(squares, 0.0) / side[1:2, :])
     here = place[0:1, 0:SLAB]
     picked = norm[:, 0:SLAB]
@@ -388,7 +401,7 @@
     )(x0, x1, far_0, far_1, weights, diag, nb)
     sent, modal, image, partial = call(
         gram_kernel,
-        (f32(PARTS, 8, FLAT + LANES),) + (f32(MODES, PART),) * 3,
+        (f32(PARTS, 24, 3 * LANES),) + (f32(MODES, PART),) * 3,
         [VMEM] * 4,
         [pltpu.VMEM((MODES, 2 * PART), jnp.float32)],
     )(z01, second, to_modes, own)
@@ -402,7 +415,7 @@
     g = lax.all_to_all(g, LAT, 0, 0, tiled=True)
     mixed, side = call(
         finish_kernel,
-        (f32(PARTS, 8, FLAT + LANES), f32(8, LANES)),
+        (f32(PARTS, 24, 3 * LANES), f32(8, LANES)),
         [VMEM] * 5,
         [pltpu.VMEM((2 * MODES, PART), jnp.float32)],
     )(g, z01, to_modes, from_modes, own)

time: 72.6 us -> 72.6 us (level)
  no operation moved by 1% of the time
where the time goes in v12:
time: 72.6 us; the launch traced here: 72.3 us
  blocking collectives  37.2 us (51%)
  starting transfers between devices  16.5 us (23%)
  Pallas kernels  13.3 us (18%)
  waiting for transfers between devices  4.63 us (6%)
  between operations  0.73 us (1%)
    all_to_all x1, blocking collectives, on_device(): g = lax.all_to_all(g, LAT, 0, 0, tiled=True)  15 us
    all_to_all x1, blocking collectives, on_device(): got = lax.all_to_all(mixed, RAD, 0, 0, tiled=True)  11.7 us
    all_to_all x1, blocking collectives, on_device(): z2 = lax.all_to_all(sent, RAD, 0, 0, tiled=True)  10.6 us
    ppermute x1, starting transfers between devices, on_device(): lax.ppermute(near_0, LAT, swaps[0])  8.94 us
    all_to_all x1, starting transfers between devices, on_device(): z01 = lax.all_to_all(first, RAD, 0, 0, tiled=True)  5.88 us
    pallas_call x1, Pallas kernels, on_device(): call(outer_kernel, f32(PARTS, 8, FLAT), [VMEM] * 7, [pltpu.VMEM((EXT2, SL...  4.83 us
    all_to_all x1, waiting for transfers between devices, on_device(): z01 = lax.all_to_all(first, RAD, 0, 0, tiled=True)  4.62 us
    pallas_call x1, Pallas kernels, on_device(): call(edge_kernel, (f32(PARTS, 2 * SLAB, PART), f32(EXT1, SLAB, LANES), f3...  2.59 us
  transfers between devices with their start and end apart: 5, of which 1 were waited for; matrix products, arithmetic and copies ran while one was open for 0% of the time, Pallas kernels for 13%

profile of v12, /device:TPU:1, one launch (start us, length us, event | category | flops | bytes accessed | tf_op | source)
XLA Modules:
  0.0 72.3 jit_solution(3732476965757359485)
XLA Ops:
  0.6 0.0 copy-start.1
  0.6 0.0 copy-start.2
  0.7 1.0 %shard_map.86 = (f32[16,1024]{1,0:T(8,128)S(1)}, f32[16,1024]{1,0:T(8,128)S(1)}, f32[8,128]{1,0:T(8,128)S(1)}, s32[31,32]{1,0:T(8,128)S(1)}, f32[1,4096]{1,0:T(1,128)S(1)}) custom-call(f32[16,4096]{1,0:T(8,128)} %src.5, f32[31,4096]{1,0:T(8,128)} %weights.7, f32[1,4096]{1,0:T(1,128)} %bitcast.3, s32[31,32]{1,0:T(8,128)} %neighbors.1, f32[1,128]{1,0:T(1,128)} %bitcast.4), custom_call_target="tpu_custom_call" | custom-call | tf_op jit(solution)/shard_map/pallas_call | solution.py:355
  1.7 8.9 %collective-permute-start = (f32[16,1024]{1,0:T(8,128)S(1)}, f32[16,1024]{1,0:T(8,128)S(1)}, u32[]{:S(2)}, u32[]{:S(2)}) collective-permute-start(f32[16,1024]{1,0:T(8,128)S(1)} %get-tuple-element.23), channel_id=1, source_target_pairs={{0,248},{8,16},{16,8},{24,32},{32,24},{40,48},{48,40},{56,64},{64,... | collective-permute-start | bytes 196616 | tf_op jit(solution)/shard_map/ppermute | solution.py:365
  10.6 0.0 collective-permute-start.1
  10.6 0.0 copy-done.1
  10.6 0.0 copy-done.2
  10.7 2.0 %shard_map.87 = (f32[16,16,128]{2,1,0:T(8,128)S(1)}, f32[32,1,128]{2,1,0:T(1,128)S(1)}, f32[8,128]{1,0:T(8,128)S(1)}, f32[32,1664]{1,0:T(8,128)S(1)}, f32[32,1664]{1,0:T(8,128)S(1)}) custom-call(f32[16,4096]{1,0:T(8,128)S(1)} %copy-done.2, f32[31,4096]{1,0:T(8,128)S(1)} %copy-done.1, f32[1,4096]{1,0:T(1,128)S(1)} %get-tuple-element.25.shifts, ...), custom_call_target="tpu_custom_call" | custom-call | flops 3000000000 | tf_op jit(solution)/shard_map/pallas_call | solution.py:367
  12.6 1.5 %collective-permute-start.2 = (f32[32,1664]{1,0:T(8,128)S(1)}, f32[32,1664]{1,0:T(8,128)S(1)}, u32[]{:S(2)}, u32[]{:S(2)}) collective-permute-start(f32[32,1664]{1,0:T(8,128)S(1)} %get-tuple-element.32), channel_id=1, source_target_pairs={{0,248},{8,16},{16,8},{24,32},{32,24},{40,48},{48,40},{56,64},{64,... | collective-permute-start | bytes 638984 | tf_op jit(solution)/shard_map/ppermute | solution.py:374
  14.2 0.1 collective-permute-start.3
  14.3 0.0 collective-permute-done.near_0
  14.3 0.0 collective-permute-done.1.near_1
  14.3 2.6 %shard_map.88 = (f32[8,32,512]{2,1,0:T(8,128)}, f32[48,16,128]{2,1,0:T(8,128)S(1)}, f32[32,16,128]{2,1,0:T(8,128)S(1)}) custom-call(f32[16,4096]{1,0:T(8,128)S(1)} %copy-done.2, f32[16,1024]{1,0:T(8,128)S(1)} %collective-permute-done.near_0, f32[16,1024]{1,0:T(8,128)S(1)} %collective-permute-done.1.near_1, f32[31,4096]{1,0:T(8,128)S(1)} %copy-done.1, ...), custom_call_target="tpu_custom_call" | custom-call | flops 3000000000 | tf_op jit(solution)/shard_map/pallas_call | solution.py:375
  16.9 5.9 %all-to-all-start = ((f32[8,32,512]{2,1,0:T(8,128)}), f32[8,32,512]{2,1,0:T(8,128)S(1)}, u32[]{:S(2)}, u32[]{:S(2)}) async-start(f32[8,32,512]{2,1,0:T(8,128)} %get-tuple-element.29), calls=%async_computation | async-start | bytes 1048576 | tf_op jit(solution)/shard_map/all_to_all | solution.py:387
  22.8 0.0 collective-permute-done.2.far_0
  22.8 0.0 collective-permute-done.3.far_1
  22.8 0.0 copy-start
  22.8 4.8 %shard_map.89.second = f32[8,8,1024]{2,1,0:T(8,128)S(1)} custom-call(f32[48,16,128]{2,1,0:T(8,128)S(1)} %get-tuple-element.30.x0_near, f32[32,16,128]{2,1,0:T(8,128)S(1)} %get-tuple-element.31.x1_own, f32[32,1664]{1,0:T(8,128)S(1)} %collective-permute-done.2.far_0, f32[32,1664]{1,0:T(8,128)S(1)} %collective-permute-done.3.far_1, f32[31,4096]{1,0:T(8,128)S(1)} %copy-done.1, ...), custom_call_target="tpu_custom_call" | custom-call | flops 10000000000 | tf_op jit(solution)/shard_map/pallas_call | solution.py:388
  27.6 4.6 %all-to-all-done.z01 = f32[8,32,512]{2,1,0:T(8,128)S(1)} async-done(((f32[8,32,512]{2,1,0:T(8,128)}), f32[8,32,512]{2,1,0:T(8,128)S(1)}, u32[]{:S(2)}, u32[]{:S(2)}) %all-to-all-start) | async-done | bytes 524320 | tf_op jit(solution)/shard_map/all_to_all | solution.py:387
  32.2 0.0 copy-done
  32.2 1.0 %shard_map.90 = (f32[8,24,384]{2,1,0:T(8,128)S(1)}, f32[128,512]{1,0:T(8,128)S(1)}, f32[128,512]{1,0:T(8,128)S(1)}, f32[128,512]{1,0:T(8,128)S(1)}) custom-call(f32[8,32,512]{2,1,0:T(8,128)S(1)} %all-to-all-done.z01, f32[8,8,1024]{2,1,0:T(8,128)S(1)} %shard_map.89.second, f32[128,128]{1,0:T(8,128)S(1)} %copy-done, f32[8,128]{1,0:T(8,128)S(1)} %get-tuple-element.34.own), custom_call_target="tpu_custom_call" | custom-call | tf_op jit(solution)/shard_map/pallas_call | solution.py:402
  33.2 10.6 %all_to_all.20.z2 = f32[8,24,384]{2,1,0:T(8,128)S(1)} all-to-all(f32[8,24,384]{2,1,0:T(8,128)S(1)} %get-tuple-element.35), channel_id=1, replica_groups=mesh['y'=4,'z'=8,'x'=4,'core'=2] {'x','core'}, dimensions={0} | all-to-all | bytes 589824 | tf_op jit(solution)/shard_map/all_to_all | solution.py:408
  43.8 0.6 shard_map.91
  44.4 0.0 copy-start.3
  44.4 15.0 %all_to_all.21.got = f32[32,1,768]{2,1,0:T(1,128)S(1)} all-to-all(f32[32,1,768]{2,1,0:T(1,128)S(1)} %shard_map.91), channel_id=1, replica_groups=mesh['y'=4,'z'=8,'x'=4,'core'=2] {'y','z'}, dimensions={0} | all-to-all | bytes 196608 | tf_op jit(solution)/shard_map/all_to_all | solution.py:415
  59.4 0.0 copy-done.3
  59.4 0.5 shard_map.92
  59.9 11.7 %all_to_all.22.got = f32[8,24,384]{2,1,0:T(8,128)S(1)} all-to-all(f32[8,24,384]{2,1,0:T(8,128)S(1)} %get-tuple-element.39), channel_id=1, replica_groups=mesh['y'=4,'z'=8,'x'=4,'core'=2] {'x','core'}, dimensions={0} | all-to-all | bytes 589824 | tf_op jit(solution)/shard_map/all_to_all | solution.py:422
  71.6 0.7 %shard_map.93 = (f32[16,4096]{1,0:T(8,128)}, f32[1,16]{1,0:T(1,128)}) custom-call(f32[8,24,384]{2,1,0:T(8,128)S(1)} %all_to_all.22.got, f32[8,128]{1,0:T(8,128)S(1)} %get-tuple-element.40.side, f32[8,128]{1,0:T(8,128)S(1)} %get-tuple-element.41.place), custom_call_target="tpu_custom_call" | custom-call | tf_op jit(solution)/shard_map/pallas_call | solution.py:423
  (1 shorter events, 0.0 us)
Async XLA Ops:
  0.6 10.0 %copy-start.1 = (f32[31,4096]{1,0:T(8,128)S(1)}, f32[31,4096]{1,0:T(8,128)}, u32[]{:S(2)}) copy-start(f32[31,4096]{1,0:T(8,128)} %weights.7) | copy-start | bytes 1523716
  0.6 10.0 %copy-start.2 = (f32[16,4096]{1,0:T(8,128)S(1)}, f32[16,4096]{1,0:T(8,128)}, u32[]{:S(2)}) copy-start(f32[16,4096]{1,0:T(8,128)} %src.5) | copy-start | bytes 786436
  1.7 12.6 %collective-permute-start = (f32[16,1024]{1,0:T(8,128)S(1)}, f32[16,1024]{1,0:T(8,128)S(1)}, u32[]{:S(2)}, u32[]{:S(2)}) collective-permute-start(f32[16,1024]{1,0:T(8,128)S(1)} %get-tuple-element.23), channel_id=1, source_target_pairs={{0,248},{8,16},{16,8},{24,32},{32,24},{40,48},{48,40},{56,64},{64,... | collective-permute-start | bytes 196616 | tf_op jit(solution)/shard_map/ppermute | solution.py:365
  10.6 3.6 %collective-permute-start.1 = (f32[16,1024]{1,0:T(8,128)S(1)}, f32[16,1024]{1,0:T(8,128)S(1)}, u32[]{:S(2)}, u32[]{:S(2)}) collective-permute-start(f32[16,1024]{1,0:T(8,128)S(1)} %get-tuple-element.24), channel_id=1, source_target_pairs={{0,8},{8,0},{16,24},{24,16},{32,40},{40,32},{48,56},{56,48},{64,72... | collective-permute-start | bytes 196616 | tf_op jit(solution)/shard_map/ppermute | solution.py:365
  12.6 10.1 %collective-permute-start.2 = (f32[32,1664]{1,0:T(8,128)S(1)}, f32[32,1664]{1,0:T(8,128)S(1)}, u32[]{:S(2)}, u32[]{:S(2)}) collective-permute-start(f32[32,1664]{1,0:T(8,128)S(1)} %get-tuple-element.32), channel_id=1, source_target_pairs={{0,248},{8,16},{16,8},{24,32},{32,24},{40,48},{48,40},{56,64},{64,... | collective-permute-start | bytes 638984 | tf_op jit(solution)/shard_map/ppermute | solution.py:374
  14.2 8.6 %collective-permute-start.3 = (f32[32,1664]{1,0:T(8,128)S(1)}, f32[32,1664]{1,0:T(8,128)S(1)}, u32[]{:S(2)}, u32[]{:S(2)}) collective-permute-start(f32[32,1664]{1,0:T(8,128)S(1)} %get-tuple-element.33), channel_id=1, source_target_pairs={{0,8},{8,0},{16,24},{24,16},{32,40},{40,32},{48,56},{56,48},{64,72... | collective-permute-start | bytes 638984 | tf_op jit(solution)/shard_map/ppermute | solution.py:374
  16.9 15.4 %all-to-all-start = ((f32[8,32,512]{2,1,0:T(8,128)}), f32[8,32,512]{2,1,0:T(8,128)S(1)}, u32[]{:S(2)}, u32[]{:S(2)}) async-start(f32[8,32,512]{2,1,0:T(8,128)} %get-tuple-element.29), calls=%async_computation | async-start | bytes 1048576 | tf_op jit(solution)/shard_map/all_to_all | solution.py:387
  22.8 9.5 %copy-start = (f32[128,128]{1,0:T(8,128)S(1)}, f32[128,128]{1,0:T(8,128)}, u32[]{:S(2)}) copy-start(f32[128,128]{1,0:T(8,128)} %to_modes.5) | copy-start | bytes 196612
  44.4 15.0 %copy-start.3 = (f32[128,128]{1,0:T(8,128)S(1)}, f32[128,128]{1,0:T(8,128)}, u32[]{:S(2)}) copy-start(f32[128,128]{1,0:T(8,128)} %from_modes.1) | copy-start | bytes 196612

commit v13 on v12

--- a/solution.py
+++ b/solution.py
@@ -106,9 +106,54 @@
     return acc
 
 
-def inner_kernel(src, weights, shifts, nb_in, place_in, x1, diag, place, far_0, far_1, nb, sems):
+def inner_kernel(src, weights, shifts, nb_in, place_in, x1, diag, place, nb, sems):
     copies = start_all(sems, [(nb_in, nb)])
     place[...] = place_in[...]
+    for j in range(BLOCKS):
+        cols = slice(j * LANES, (j + 1) * LANES)
+        diag[j] = jnp.sum(weights[:, cols], axis=0, keepdims=True) + shifts[:, cols]
+    wait_all(copies)
+
+    for b in range(HALO, BLOCKS - HALO):
+        x1[b - HALO] = apply(
+            lambda c: src[:, column(0, c)],
+            b,
+            diag[b],
+            lambda s: weights[s : s + 1, column(0, b)],
+            lambda s: nb[s, b],
+        )
+
+
+def side(swap):
+    return jnp.where(rightward(swap), BLOCKS - HALO, 0)
+
+
+def extend(x0, src, nears):
+    for k, near in nears:
+        base = jnp.where(rightward(k), HALO + BLOCKS, 0)
+        for j in range(HALO):
+            x0[base + j] = near[:, j * LANES : (j + 1) * LANES]
+    for j in range(BLOCKS):
+        x0[HALO + j] = src[:, j * LANES : (j + 1) * LANES]
+
+
+def apply_side(swap, x0, diag, weights, nb, put):
+    for j in range(HALO):
+        b = side(swap) + j
+        put(
+            j,
+            apply(
+                lambda c: x0[c],
+                b + HALO,
+                diag[b],
+                lambda s: weights[s : s + 1, column(0, b)],
+                lambda s: nb[s, b],
+            ),
+        )
+
+
+def early_kernel(src, near_1, weights, shifts, diag, nb_in, done, far_0, far_1, x0, nb, sems):
+    copies = start_all(sems, [(nb_in, nb)])
     offsets = nb_in[...].astype(jnp.float32)
     for k, out in enumerate((far_0, far_1)):
         up = rightward(k)
@@ -122,55 +167,47 @@
         out[0:STENCIL, TAIL : TAIL + HALO] = jnp.where(
             up, offsets[:, BLOCKS - HALO :], offsets[:, :HALO]
         )
-    for j in range(BLOCKS):
-        cols = slice(j * LANES, (j + 1) * LANES)
-        diag[j] = jnp.sum(weights[:, cols], axis=0, keepdims=True) + shifts[:, cols]
+    extend(x0, src, ((1, near_1),))
     wait_all(copies)
 
-    for b in range(HALO, BLOCKS - HALO):
-        x1[b - HALO] = apply(
-            lambda c: src[:, column(0, c)],
-            b,
-            diag[b],
-            lambda s: weights[s : s + 1, column(0, b)],
-            lambda s: nb[s, b],
-        )
-
-
-def edge_kernel(src, near_0, near_1, weights, diag, inner, nb_in, out, x0, x1, nb, buffer, sems):
+    def put(j, value):
+        done[j] = value
+
+    apply_side(1, x0, diag, weights, nb, put)
+
+
+def edge_kernel(src, near_0, near_1, weights, diag, inner, early, nb_in, out, x0, x1, nb, buffer, sems):
     offsets = pltpu.make_async_copy(nb_in, nb, sems.at[PARTS])
     offsets.start()
-    for k, near in enumerate((near_0, near_1)):
-        base = jnp.where(rightward(k), HALO + BLOCKS, 0)
-        for j in range(HALO):
-            x0[base + j] = near[:, j * LANES : (j + 1) * LANES]
-    for j in range(BLOCKS):
-        x0[HALO + j] = src[:, j * LANES : (j + 1) * LANES]
+    extend(x0, src, ((0, near_0), (1, near_1)))
     for r in range(PARTS):
         buffer[r, 0:SLAB, :] = src[:, r * PART : (r + 1) * PART]
+    per_part = PART // LANES
     for j in range(HALO, BLOCKS - HALO):
         x1[j] = inner[j - HALO]
-        part, place = divmod(j, PART // LANES)
+        part, place = divmod(j, per_part)
         buffer[part, SLAB:, place * LANES : (place + 1) * LANES] = inner[j - HALO]
     parts = [pltpu.make_async_copy(buffer.at[r], out.at[r], sems.at[r]) for r in range(PARTS)]
-    per_part = PART // LANES
-    for r in range(HALO // per_part, (BLOCKS - HALO) // per_part):
+    inside = range(HALO // per_part, (BLOCKS - HALO) // per_part)
+    for r in inside:
         parts[r].start()
+
+    def put_at(swap):
+        def put(j, value):
+            x1[side(swap) + j] = value
+            part, place = divmod(j, per_part)
+            cols = slice(place * LANES, (place + 1) * LANES)
+            buffer[lax.div(side(swap), per_part) + part, SLAB:, cols] = value
+
+        return put
+
+    for j in range(HALO):
+        put_at(1)(j, early[j])
     offsets.wait()
-
-    for b in (*range(HALO), *range(BLOCKS - HALO, BLOCKS)):
-        value = apply(
-            lambda c: x0[c],
-            b + HALO,
-            diag[b],
-            lambda s: weights[s : s + 1, column(0, b)],
-            lambda s: nb[s, b],
-        )
-        x1[b] = value
-        part, place = divmod(b, per_part)
-        buffer[part, SLAB:, place * LANES : (place + 1) * LANES] = value
-        if place == per_part - 1:
-            parts[part].start()
+    apply_side(0, x0, diag, weights, nb, put_at(0))
+    for r in range(PARTS):
+        if r not in inside:
+            parts[r].start()
     wait_all(parts)
 
 
@@ -364,18 +401,29 @@
     ]
     near_0, near_1 = lax.ppermute(near_0, LAT, swaps[0]), lax.ppermute(near_1, LAT, swaps[1])
     smem_offsets = pltpu.SMEM((STENCIL, BLOCKS), jnp.int32)
-    inner, diag, place, far_0, far_1 = call(
+    inner, diag, place = call(
         inner_kernel,
-        (f32(BLOCKS - 2 * HALO, SLAB, LANES), f32(BLOCKS, 1, LANES), f32(8, LANES), fars, fars),
+        (f32(BLOCKS - 2 * HALO, SLAB, LANES), f32(BLOCKS, 1, LANES), f32(8, LANES)),
         [VMEM] * 5,
         [smem_offsets, pltpu.SemaphoreType.DMA((1,))],
         cost=COST_0,
     )(source, weights, shift_row, nb, place)
+    early, far_0, far_1 = call(
+        early_kernel,
+        (f32(HALO, SLAB, LANES), fars, fars),
+        [VMEM] * 6,
+        [
+            pltpu.VMEM((EXT1, SLAB, LANES), jnp.float32),
+            smem_offsets,
+            pltpu.SemaphoreType.DMA((1,)),
+        ],
+        cost=COST_0,
+    )(source, near_1, weights, shift_row, diag, nb)
     far_0, far_1 = lax.ppermute(far_0, LAT, swaps[0]), lax.ppermute(far_1, LAT, swaps[1])
     first, x0, x1 = call(
         edge_kernel,
         (f32(PARTS, 2 * SLAB, PART), f32(EXT1, SLAB, LANES), f32(BLOCKS, SLAB, LANES)),
-        [VMEM] * 7,
+        [VMEM] * 8,
         [
             smem_offsets,
             pltpu.VMEM((PARTS, 2 * SLAB, PART), jnp.float32),
@@ -383,7 +431,7 @@
         ],
         out_specs=(HBM, VMEM, VMEM),
         cost=COST_1,
-    )(source, near_0, near_1, weights, diag, inner, nb)
+    )(source, near_0, near_1, weights, diag, inner, early, nb)
     z01 = lax.all_to_all(first, RAD, 0, 0, tiled=True)
     second = call(
         outer_kernel,

time: 72.6 us -> 75.9 us (1.045)
  blocking collectives: 37.2 us -> 39.3 us
  waiting for transfers between devices: 4.63 us -> 5.81 us
  starting transfers between devices: 16.5 us -> 15.6 us
  Pallas kernels: 13.3 us -> 14.2 us
    all_to_all x1, blocking collectives: 15 us -> 17 us  [on_device(): g = lax.all_to_all(g, LAT, 0, 0, tiled=True)]
    pallas_call x0 -> x1, Pallas kernels: none -> 1.42 us  [on_device(): call(early_kernel, (f32(HALO, SLAB, LANES), fars, fars), [VMEM] * 6, [plt...]
    ppermute x1, waiting for transfers between devices: 0.01 us -> 1.18 us  [on_device(): lax.ppermute(near_1, LAT, swaps[1])]
    ppermute x1, starting transfers between devices: 1.53 us -> 0.36 us  [on_device(): lax.ppermute(far_0, LAT, swaps[0])]
  transfers between devices with their start and end apart: 5 -> 5, of which waited for: 1 -> 2; matrix products, arithmetic and copies ran while one was open for 0% -> 0% of each run, Pallas kernels for 13% -> 14%
where the time goes in v13:
time: 75.9 us; the launch traced here: 75.6 us
  blocking collectives  39.3 us (52%)
  starting transfers between devices  15.6 us (21%)
  Pallas kernels  14.2 us (19%)
  waiting for transfers between devices  5.81 us (8%)
    all_to_all x1, blocking collectives, on_device(): g = lax.all_to_all(g, LAT, 0, 0, tiled=True)  17 us
    all_to_all x1, blocking collectives, on_device(): got = lax.all_to_all(mixed, RAD, 0, 0, tiled=True)  11.7 us
    all_to_all x1, blocking collectives, on_device(): z2 = lax.all_to_all(sent, RAD, 0, 0, tiled=True)  10.6 us
    ppermute x1, starting transfers between devices, on_device(): lax.ppermute(near_0, LAT, swaps[0])  8.94 us
    all_to_all x1, starting transfers between devices, on_device(): z01 = lax.all_to_all(first, RAD, 0, 0, tiled=True)  6.16 us
    pallas_call x1, Pallas kernels, on_device(): call(outer_kernel, f32(PARTS, 8, FLAT), [VMEM] * 7, [pltpu.VMEM((EXT2, SL...  4.83 us
    all_to_all x1, waiting for transfers between devices, on_device(): z01 = lax.all_to_all(first, RAD, 0, 0, tiled=True)  4.63 us
    pallas_call x1, Pallas kernels, on_device(): call(edge_kernel, (f32(PARTS, 2 * SLAB, PART), f32(EXT1, SLAB, LANES), f3...  2.16 us
  transfers between devices with their start and end apart: 5, of which 2 were waited for; matrix products, arithmetic and copies ran while one was open for 0% of the time, Pallas kernels for 14%

profile of v13, /device:TPU:1, one launch (start us, length us, event | category | flops | bytes accessed | tf_op | source)
XLA Modules:
  0.0 75.6 jit_solution(7203402899566710537)
XLA Ops:
  0.6 0.0 copy-start.1
  0.6 0.0 copy-start.2
  0.7 1.0 %shard_map.86 = (f32[16,1024]{1,0:T(8,128)S(1)}, f32[16,1024]{1,0:T(8,128)S(1)}, f32[8,128]{1,0:T(8,128)S(1)}, s32[31,32]{1,0:T(8,128)S(1)}, f32[1,4096]{1,0:T(1,128)S(1)}) custom-call(f32[16,4096]{1,0:T(8,128)} %src.7, f32[31,4096]{1,0:T(8,128)} %weights.9, f32[1,4096]{1,0:T(1,128)} %bitcast.3, s32[31,32]{1,0:T(8,128)} %neighbors.1, f32[1,128]{1,0:T(1,128)} %bitcast.4), custom_call_target="tpu_custom_call" | custom-call | tf_op jit(solution)/shard_map/pallas_call | solution.py:392
  1.7 8.9 %collective-permute-start = (f32[16,1024]{1,0:T(8,128)S(1)}, f32[16,1024]{1,0:T(8,128)S(1)}, u32[]{:S(2)}, u32[]{:S(2)}) collective-permute-start(f32[16,1024]{1,0:T(8,128)S(1)} %get-tuple-element.24), channel_id=1, source_target_pairs={{0,248},{8,16},{16,8},{24,32},{32,24},{40,48},{48,40},{56,64},{64,... | collective-permute-start | bytes 196616 | tf_op jit(solution)/shard_map/ppermute | solution.py:402
  10.6 0.0 collective-permute-start.1
  10.6 0.0 copy-done.1
  10.6 0.0 copy-done.2
  10.7 1.9 %shard_map.87 = (f32[16,16,128]{2,1,0:T(8,128)S(1)}, f32[32,1,128]{2,1,0:T(1,128)S(1)}, f32[8,128]{1,0:T(8,128)S(1)}) custom-call(f32[16,4096]{1,0:T(8,128)S(1)} %copy-done.2, f32[31,4096]{1,0:T(8,128)S(1)} %copy-done.1, f32[1,4096]{1,0:T(1,128)S(1)} %get-tuple-element.26.shifts, s32[31,32]{1,0:T(8,128)S(1)} %get-tuple-element.27.nb_in, ...), custom_call_target="tpu_custom_call" | custom-call | flops 3000000000 | tf_op jit(solution)/shard_map/pallas_call | solution.py:404
  12.6 1.2 %collective-permute-done.1.near_1 = f32[16,1024]{1,0:T(8,128)S(1)} collective-permute-done((f32[16,1024]{1,0:T(8,128)S(1)}, f32[16,1024]{1,0:T(8,128)S(1)}, u32[]{:S(2)}, u32[]{:S(2)}) %collective-permute-start.1) | collective-permute-done | bytes 65568 | tf_op jit(solution)/shard_map/ppermute | solution.py:402
  13.8 1.4 %shard_map.88 = (f32[8,16,128]{2,1,0:T(8,128)S(1)}, f32[32,1664]{1,0:T(8,128)S(1)}, f32[32,1664]{1,0:T(8,128)S(1)}) custom-call(f32[16,4096]{1,0:T(8,128)S(1)} %copy-done.2, f32[16,1024]{1,0:T(8,128)S(1)} %collective-permute-done.1.near_1, f32[31,4096]{1,0:T(8,128)S(1)} %copy-done.1, f32[1,4096]{1,0:T(1,128)S(1)} %get-tuple-element.26.shifts, ...), custom_call_target="tpu_custom_call" | custom-call | flops 3000000000 | tf_op jit(solution)/shard_map/pallas_call | solution.py:411
  15.2 0.4 collective-permute-start.2
  15.5 0.1 collective-permute-start.3
  15.7 0.0 collective-permute-done.near_0
  15.7 2.2 %shard_map.89 = (f32[8,32,512]{2,1,0:T(8,128)}, f32[48,16,128]{2,1,0:T(8,128)S(1)}, f32[32,16,128]{2,1,0:T(8,128)S(1)}) custom-call(f32[16,4096]{1,0:T(8,128)S(1)} %copy-done.2, f32[16,1024]{1,0:T(8,128)S(1)} %collective-permute-done.near_0, f32[16,1024]{1,0:T(8,128)S(1)} %collective-permute-done.1.near_1, f32[31,4096]{1,0:T(8,128)S(1)} %copy-done.1, ...), custom_call_target="tpu_custom_call" | custom-call | flops 3000000000 | tf_op jit(solution)/shard_map/pallas_call | solution.py:423
  17.8 6.2 %all-to-all-start = ((f32[8,32,512]{2,1,0:T(8,128)}), f32[8,32,512]{2,1,0:T(8,128)S(1)}, u32[]{:S(2)}, u32[]{:S(2)}) async-start(f32[8,32,512]{2,1,0:T(8,128)} %get-tuple-element.31), calls=%async_computation | async-start | bytes 1048576 | tf_op jit(solution)/shard_map/all_to_all | solution.py:435
  24.0 0.0 collective-permute-done.2.far_0
  24.0 0.0 collective-permute-done.3.far_1
  24.0 0.0 copy-start
  24.0 4.8 %shard_map.90.second = f32[8,8,1024]{2,1,0:T(8,128)S(1)} custom-call(f32[48,16,128]{2,1,0:T(8,128)S(1)} %get-tuple-element.32.x0_near, f32[32,16,128]{2,1,0:T(8,128)S(1)} %get-tuple-element.33.x1_own, f32[32,1664]{1,0:T(8,128)S(1)} %collective-permute-done.2.far_0, f32[32,1664]{1,0:T(8,128)S(1)} %collective-permute-done.3.far_1, f32[31,4096]{1,0:T(8,128)S(1)} %copy-done.1, ...), custom_call_target="tpu_custom_call" | custom-call | flops 10000000000 | tf_op jit(solution)/shard_map/pallas_call | solution.py:436
  28.8 4.6 %all-to-all-done.z01 = f32[8,32,512]{2,1,0:T(8,128)S(1)} async-done(((f32[8,32,512]{2,1,0:T(8,128)}), f32[8,32,512]{2,1,0:T(8,128)S(1)}, u32[]{:S(2)}, u32[]{:S(2)}) %all-to-all-start) | async-done | bytes 524320 | tf_op jit(solution)/shard_map/all_to_all | solution.py:435
  33.5 0.0 copy-done
  33.5 1.0 %shard_map.91 = (f32[8,24,384]{2,1,0:T(8,128)S(1)}, f32[128,512]{1,0:T(8,128)S(1)}, f32[128,512]{1,0:T(8,128)S(1)}, f32[128,512]{1,0:T(8,128)S(1)}) custom-call(f32[8,32,512]{2,1,0:T(8,128)S(1)} %all-to-all-done.z01, f32[8,8,1024]{2,1,0:T(8,128)S(1)} %shard_map.90.second, f32[128,128]{1,0:T(8,128)S(1)} %copy-done, f32[8,128]{1,0:T(8,128)S(1)} %get-tuple-element.36.own), custom_call_target="tpu_custom_call" | custom-call | tf_op jit(solution)/shard_map/pallas_call | solution.py:450
  34.4 10.6 %all_to_all.20.z2 = f32[8,24,384]{2,1,0:T(8,128)S(1)} all-to-all(f32[8,24,384]{2,1,0:T(8,128)S(1)} %get-tuple-element.37), channel_id=1, replica_groups=mesh['y'=4,'z'=8,'x'=4,'core'=2] {'x','core'}, dimensions={0} | all-to-all | bytes 589824 | tf_op jit(solution)/shard_map/all_to_all | solution.py:456
  45.0 0.6 shard_map.92
  45.6 0.0 copy-start.3
  45.7 17.0 %all_to_all.21.got = f32[32,1,768]{2,1,0:T(1,128)S(1)} all-to-all(f32[32,1,768]{2,1,0:T(1,128)S(1)} %shard_map.92), channel_id=1, replica_groups=mesh['y'=4,'z'=8,'x'=4,'core'=2] {'y','z'}, dimensions={0} | all-to-all | bytes 196608 | tf_op jit(solution)/shard_map/all_to_all | solution.py:463
  62.7 0.0 copy-done.3
  62.7 0.5 shard_map.93
  63.2 11.7 %all_to_all.22.got = f32[8,24,384]{2,1,0:T(8,128)S(1)} all-to-all(f32[8,24,384]{2,1,0:T(8,128)S(1)} %get-tuple-element.41), channel_id=1, replica_groups=mesh['y'=4,'z'=8,'x'=4,'core'=2] {'x','core'}, dimensions={0} | all-to-all | bytes 589824 | tf_op jit(solution)/shard_map/all_to_all | solution.py:470
  74.9 0.7 shard_map.94
  (1 shorter events, 0.0 us)
Async XLA Ops:
  0.6 10.0 %copy-start.1 = (f32[31,4096]{1,0:T(8,128)S(1)}, f32[31,4096]{1,0:T(8,128)}, u32[]{:S(2)}) copy-start(f32[31,4096]{1,0:T(8,128)} %weights.9) | copy-start | bytes 1523716
  0.6 10.0 %copy-start.2 = (f32[16,4096]{1,0:T(8,128)S(1)}, f32[16,4096]{1,0:T(8,128)}, u32[]{:S(2)}) copy-start(f32[16,4096]{1,0:T(8,128)} %src.7) | copy-start | bytes 786436
  1.7 14.0 %collective-permute-start = (f32[16,1024]{1,0:T(8,128)S(1)}, f32[16,1024]{1,0:T(8,128)S(1)}, u32[]{:S(2)}, u32[]{:S(2)}) collective-permute-start(f32[16,1024]{1,0:T(8,128)S(1)} %get-tuple-element.24), channel_id=1, source_target_pairs={{0,248},{8,16},{16,8},{24,32},{32,24},{40,48},{48,40},{56,64},{64,... | collective-permute-start | bytes 196616 | tf_op jit(solution)/shard_map/ppermute | solution.py:402
  10.6 3.1 %collective-permute-start.1 = (f32[16,1024]{1,0:T(8,128)S(1)}, f32[16,1024]{1,0:T(8,128)S(1)}, u32[]{:S(2)}, u32[]{:S(2)}) collective-permute-start(f32[16,1024]{1,0:T(8,128)S(1)} %get-tuple-element.25), channel_id=1, source_target_pairs={{0,8},{8,0},{16,24},{24,16},{32,40},{40,32},{48,56},{56,48},{64,72... | collective-permute-start | bytes 196616 | tf_op jit(solution)/shard_map/ppermute | solution.py:402
  15.2 8.8 %collective-permute-start.2 = (f32[32,1664]{1,0:T(8,128)S(1)}, f32[32,1664]{1,0:T(8,128)S(1)}, u32[]{:S(2)}, u32[]{:S(2)}) collective-permute-start(f32[32,1664]{1,0:T(8,128)S(1)} %get-tuple-element.34), channel_id=1, source_target_pairs={{0,248},{8,16},{16,8},{24,32},{32,24},{40,48},{48,40},{56,64},{64,... | collective-permute-start | bytes 638984 | tf_op jit(solution)/shard_map/ppermute | solution.py:422
  15.5 8.4 %collective-permute-start.3 = (f32[32,1664]{1,0:T(8,128)S(1)}, f32[32,1664]{1,0:T(8,128)S(1)}, u32[]{:S(2)}, u32[]{:S(2)}) collective-permute-start(f32[32,1664]{1,0:T(8,128)S(1)} %get-tuple-element.35), channel_id=1, source_target_pairs={{0,8},{8,0},{16,24},{24,16},{32,40},{40,32},{48,56},{56,48},{64,72... | collective-permute-start | bytes 638984 | tf_op jit(solution)/shard_map/ppermute | solution.py:422
  17.8 15.6 %all-to-all-start = ((f32[8,32,512]{2,1,0:T(8,128)}), f32[8,32,512]{2,1,0:T(8,128)S(1)}, u32[]{:S(2)}, u32[]{:S(2)}) async-start(f32[8,32,512]{2,1,0:T(8,128)} %get-tuple-element.31), calls=%async_computation | async-start | bytes 1048576 | tf_op jit(solution)/shard_map/all_to_all | solution.py:435
  24.0 9.5 %copy-start = (f32[128,128]{1,0:T(8,128)S(1)}, f32[128,128]{1,0:T(8,128)}, u32[]{:S(2)}) copy-start(f32[128,128]{1,0:T(8,128)} %to_modes.5) | copy-start | bytes 196612
  45.6 17.0 %copy-start.3 = (f32[128,128]{1,0:T(8,128)S(1)}, f32[128,128]{1,0:T(8,128)}, u32[]{:S(2)}) copy-start(f32[128,128]{1,0:T(8,128)} %from_modes.1) | copy-start | bytes 196612

commit v14 on v12

--- a/solution.py
+++ b/solution.py
@@ -242,10 +242,14 @@
     stack = jnp.concatenate(folded, axis=1)
     shape = (8, stack.shape[1])
     which = lax.broadcasted_iota(jnp.int32, shape, 1) // LANES + first
-    pick = (which == lax.broadcasted_iota(jnp.int32, shape, 0)).astype(jnp.float32)
-    return lax.dot_general(
-        pick, stack, (((1,), (1,)), ((), ())), precision=HIGHEST, preferred_element_type=jnp.float32
+    pick = (which == lax.broadcasted_iota(jnp.int32, shape, 0)).astype(jnp.bfloat16)
+    over_lanes = functools.partial(
+        lax.dot_general,
+        dimension_numbers=(((1,), (1,)), ((), ())),
+        preferred_element_type=jnp.float32,
     )
+    high, low = split(stack)
+    return over_lanes(pick, high) + over_lanes(pick, low)
 
 
 def gram_kernel(z01, second, to_modes, own, out, modal, image, partial, s):
@@ -314,10 +318,17 @@
         out[(r, *RIDE)] = ours
 
 
-def unpack_kernel(got, side, place, out, mine):
+def unpack_kernel(got, side, place, out, mine, columns, sems):
+    copies = []
     for r in range(PARTS):
         for t, rows, cols in tiles(0):
-            out[rows, r * PART + cols.start : r * PART + cols.stop] = got[(r, *tile(t))]
+            columns[rows, r * PART + cols.start : r * PART + cols.stop] = got[(r, *tile(t))]
+        if r % 2:
+            done = pl.ds((r - 1) * PART, 2 * PART)
+            copies.append(
+                pltpu.make_async_copy(columns.at[:, done], out.at[:, done], sems.at[r // 2])
+            )
+            copies[-1].start()
     squares = side[0:1, :] + sum(got[r, 16:17, RIDE[1]] for r in range(PARTS))
     norm = jnp.sqrt(jnp.maximum(squares, 0.0) / side[1:2, :])
     here = place[0:1, 0:SLAB]
@@ -325,6 +336,7 @@
     for r in range(1, PARTS):
         picked = jnp.where(here == r, norm[:, r * SLAB : (r + 1) * SLAB], picked)
     mine[...] = picked
+    wait_all(copies)
 
 
 def call(kernel, out_shape, in_specs, scratch=(), out_specs=None, cost=None):
@@ -421,7 +433,14 @@
     )(g, z01, to_modes, from_modes, own)
     got = lax.all_to_all(mixed, RAD, 0, 0, tiled=True)
     smoothed, residual_norm = call(
-        unpack_kernel, (f32(SLAB, BLOCKS * LANES), f32(1, SLAB)), [VMEM] * 3
+        unpack_kernel,
+        (f32(SLAB, BLOCKS * LANES), f32(1, SLAB)),
+        [VMEM] * 3,
+        [
+            pltpu.VMEM((SLAB, BLOCKS * LANES), jnp.float32),
+            pltpu.SemaphoreType.DMA((PARTS // 2,)),
+        ],
+        out_specs=(HBM, VMEM),
     )(got, side, place)
     return smoothed, residual_norm.reshape(SLAB)
 

time: 72.6 us -> 72.6 us (level)
  no operation moved by 1% of the time
where the time goes in v14:
time: 72.6 us; the launch traced here: 72.3 us
  blocking collectives  37.2 us (51%)
  starting transfers between devices  16.5 us (23%)
  Pallas kernels  13.2 us (18%)
  waiting for transfers between devices  4.63 us (6%)
  between operations  0.73 us (1%)
    all_to_all x1, blocking collectives, on_device(): g = lax.all_to_all(g, LAT, 0, 0, tiled=True)  15 us
    all_to_all x1, blocking collectives, on_device(): got = lax.all_to_all(mixed, RAD, 0, 0, tiled=True)  11.7 us
    all_to_all x1, blocking collectives, on_device(): z2 = lax.all_to_all(sent, RAD, 0, 0, tiled=True)  10.6 us
    ppermute x1, starting transfers between devices, on_device(): lax.ppermute(near_0, LAT, swaps[0])  8.94 us
    all_to_all x1, starting transfers between devices, on_device(): z01 = lax.all_to_all(first, RAD, 0, 0, tiled=True)  5.88 us
    pallas_call x1, Pallas kernels, on_device(): call(outer_kernel, f32(PARTS, 8, FLAT), [VMEM] * 7, [pltpu.VMEM((EXT2, SL...  4.83 us
    all_to_all x1, waiting for transfers between devices, on_device(): z01 = lax.all_to_all(first, RAD, 0, 0, tiled=True)  4.62 us
    pallas_call x1, Pallas kernels, on_device(): call(edge_kernel, (f32(PARTS, 2 * SLAB, PART), f32(EXT1, SLAB, LANES), f3...  2.59 us
  transfers between devices with their start and end apart: 5, of which 1 were waited for; matrix products, arithmetic and copies ran while one was open for 0% of the time, Pallas kernels for 13%

profile of v14, /device:TPU:1, one launch (start us, length us, event | category | flops | bytes accessed | tf_op | source)
XLA Modules:
  0.0 72.3 jit_solution(17858696812440600711)
XLA Ops:
  0.6 0.0 copy-start.1
  0.6 0.0 copy-start.2
  0.7 1.0 %shard_map.86 = (f32[16,1024]{1,0:T(8,128)S(1)}, f32[16,1024]{1,0:T(8,128)S(1)}, f32[8,128]{1,0:T(8,128)S(1)}, s32[31,32]{1,0:T(8,128)S(1)}, f32[1,4096]{1,0:T(1,128)S(1)}) custom-call(f32[16,4096]{1,0:T(8,128)} %src.5, f32[31,4096]{1,0:T(8,128)} %weights.7, f32[1,4096]{1,0:T(1,128)} %bitcast.3, s32[31,32]{1,0:T(8,128)} %neighbors.1, f32[1,128]{1,0:T(1,128)} %bitcast.4), custom_call_target="tpu_custom_call" | custom-call | tf_op jit(solution)/shard_map/pallas_call | solution.py:367
  1.7 8.9 %collective-permute-start = (f32[16,1024]{1,0:T(8,128)S(1)}, f32[16,1024]{1,0:T(8,128)S(1)}, u32[]{:S(2)}, u32[]{:S(2)}) collective-permute-start(f32[16,1024]{1,0:T(8,128)S(1)} %get-tuple-element.23), channel_id=1, source_target_pairs={{0,248},{8,16},{16,8},{24,32},{32,24},{40,48},{48,40},{56,64},{64,... | collective-permute-start | bytes 196616 | tf_op jit(solution)/shard_map/ppermute | solution.py:377
  10.6 0.0 collective-permute-start.1
  10.6 0.0 copy-done.1
  10.6 0.0 copy-done.2
  10.7 2.0 %shard_map.87 = (f32[16,16,128]{2,1,0:T(8,128)S(1)}, f32[32,1,128]{2,1,0:T(1,128)S(1)}, f32[8,128]{1,0:T(8,128)S(1)}, f32[32,1664]{1,0:T(8,128)S(1)}, f32[32,1664]{1,0:T(8,128)S(1)}) custom-call(f32[16,4096]{1,0:T(8,128)S(1)} %copy-done.2, f32[31,4096]{1,0:T(8,128)S(1)} %copy-done.1, f32[1,4096]{1,0:T(1,128)S(1)} %get-tuple-element.25.shifts, ...), custom_call_target="tpu_custom_call" | custom-call | flops 3000000000 | tf_op jit(solution)/shard_map/pallas_call | solution.py:379
  12.6 1.5 %collective-permute-start.2 = (f32[32,1664]{1,0:T(8,128)S(1)}, f32[32,1664]{1,0:T(8,128)S(1)}, u32[]{:S(2)}, u32[]{:S(2)}) collective-permute-start(f32[32,1664]{1,0:T(8,128)S(1)} %get-tuple-element.32), channel_id=1, source_target_pairs={{0,248},{8,16},{16,8},{24,32},{32,24},{40,48},{48,40},{56,64},{64,... | collective-permute-start | bytes 638984 | tf_op jit(solution)/shard_map/ppermute | solution.py:386
  14.2 0.1 collective-permute-start.3
  14.3 0.0 collective-permute-done.near_0
  14.3 0.0 collective-permute-done.1.near_1
  14.3 2.6 %shard_map.88 = (f32[8,32,512]{2,1,0:T(8,128)}, f32[48,16,128]{2,1,0:T(8,128)S(1)}, f32[32,16,128]{2,1,0:T(8,128)S(1)}) custom-call(f32[16,4096]{1,0:T(8,128)S(1)} %copy-done.2, f32[16,1024]{1,0:T(8,128)S(1)} %collective-permute-done.near_0, f32[16,1024]{1,0:T(8,128)S(1)} %collective-permute-done.1.near_1, f32[31,4096]{1,0:T(8,128)S(1)} %copy-done.1, ...), custom_call_target="tpu_custom_call" | custom-call | flops 3000000000 | tf_op jit(solution)/shard_map/pallas_call | solution.py:387
  16.9 5.9 %all-to-all-start = ((f32[8,32,512]{2,1,0:T(8,128)}), f32[8,32,512]{2,1,0:T(8,128)S(1)}, u32[]{:S(2)}, u32[]{:S(2)}) async-start(f32[8,32,512]{2,1,0:T(8,128)} %get-tuple-element.29), calls=%async_computation | async-start | bytes 1048576 | tf_op jit(solution)/shard_map/all_to_all | solution.py:399
  22.8 0.0 collective-permute-done.2.far_0
  22.8 0.0 collective-permute-done.3.far_1
  22.8 0.0 copy-start
  22.8 4.8 %shard_map.89.second = f32[8,8,1024]{2,1,0:T(8,128)S(1)} custom-call(f32[48,16,128]{2,1,0:T(8,128)S(1)} %get-tuple-element.30.x0_near, f32[32,16,128]{2,1,0:T(8,128)S(1)} %get-tuple-element.31.x1_own, f32[32,1664]{1,0:T(8,128)S(1)} %collective-permute-done.2.far_0, f32[32,1664]{1,0:T(8,128)S(1)} %collective-permute-done.3.far_1, f32[31,4096]{1,0:T(8,128)S(1)} %copy-done.1, ...), custom_call_target="tpu_custom_call" | custom-call | flops 10000000000 | tf_op jit(solution)/shard_map/pallas_call | solution.py:400
  27.6 4.6 %all-to-all-done.z01 = f32[8,32,512]{2,1,0:T(8,128)S(1)} async-done(((f32[8,32,512]{2,1,0:T(8,128)}), f32[8,32,512]{2,1,0:T(8,128)S(1)}, u32[]{:S(2)}, u32[]{:S(2)}) %all-to-all-start) | async-done | bytes 524320 | tf_op jit(solution)/shard_map/all_to_all | solution.py:399
  32.2 0.0 copy-done
  32.2 0.6 shard_map.90
  32.8 10.6 %all_to_all.20.z2 = f32[8,24,384]{2,1,0:T(8,128)S(1)} all-to-all(f32[8,24,384]{2,1,0:T(8,128)S(1)} %get-tuple-element.35), channel_id=1, replica_groups=mesh['y'=4,'z'=8,'x'=4,'core'=2] {'x','core'}, dimensions={0} | all-to-all | bytes 589824 | tf_op jit(solution)/shard_map/all_to_all | solution.py:420
  43.4 0.5 shard_map.91
  43.9 0.0 copy-start.3
  43.9 15.0 %all_to_all.21.got = f32[32,1,768]{2,1,0:T(1,128)S(1)} all-to-all(f32[32,1,768]{2,1,0:T(1,128)S(1)} %shard_map.91), channel_id=1, replica_groups=mesh['y'=4,'z'=8,'x'=4,'core'=2] {'y','z'}, dimensions={0} | all-to-all | bytes 196608 | tf_op jit(solution)/shard_map/all_to_all | solution.py:427
  58.9 0.0 copy-done.3
  58.9 0.5 shard_map.92
  59.4 11.7 %all_to_all.22.got = f32[8,24,384]{2,1,0:T(8,128)S(1)} all-to-all(f32[8,24,384]{2,1,0:T(8,128)S(1)} %get-tuple-element.39), channel_id=1, replica_groups=mesh['y'=4,'z'=8,'x'=4,'core'=2] {'x','core'}, dimensions={0} | all-to-all | bytes 589824 | tf_op jit(solution)/shard_map/all_to_all | solution.py:434
  71.1 1.2 %shard_map.93 = (f32[16,4096]{1,0:T(8,128)}, f32[1,16]{1,0:T(1,128)}) custom-call(f32[8,24,384]{2,1,0:T(8,128)S(1)} %all_to_all.22.got, f32[8,128]{1,0:T(8,128)S(1)} %get-tuple-element.40.side, f32[8,128]{1,0:T(8,128)S(1)} %get-tuple-element.41.place), custom_call_target="tpu_custom_call" | custom-call | tf_op jit(solution)/shard_map/pallas_call | solution.py:435
  (1 shorter events, 0.0 us)
Async XLA Ops:
  0.6 10.0 %copy-start.1 = (f32[31,4096]{1,0:T(8,128)S(1)}, f32[31,4096]{1,0:T(8,128)}, u32[]{:S(2)}) copy-start(f32[31,4096]{1,0:T(8,128)} %weights.7) | copy-start | bytes 1523716
  0.6 10.0 %copy-start.2 = (f32[16,4096]{1,0:T(8,128)S(1)}, f32[16,4096]{1,0:T(8,128)}, u32[]{:S(2)}) copy-start(f32[16,4096]{1,0:T(8,128)} %src.5) | copy-start | bytes 786436
  1.7 12.6 %collective-permute-start = (f32[16,1024]{1,0:T(8,128)S(1)}, f32[16,1024]{1,0:T(8,128)S(1)}, u32[]{:S(2)}, u32[]{:S(2)}) collective-permute-start(f32[16,1024]{1,0:T(8,128)S(1)} %get-tuple-element.23), channel_id=1, source_target_pairs={{0,248},{8,16},{16,8},{24,32},{32,24},{40,48},{48,40},{56,64},{64,... | collective-permute-start | bytes 196616 | tf_op jit(solution)/shard_map/ppermute | solution.py:377
  10.6 3.6 %collective-permute-start.1 = (f32[16,1024]{1,0:T(8,128)S(1)}, f32[16,1024]{1,0:T(8,128)S(1)}, u32[]{:S(2)}, u32[]{:S(2)}) collective-permute-start(f32[16,1024]{1,0:T(8,128)S(1)} %get-tuple-element.24), channel_id=1, source_target_pairs={{0,8},{8,0},{16,24},{24,16},{32,40},{40,32},{48,56},{56,48},{64,72... | collective-permute-start | bytes 196616 | tf_op jit(solution)/shard_map/ppermute | solution.py:377
  12.6 10.1 %collective-permute-start.2 = (f32[32,1664]{1,0:T(8,128)S(1)}, f32[32,1664]{1,0:T(8,128)S(1)}, u32[]{:S(2)}, u32[]{:S(2)}) collective-permute-start(f32[32,1664]{1,0:T(8,128)S(1)} %get-tuple-element.32), channel_id=1, source_target_pairs={{0,248},{8,16},{16,8},{24,32},{32,24},{40,48},{48,40},{56,64},{64,... | collective-permute-start | bytes 638984 | tf_op jit(solution)/shard_map/ppermute | solution.py:386
  14.2 8.6 %collective-permute-start.3 = (f32[32,1664]{1,0:T(8,128)S(1)}, f32[32,1664]{1,0:T(8,128)S(1)}, u32[]{:S(2)}, u32[]{:S(2)}) collective-permute-start(f32[32,1664]{1,0:T(8,128)S(1)} %get-tuple-element.33), channel_id=1, source_target_pairs={{0,8},{8,0},{16,24},{24,16},{32,40},{40,32},{48,56},{56,48},{64,72... | collective-permute-start | bytes 638984 | tf_op jit(solution)/shard_map/ppermute | solution.py:386
  16.9 15.4 %all-to-all-start = ((f32[8,32,512]{2,1,0:T(8,128)}), f32[8,32,512]{2,1,0:T(8,128)S(1)}, u32[]{:S(2)}, u32[]{:S(2)}) async-start(f32[8,32,512]{2,1,0:T(8,128)} %get-tuple-element.29), calls=%async_computation | async-start | bytes 1048576 | tf_op jit(solution)/shard_map/all_to_all | solution.py:399
  22.8 9.5 %copy-start = (f32[128,128]{1,0:T(8,128)S(1)}, f32[128,128]{1,0:T(8,128)}, u32[]{:S(2)}) copy-start(f32[128,128]{1,0:T(8,128)} %to_modes.5) | copy-start | bytes 196612
  43.9 15.0 %copy-start.3 = (f32[128,128]{1,0:T(8,128)S(1)}, f32[128,128]{1,0:T(8,128)}, u32[]{:S(2)}) copy-start(f32[128,128]{1,0:T(8,128)} %from_modes.1) | copy-start | bytes 196612

commit v15 on v12

--- a/solution.py
+++ b/solution.py
@@ -242,10 +242,14 @@
     stack = jnp.concatenate(folded, axis=1)
     shape = (8, stack.shape[1])
     which = lax.broadcasted_iota(jnp.int32, shape, 1) // LANES + first
-    pick = (which == lax.broadcasted_iota(jnp.int32, shape, 0)).astype(jnp.float32)
-    return lax.dot_general(
-        pick, stack, (((1,), (1,)), ((), ())), precision=HIGHEST, preferred_element_type=jnp.float32
+    pick = (which == lax.broadcasted_iota(jnp.int32, shape, 0)).astype(jnp.bfloat16)
+    over_lanes = functools.partial(
+        lax.dot_general,
+        dimension_numbers=(((1,), (1,)), ((), ())),
+        preferred_element_type=jnp.float32,
     )
+    high, low = split(stack)
+    return over_lanes(pick, high) + over_lanes(pick, low)
 
 
 def gram_kernel(z01, second, to_modes, own, out, modal, image, partial, s):

time: 72.6 us -> 72.1 us (level)
  no operation moved by 1% of the time
where the time goes in v15:
time: 72.1 us; the launch traced here: 71.8 us
  blocking collectives  37.2 us (52%)
  starting transfers between devices  16.5 us (23%)
  Pallas kernels  12.7 us (18%)
  waiting for transfers between devices  4.64 us (6%)
  between operations  0.73 us (1%)
    all_to_all x1, blocking collectives, on_device(): g = lax.all_to_all(g, LAT, 0, 0, tiled=True)  15 us
    all_to_all x1, blocking collectives, on_device(): got = lax.all_to_all(mixed, RAD, 0, 0, tiled=True)  11.7 us
    all_to_all x1, blocking collectives, on_device(): z2 = lax.all_to_all(sent, RAD, 0, 0, tiled=True)  10.6 us
    ppermute x1, starting transfers between devices, on_device(): lax.ppermute(near_0, LAT, swaps[0])  8.94 us
    all_to_all x1, starting transfers between devices, on_device(): z01 = lax.all_to_all(first, RAD, 0, 0, tiled=True)  5.88 us
    pallas_call x1, Pallas kernels, on_device(): call(outer_kernel, f32(PARTS, 8, FLAT), [VMEM] * 7, [pltpu.VMEM((EXT2, SL...  4.82 us
    all_to_all x1, waiting for transfers between devices, on_device(): z01 = lax.all_to_all(first, RAD, 0, 0, tiled=True)  4.63 us
    pallas_call x1, Pallas kernels, on_device(): call(edge_kernel, (f32(PARTS, 2 * SLAB, PART), f32(EXT1, SLAB, LANES), f3...  2.59 us
  transfers between devices with their start and end apart: 5, of which 1 were waited for; matrix products, arithmetic and copies ran while one was open for 0% of the time, Pallas kernels for 13%

profile of v15, /device:TPU:1, one launch (start us, length us, event | category | flops | bytes accessed | tf_op | source)
XLA Modules:
  0.0 71.8 jit_solution(8160968270925197050)
XLA Ops:
  0.6 0.0 copy-start.1
  0.6 0.0 copy-start.2
  0.7 1.0 %shard_map.86 = (f32[16,1024]{1,0:T(8,128)S(1)}, f32[16,1024]{1,0:T(8,128)S(1)}, f32[8,128]{1,0:T(8,128)S(1)}, s32[31,32]{1,0:T(8,128)S(1)}, f32[1,4096]{1,0:T(1,128)S(1)}) custom-call(f32[16,4096]{1,0:T(8,128)} %src.5, f32[31,4096]{1,0:T(8,128)} %weights.7, f32[1,4096]{1,0:T(1,128)} %bitcast.3, s32[31,32]{1,0:T(8,128)} %neighbors.1, f32[1,128]{1,0:T(1,128)} %bitcast.4), custom_call_target="tpu_custom_call" | custom-call | tf_op jit(solution)/shard_map/pallas_call | solution.py:359
  1.7 8.9 %collective-permute-start = (f32[16,1024]{1,0:T(8,128)S(1)}, f32[16,1024]{1,0:T(8,128)S(1)}, u32[]{:S(2)}, u32[]{:S(2)}) collective-permute-start(f32[16,1024]{1,0:T(8,128)S(1)} %get-tuple-element.23), channel_id=1, source_target_pairs={{0,248},{8,16},{16,8},{24,32},{32,24},{40,48},{48,40},{56,64},{64,... | collective-permute-start | bytes 196616 | tf_op jit(solution)/shard_map/ppermute | solution.py:369
  10.6 0.0 collective-permute-start.1
  10.6 0.0 copy-done.1
  10.6 0.0 copy-done.2
  10.7 2.0 %shard_map.87 = (f32[16,16,128]{2,1,0:T(8,128)S(1)}, f32[32,1,128]{2,1,0:T(1,128)S(1)}, f32[8,128]{1,0:T(8,128)S(1)}, f32[32,1664]{1,0:T(8,128)S(1)}, f32[32,1664]{1,0:T(8,128)S(1)}) custom-call(f32[16,4096]{1,0:T(8,128)S(1)} %copy-done.2, f32[31,4096]{1,0:T(8,128)S(1)} %copy-done.1, f32[1,4096]{1,0:T(1,128)S(1)} %get-tuple-element.25.shifts, ...), custom_call_target="tpu_custom_call" | custom-call | flops 3000000000 | tf_op jit(solution)/shard_map/pallas_call | solution.py:371
  12.6 1.5 %collective-permute-start.2 = (f32[32,1664]{1,0:T(8,128)S(1)}, f32[32,1664]{1,0:T(8,128)S(1)}, u32[]{:S(2)}, u32[]{:S(2)}) collective-permute-start(f32[32,1664]{1,0:T(8,128)S(1)} %get-tuple-element.32), channel_id=1, source_target_pairs={{0,248},{8,16},{16,8},{24,32},{32,24},{40,48},{48,40},{56,64},{64,... | collective-permute-start | bytes 638984 | tf_op jit(solution)/shard_map/ppermute | solution.py:378
  14.2 0.1 collective-permute-start.3
  14.3 0.0 collective-permute-done.near_0
  14.3 0.0 collective-permute-done.1.near_1
  14.3 2.6 %shard_map.88 = (f32[8,32,512]{2,1,0:T(8,128)}, f32[48,16,128]{2,1,0:T(8,128)S(1)}, f32[32,16,128]{2,1,0:T(8,128)S(1)}) custom-call(f32[16,4096]{1,0:T(8,128)S(1)} %copy-done.2, f32[16,1024]{1,0:T(8,128)S(1)} %collective-permute-done.near_0, f32[16,1024]{1,0:T(8,128)S(1)} %collective-permute-done.1.near_1, f32[31,4096]{1,0:T(8,128)S(1)} %copy-done.1, ...), custom_call_target="tpu_custom_call" | custom-call | flops 3000000000 | tf_op jit(solution)/shard_map/pallas_call | solution.py:379
  16.9 5.9 %all-to-all-start = ((f32[8,32,512]{2,1,0:T(8,128)}), f32[8,32,512]{2,1,0:T(8,128)S(1)}, u32[]{:S(2)}, u32[]{:S(2)}) async-start(f32[8,32,512]{2,1,0:T(8,128)} %get-tuple-element.29), calls=%async_computation | async-start | bytes 1048576 | tf_op jit(solution)/shard_map/all_to_all | solution.py:391
  22.8 0.0 collective-permute-done.2.far_0
  22.8 0.0 collective-permute-done.3.far_1
  22.8 0.0 copy-start
  22.8 4.8 %shard_map.89.second = f32[8,8,1024]{2,1,0:T(8,128)S(1)} custom-call(f32[48,16,128]{2,1,0:T(8,128)S(1)} %get-tuple-element.30.x0_near, f32[32,16,128]{2,1,0:T(8,128)S(1)} %get-tuple-element.31.x1_own, f32[32,1664]{1,0:T(8,128)S(1)} %collective-permute-done.2.far_0, f32[32,1664]{1,0:T(8,128)S(1)} %collective-permute-done.3.far_1, f32[31,4096]{1,0:T(8,128)S(1)} %copy-done.1, ...), custom_call_target="tpu_custom_call" | custom-call | flops 10000000000 | tf_op jit(solution)/shard_map/pallas_call | solution.py:392
  27.6 4.6 %all-to-all-done.z01 = f32[8,32,512]{2,1,0:T(8,128)S(1)} async-done(((f32[8,32,512]{2,1,0:T(8,128)}), f32[8,32,512]{2,1,0:T(8,128)S(1)}, u32[]{:S(2)}, u32[]{:S(2)}) %all-to-all-start) | async-done | bytes 524320 | tf_op jit(solution)/shard_map/all_to_all | solution.py:391
  32.2 0.0 copy-done
  32.2 0.5 shard_map.90
  32.8 10.6 %all_to_all.20.z2 = f32[8,24,384]{2,1,0:T(8,128)S(1)} all-to-all(f32[8,24,384]{2,1,0:T(8,128)S(1)} %get-tuple-element.35), channel_id=1, replica_groups=mesh['y'=4,'z'=8,'x'=4,'core'=2] {'x','core'}, dimensions={0} | all-to-all | bytes 589824 | tf_op jit(solution)/shard_map/all_to_all | solution.py:412
  43.4 0.5 shard_map.91
  43.9 0.0 copy-start.3
  43.9 15.0 %all_to_all.21.got = f32[32,1,768]{2,1,0:T(1,128)S(1)} all-to-all(f32[32,1,768]{2,1,0:T(1,128)S(1)} %shard_map.91), channel_id=1, replica_groups=mesh['y'=4,'z'=8,'x'=4,'core'=2] {'y','z'}, dimensions={0} | all-to-all | bytes 196608 | tf_op jit(solution)/shard_map/all_to_all | solution.py:419
  58.9 0.0 copy-done.3
  58.9 0.5 shard_map.92
  59.4 11.7 %all_to_all.22.got = f32[8,24,384]{2,1,0:T(8,128)S(1)} all-to-all(f32[8,24,384]{2,1,0:T(8,128)S(1)} %get-tuple-element.39), channel_id=1, replica_groups=mesh['y'=4,'z'=8,'x'=4,'core'=2] {'x','core'}, dimensions={0} | all-to-all | bytes 589824 | tf_op jit(solution)/shard_map/all_to_all | solution.py:426
  71.1 0.7 %shard_map.93 = (f32[16,4096]{1,0:T(8,128)}, f32[1,16]{1,0:T(1,128)}) custom-call(f32[8,24,384]{2,1,0:T(8,128)S(1)} %all_to_all.22.got, f32[8,128]{1,0:T(8,128)S(1)} %get-tuple-element.40.side, f32[8,128]{1,0:T(8,128)S(1)} %get-tuple-element.41.place), custom_call_target="tpu_custom_call" | custom-call | tf_op jit(solution)/shard_map/pallas_call | solution.py:427
  (1 shorter events, 0.0 us)
Async XLA Ops:
  0.6 10.0 %copy-start.1 = (f32[31,4096]{1,0:T(8,128)S(1)}, f32[31,4096]{1,0:T(8,128)}, u32[]{:S(2)}) copy-start(f32[31,4096]{1,0:T(8,128)} %weights.7) | copy-start | bytes 1523716
  0.6 10.0 %copy-start.2 = (f32[16,4096]{1,0:T(8,128)S(1)}, f32[16,4096]{1,0:T(8,128)}, u32[]{:S(2)}) copy-start(f32[16,4096]{1,0:T(8,128)} %src.5) | copy-start | bytes 786436
  1.7 12.6 %collective-permute-start = (f32[16,1024]{1,0:T(8,128)S(1)}, f32[16,1024]{1,0:T(8,128)S(1)}, u32[]{:S(2)}, u32[]{:S(2)}) collective-permute-start(f32[16,1024]{1,0:T(8,128)S(1)} %get-tuple-element.23), channel_id=1, source_target_pairs={{0,248},{8,16},{16,8},{24,32},{32,24},{40,48},{48,40},{56,64},{64,... | collective-permute-start | bytes 196616 | tf_op jit(solution)/shard_map/ppermute | solution.py:369
  10.6 3.6 %collective-permute-start.1 = (f32[16,1024]{1,0:T(8,128)S(1)}, f32[16,1024]{1,0:T(8,128)S(1)}, u32[]{:S(2)}, u32[]{:S(2)}) collective-permute-start(f32[16,1024]{1,0:T(8,128)S(1)} %get-tuple-element.24), channel_id=1, source_target_pairs={{0,8},{8,0},{16,24},{24,16},{32,40},{40,32},{48,56},{56,48},{64,72... | collective-permute-start | bytes 196616 | tf_op jit(solution)/shard_map/ppermute | solution.py:369
  12.6 10.1 %collective-permute-start.2 = (f32[32,1664]{1,0:T(8,128)S(1)}, f32[32,1664]{1,0:T(8,128)S(1)}, u32[]{:S(2)}, u32[]{:S(2)}) collective-permute-start(f32[32,1664]{1,0:T(8,128)S(1)} %get-tuple-element.32), channel_id=1, source_target_pairs={{0,248},{8,16},{16,8},{24,32},{32,24},{40,48},{48,40},{56,64},{64,... | collective-permute-start | bytes 638984 | tf_op jit(solution)/shard_map/ppermute | solution.py:378
  14.2 8.6 %collective-permute-start.3 = (f32[32,1664]{1,0:T(8,128)S(1)}, f32[32,1664]{1,0:T(8,128)S(1)}, u32[]{:S(2)}, u32[]{:S(2)}) collective-permute-start(f32[32,1664]{1,0:T(8,128)S(1)} %get-tuple-element.33), channel_id=1, source_target_pairs={{0,8},{8,0},{16,24},{24,16},{32,40},{40,32},{48,56},{56,48},{64,72... | collective-permute-start | bytes 638984 | tf_op jit(solution)/shard_map/ppermute | solution.py:378
  16.9 15.4 %all-to-all-start = ((f32[8,32,512]{2,1,0:T(8,128)}), f32[8,32,512]{2,1,0:T(8,128)S(1)}, u32[]{:S(2)}, u32[]{:S(2)}) async-start(f32[8,32,512]{2,1,0:T(8,128)} %get-tuple-element.29), calls=%async_computation | async-start | bytes 1048576 | tf_op jit(solution)/shard_map/all_to_all | solution.py:391
  22.8 9.5 %copy-start = (f32[128,128]{1,0:T(8,128)S(1)}, f32[128,128]{1,0:T(8,128)}, u32[]{:S(2)}) copy-start(f32[128,128]{1,0:T(8,128)} %to_modes.5) | copy-start | bytes 196612
  43.9 15.0 %copy-start.3 = (f32[128,128]{1,0:T(8,128)S(1)}, f32[128,128]{1,0:T(8,128)}, u32[]{:S(2)}) copy-start(f32[128,128]{1,0:T(8,128)} %from_modes.1) | copy-start | bytes 196612
